TPU v7x, 256 devices: a whole 4x4x8 slice. The times are simulated.
256 devices in a mesh: span: 16 (over y_lo, z), chord: 4 (over x), normal: 4 (over y_hi, core).
Axes of the slice: x: 4, y: 4 (y_hi: 2, y_lo: 2; y = y_hi * 2 + y_lo), z: 8, core: 2. Of those that a mesh axis runs over, the one named last changes fastest.
Arguments:
- adjoint: float32 [5, 128, 32, 512], P(None, 'span', 'chord', 'normal'), may hold values from -6 to 6
- jacobian: bfloat16 [7, 5, 5, 128, 32, 512], P(None, None, None, 'span', 'chord', 'normal'), may hold values from -1 to 1
- wall_table: float32 [3, 5, 5], replicated, may hold values from -3 to 3
- face_type: int32 [128, 32], P('span', 'chord'), may hold values from 0 to 2
- mesh_map: float32 [3, 5], replicated, may hold values from -2.5 to 2.5
- stiffness: float32 [7, 128, 32, 512], P(None, 'span', 'chord', 'normal'), may hold values from 0.1 to 1
- box_map: int32 [16, 4, 4], P('span', 'chord', 'normal'), may hold values from 0 to 15
- offsets: int32 [16, 4, 4, 3], P('span', 'chord', 'normal'), may hold values from 0 to 88, as said below
Outputs:
- mesh_adjoint: float32 [3, 128, 32, 512], P(None, 'span', 'chord', 'normal')
- ffd_grad: float32 [16, 3, 49152], P('span', None, ('chord', 'normal'))
Inputs may be any that keep to these rules, and one draw needn't show every extreme that they name: `offsets`: column 0 is at most 88, column 1 at most 24, column 2 at most 8, so every window lies inside its box.
All inputs are finite; a program needn't handle non-finite values.
Results may differ from a plain program's by a relative error of at most 0.0003.
Values sent between devices are 32-bit elements; how exact they have to be, the bound alone decides.
No kernel may reach another device: no remote copies, remote signals or barrier semaphores. Data moves between devices by JAX's collectives and lax.ppermute only.
A program may use at most 192 MiB of HBM per device.

v0:
```python
import math

import jax
import jax.numpy as jnp
import numpy as np
from jax import lax
from jax.experimental import pallas as pl
from jax.experimental.pallas import tpu as pltpu
from jax.sharding import PartitionSpec as P

F32 = jnp.float32
HIGHEST = lax.Precision.HIGHEST
ALL = ("span", "chord", "normal")
CX, CY, CZ = 8, 8, 128
LA = 96
ROWS = LA // 16
SLOT = 16
WINDOWS = 32


def bernstein(count, cells):
    degree = count - 1
    u = (np.arange(cells) + 0.5) / cells
    return np.stack([math.comb(degree, a) * u**a * (1 - u) ** (degree - a) for a in range(count)])


def tables():
    bx, by, bz = bernstein(8, CX), bernstein(8, CY), bernstein(8, CZ)
    along_z = np.zeros((CZ, 8, 2, 8))
    along_z[:] = bz.T[:, None, None, :]
    along_y = np.repeat(by.T, 16, axis=1)
    along_x = np.zeros((2, 4, 4, 3, CX, CY))
    for r in range(3):
        along_x[:, r, :, r] = 8.0 * bx.reshape(2, 4, CX)[..., None]
    return (
        along_z.reshape(CZ, 128).astype(np.float32),
        along_y.astype(np.float32),
        along_x.reshape(32, 192).astype(np.float32),
    )


def iotas():
    lane = lax.broadcasted_iota(jnp.int32, (8, 128), 1)
    row = lax.broadcasted_iota(jnp.int32, (8, 128), 0)
    return lane, row


def odd(axis):
    return lax.rem(lax.axis_index(axis), 2) == 1


def pick(flag, one, two):
    return jnp.where(jnp.full(one.shape, flag), one, two)


def pack(tile_of, fields, sends):
    lane, _ = iotas()
    xa, xb, ya, yb, za, zb = sends
    by_x, by_y, by_z = odd("span"), odd("chord"), odd("normal")
    low = jnp.zeros((8, 128), F32)
    high = jnp.zeros((8, 128), F32)
    for v in range(fields):
        first, last = tile_of(v, 0), tile_of(v, CX - 1)
        xa[v] = pick(by_x, first, last)
        xb[v] = pick(by_x, last, first)
        for x in range(CX):
            tile = tile_of(v, x)
            k = v * CX + x
            ya[k : k + 1, :] = pick(by_y, tile[0:1, :], tile[7:8, :])
            yb[k : k + 1, :] = pick(by_y, tile[7:8, :], tile[0:1, :])
            low = jnp.where(lane == k, pltpu.roll(tile, k, 1) if k else tile, low)
            high = jnp.where(lane == k, pltpu.roll(tile, k + 1, 1), high)
    za[...] = pick(by_z, low, high)
    zb[...] = pick(by_z, high, low)


def unpack(halo, planes_ref, rows_ref):
    xa, xb, ya, yb, za, zb = halo
    by_x, by_y, by_z = odd("span"), odd("chord"), odd("normal")
    planes_ref[0] = pick(by_x, xa[...], xb[...])
    planes_ref[1] = pick(by_x, xb[...], xa[...])
    rows_ref[0] = pick(by_y, ya[...], yb[...])
    rows_ref[1] = pick(by_y, yb[...], ya[...])
    return pick(by_z, za[...], zb[...]), pick(by_z, zb[...], za[...])


def neighbour(e, tile_of, v, x, planes_ref, rows_ref, low, high):
    lane, row = iotas()
    k = v * CX + x
    if e == 1:
        return planes_ref[0, v] if x == 0 else tile_of(v, x - 1)
    if e == 2:
        return planes_ref[1, v] if x == CX - 1 else tile_of(v, x + 1)
    tile = tile_of(v, x)
    if e == 0:
        return tile
    if e == 3:
        return jnp.where(row == 0, rows_ref[0, k : k + 1, :], pltpu.roll(tile, 1, 0))
    if e == 4:
        return jnp.where(row == 7, rows_ref[1, k : k + 1, :], pltpu.roll(tile, 7, 0))
    if e == 5:
        return jnp.where(lane == 0, pltpu.roll(low, (128 - k) % 128, 1) if k else low, pltpu.roll(tile, 1, 1))
    return jnp.where(lane == 127, pltpu.roll(high, 127 - k, 1), pltpu.roll(tile, 127, 1))


def edges_kernel(adjoint_any, *refs):
    sends, (adjoint_ref, sem) = refs[:6], refs[6:]
    fetch = pltpu.make_async_copy(adjoint_any, adjoint_ref, sem)
    fetch.start()
    fetch.wait()
    pack(lambda v, x: adjoint_ref[v, x], 5, sends)


def flux_kernel(wall_any, map_any, adjoint_any, jacobian_any, face_any, stiff_any, *refs):
    halo, out_ref, sends = refs[:6], refs[6], refs[7:13]
    wall_ref, map_ref, adjoint_ref, jacobian_ref, face_ref, stiff_ref, total_ref, planes_ref, rows_ref, sems = refs[13:]
    copies = [
        pltpu.make_async_copy(wall_any, wall_ref, sems.at[0]),
        pltpu.make_async_copy(map_any, map_ref, sems.at[1]),
        pltpu.make_async_copy(adjoint_any, adjoint_ref, sems.at[2]),
        pltpu.make_async_copy(face_any, face_ref, sems.at[3]),
        pltpu.make_async_copy(stiff_any, stiff_ref, sems.at[4]),
    ]
    parts = [pltpu.make_async_copy(jacobian_any.at[e], jacobian_ref.at[e], sems.at[5 + e]) for e in range(7)]
    for copy in (copies[2], *parts, *copies[:2], copies[3], copies[4]):
        copy.start()
    lane, _ = iotas()
    on_wall = (lane == 0) & (lax.axis_index("normal") == 0)
    low, high = unpack(halo, planes_ref, rows_ref)
    tile_of = lambda v, x: adjoint_ref[v, x]
    copies[2].wait()
    for e in range(7):
        parts[e].wait()
        for x in range(CX):
            views = [neighbour(e, tile_of, p, x, planes_ref, rows_ref, low, high) for p in range(5)]
            total = [jnp.zeros((8, 128), F32) if e == 0 else total_ref[q, x] for q in range(5)]
            for p in range(5):
                for q in range(5):
                    total[q] = total[q] + jacobian_ref[e, p, q, x].astype(F32) * views[p]
            for q in range(5):
                total_ref[q, x] = total[q]
    for copy in (*copies[:2], *copies[3:]):
        copy.wait()
    square = lax.broadcasted_iota(jnp.int32, (8, 8), 0) == lax.broadcasted_iota(jnp.int32, (8, 8), 1)
    for x in range(CX):
        total = [total_ref[q, x] for q in range(5)]
        faces = jnp.broadcast_to(face_ref[x : x + 1, :], (8, 8)).astype(F32)
        face = jnp.sum(jnp.where(square, faces, 0.0), axis=1, keepdims=True)
        face = jnp.broadcast_to(face, (8, 128))
        for t in range(3):
            mask = on_wall & (face == float(t))
            for p in range(5):
                part = jnp.where(mask, adjoint_ref[p, x], 0.0)
                for q in range(5):
                    total[q] = total[q] + wall_ref[p, t, q] * part
        inverse = inverse_diagonal(stiff_ref, x)
        for r in range(3):
            sens = map_ref[r, 0] * total[0]
            for q in range(1, 5):
                sens = sens + map_ref[r, q] * total[q]
            out_ref[r, x] = sens * inverse
    pack(lambda v, x: out_ref[v, x], 3, sends)


def inverse_diagonal(stiff_ref, x):
    diagonal = stiff_ref[0, x]
    for e in range(1, 7):
        diagonal = diagonal + stiff_ref[e, x]
    return 1.0 / diagonal


def sweep(now_ref, start_ref, stiff_ref, halo, planes_ref, rows_ref, store):
    low, high = unpack(halo, planes_ref, rows_ref)
    tile_of = lambda v, x: now_ref[v, x]
    for x in range(CX):
        inverse = inverse_diagonal(stiff_ref, x)
        for v in range(3):
            total = stiff_ref[1, x] * neighbour(1, tile_of, v, x, planes_ref, rows_ref, low, high)
            for e in range(2, 7):
                total = total + stiff_ref[e, x] * neighbour(e, tile_of, v, x, planes_ref, rows_ref, low, high)
            store(v, x, start_ref[v, x] + total * inverse)


def middle_kernel(start_ref, stiff_ref, *refs):
    halo, out_ref, sends, planes_ref, rows_ref = refs[:6], refs[6], refs[7:13], *refs[13:]

    def store(v, x, tile):
        out_ref[v, x] = tile

    sweep(start_ref, start_ref, stiff_ref, halo, planes_ref, rows_ref, store)
    pack(lambda v, x: out_ref[v, x], 3, sends)


def window_kernel(box_ref, corner_ref, now_ref, start_ref, stiff_ref, bz_ref, by_ref, bx_ref, *refs):
    halo, out_ref, send_ref, planes_ref, rows_ref, flat_ref = refs[:6], *refs[6:]

    def store(v, x, tile):
        out_ref[v, x] = tile
        base = (v * CX + x) * CY
        flat_ref[base : base + CY, :] = tile

    sweep(now_ref, start_ref, stiff_ref, halo, planes_ref, rows_ref, store)
    inner = jnp.dot(flat_ref[...], bz_ref[...], precision=HIGHEST, preferred_element_type=F32)
    inner = inner * jnp.concatenate([by_ref[...]] * 24, axis=0)
    window = jnp.dot(bx_ref[...], inner, precision=HIGHEST, preferred_element_type=F32)
    lane = lax.broadcasted_iota(jnp.int32, (SLOT, 128), 1)
    row = lax.broadcasted_iota(jnp.int32, (SLOT, 128), 0)
    box = box_ref[0]
    oa, ob, oc = corner_ref[0], corner_ref[1], corner_ref[2]
    window = jnp.where(lax.rem(lane, 16) < 8, window[0:SLOT], window[SLOT : 2 * SLOT])
    shift = oc + 16 * lax.rem(ob, 8)
    window = pltpu.roll(window, shift, 1)
    inside = lax.rem(lane - shift + 128, 16) < 8
    block = jnp.where(inside, lax.div(ob, 8) + jnp.where(lane < shift, 1, 0), -1)
    for s in range(16):
        where = jnp.where(box == s, block, -1)
        there = jnp.where(row == 12, where, oa).astype(F32)
        there = jnp.where(row < 12, window, there)
        send_ref[2 * s] = there
        send_ref[2 * s + 1] = there


def place_kernel(got_ref, send_ref, wide_ref):
    half = lax.div(lax.axis_index("normal"), 2)
    where = got_ref[pl.ds(12, WINDOWS, stride=SLOT), :]
    start = got_ref[pl.ds(13, WINDOWS, stride=SLOT), :]
    lane = lax.broadcasted_iota(jnp.int32, (WINDOWS, 128), 1)
    row = lax.broadcasted_iota(jnp.int32, (WINDOWS, 128), 0)
    start = jnp.sum(jnp.where(lax.rem(lane, WINDOWS) == row, start, 0.0), axis=0, keepdims=True)
    step = lax.div(lax.broadcasted_iota(jnp.int32, (1, 128), 1), WINDOWS).astype(F32)
    first = start + step
    line = lax.broadcasted_iota(jnp.int32, (64, 128), 0)
    chunk = lax.div(line, 8)
    owner = lax.div(chunk, 2) * 4 + half * 2 + lax.rem(chunk, 2)
    point = jnp.where(lax.rem(line, 8) < ROWS, owner * ROWS + lax.rem(line, 8), -1).astype(F32)
    hits = jnp.concatenate(
        [jnp.where(point == jnp.broadcast_to(first + 4.0 * h, (64, 128)), 1.0, 0.0) for h in range(2)], axis=1
    )
    masks = [where == float(block) for block in range(4)]
    for r in range(3):
        for a in range(4):
            tile = got_ref[pl.ds(r * 4 + a, WINDOWS, stride=SLOT), :]
            for h in range(2):
                base = (h * 4 + a) * WINDOWS
                view = pltpu.roll(tile, 120, 1) if h else tile
                for block in range(4):
                    wide_ref[r, base : base + WINDOWS, block * 128 : block * 128 + 128] = jnp.where(
                        masks[block], view, 0.0
                    )
        placed = jnp.dot(hits, wide_ref[r], precision=HIGHEST, preferred_element_type=F32)
        for i in range(8):
            for block in range(4):
                base = (r * 4 + block) * ROWS
                send_ref[i, base : base + ROWS, :] = placed[
                    i * 8 : i * 8 + ROWS, block * 128 : block * 128 + 128
                ]


def sum_kernel(got_ref, out_ref, total_ref):
    total = got_ref[0]
    for j in range(1, 8):
        total = total + got_ref[j]
    total_ref[...] = total
    for r in range(3):
        for block in range(4):
            for a in range(ROWS):
                base = a * 512 + block * 128
                at = (r * 4 + block) * ROWS + a
                out_ref[r, 0:1, base : base + 128] = total_ref[at : at + 1, :]


VMEM = pl.BlockSpec(memory_space=pltpu.VMEM)
SMEM = pl.BlockSpec(memory_space=pltpu.SMEM)


def shape(*dims):
    return jax.ShapeDtypeStruct(dims, F32)


def call(body, outs, ins, scratch=(), scalars=0, limit=24 << 20, remote=()):
    specs = [SMEM] * scalars + [VMEM] * (len(ins) - scalars)
    for at in remote:
        specs[at] = HBM
    return pl.pallas_call(
        body,
        out_shape=outs,
        in_specs=specs,
        out_specs=jax.tree.map(lambda _: VMEM, outs),
        scratch_shapes=[pltpu.VMEM(a, F32) if isinstance(a, tuple) else a for a in scratch],
        compiler_params=pltpu.CompilerParams(vmem_limit_bytes=limit),
    )(*ins)


def in_hbm(one):
    return pltpu.with_memory_space_constraint(one, pltpu.HBM)


HBM = pl.BlockSpec(memory_space=pltpu.HBM)
DMA = pltpu.SemaphoreType.DMA


AXES = {"s": "span", "c": "chord", "n": "normal"}


def pairing(axis, start):
    pairs = [(i, i + 1) for i in range(start, lax.axis_size(axis) - 1, 2)]
    return pairs + [(j, i) for i, j in pairs]


def swap(*sends):
    got = []
    for at, one in enumerate(sends):
        name = "scn"[at // 2]
        got.append(lax.ppermute(one, AXES[name], pairing(AXES[name], at % 2)))
    return got


def ffd_groups():
    index = np.arange(256).reshape(16, 4, 2, 2)
    owners = index.transpose(1, 3, 0, 2).reshape(8, 32).tolist()
    sharers = index.transpose(0, 2, 1, 3).reshape(32, 8).tolist()
    return owners, sharers


def ends(v):
    return (shape(v, 8, 128),) * 2 + (shape(v * 8, 128),) * 2 + (shape(8, 128),) * 2


def local(adjoint, jacobian, wall_table, face_type, mesh_map, stiffness, box_map, offsets):
    block = shape(3, CX, CY, CZ)
    out = call(edges_kernel, ends(5), (in_hbm(adjoint),), scratch=((5, CX, CY, CZ), DMA), remote=(0,))
    halo = swap(*out)
    fixed = (wall_table.transpose(1, 0, 2), mesh_map, adjoint, jacobian, face_type, stiffness)
    spaces = (pltpu.SMEM, pltpu.SMEM) + (pltpu.VMEM,) * 4
    start, *out = call(
        flux_kernel,
        (block, *ends(3)),
        (*map(in_hbm, fixed), *halo),
        scratch=(
            *(space(one.shape, one.dtype) for space, one in zip(spaces, fixed)),
            (5, CX, CY, CZ),
            (2, 5, 8, 128),
            (2, 40, 128),
            DMA((12,)),
        ),
        remote=range(6),
    )
    halo = swap(*out)
    kept = ((2, 3, 8, 128), (2, 24, 128))
    middle, *out = call(middle_kernel, (block, *ends(3)), (start, stiffness, *halo), scratch=kept)
    halo = swap(*out)
    bz, by, bx = tables()
    final, windows = call(
        window_kernel,
        (block, shape(WINDOWS, SLOT, 128)),
        (box_map.reshape(1), offsets.reshape(3), middle, start, stiffness, bz, by, bx, *halo),
        scratch=(*kept, (192, 128)),
        scalars=2,
    )
    owners, sharers = ffd_groups()
    got = lax.all_to_all(windows, ALL, 0, 0, axis_index_groups=owners, tiled=True)
    chunks = call(place_kernel, shape(8, 72, 128), (got.reshape(WINDOWS * SLOT, 128),), scratch=((3, 256, 512),))
    got = lax.all_to_all(chunks, ALL, 0, 0, axis_index_groups=sharers, tiled=True)
    grad = call(sum_kernel, shape(3, 1, 3072), (got,), scratch=((72, 128),))
    return final, grad.reshape(1, 3, 3072)


def solution(mesh):
    placed = (
        P(None, "span", "chord", "normal"),
        P(None, None, None, "span", "chord", "normal"),
        P(),
        P("span", "chord"),
        P(),
        P(None, "span", "chord", "normal"),
        P("span", "chord", "normal"),
        P("span", "chord", "normal", None),
    )
    return jax.shard_map(
        local,
        mesh=mesh,
        in_specs=placed,
        out_specs=(P(None, "span", "chord", "normal"), P("span", None, ("chord", "normal"))),
        check_vma=False,
    )
```

profile of v0, /device:TPU:1, one launch (start us, length us, event | category | flops | bytes accessed | tf_op | source)
XLA Modules:
  0.0 90.0 jit_solution(4089195664202412269)
XLA Ops:
  0.6 0.0 copy-start.2
  0.6 0.0 copy-start.3
  0.7 0.0 copy-start.1
  0.7 0.0 copy-start
  0.7 1.2 %shard_map.122 = (f32[5,8,128]{2,1,0:T(8,128)S(1)}, f32[5,8,128]{2,1,0:T(8,128)S(1)}, f32[40,128]{1,0:T(8,128)S(1)}, f32[40,128]{1,0:T(8,128)S(1)}, f32[8,128]{1,0:T(8,128)S(1)}, /*index=5*/f32[8,128]{1,0:T(8,128)S(1)}) custom-call(f32[5,8,8,128]{3,2,1,0:T(8,128)} %adjoint_any.3), custom_call_target="tpu_custom_call" | custom-call | tf_op jit(solution)/shard_map/pallas_call | solution.py:284
  1.9 2.5 %collective-permute-start = (f32[5,8,128]{2,1,0:T(8,128)S(1)}, f32[5,8,128]{2,1,0:T(8,128)S(1)}, u32[]{:S(2)}, u32[]{:S(2)}) collective-permute-start(f32[5,8,128]{2,1,0:T(8,128)S(1)} %get-tuple-element.24), channel_id=1, source_target_pairs={{0,16},{32,48},{64,80},{96,112},{128,144},{160,176},{192,208},{224... | collective-permute-start | bytes 61448 | tf_op jit(solution)/shard_map/ppermute | solution.py:314
  4.4 0.7 collective-permute-start.1
  5.1 1.3 %collective-permute-start.2 = (f32[40,128]{1,0:T(8,128)S(1)}, f32[40,128]{1,0:T(8,128)S(1)}, u32[]{:S(2)}, u32[]{:S(2)}) collective-permute-start(f32[40,128]{1,0:T(8,128)S(1)} %get-tuple-element.26), channel_id=1, source_target_pairs={{0,4},{8,12},{4,0},{12,8},{1,5},{9,13},{5,1},{13,9},{2,6},{10,14},... | collective-permute-start | bytes 61448 | tf_op jit(solution)/shard_map/ppermute | solution.py:314
  6.3 0.7 collective-permute-start.3
  7.0 1.3 %collective-permute-start.4 = (f32[8,128]{1,0:T(8,128)S(1)}, f32[8,128]{1,0:T(8,128)S(1)}, u32[]{:S(2)}, u32[]{:S(2)}) collective-permute-start(f32[8,128]{1,0:T(8,128)S(1)} %get-tuple-element.28), channel_id=1, source_target_pairs={{0,1},{2,3},{1,0},{3,2},{4,5},{6,7},{5,4},{7,6},{8,9},{10,11},{9,8... | collective-permute-start | bytes 12296 | tf_op jit(solution)/shard_map/ppermute | solution.py:314
  8.3 0.8 collective-permute-done.4.refs_4_
  9.2 5.0 %collective-permute-start.5 = (f32[8,128]{1,0:T(8,128)S(1)}, f32[8,128]{1,0:T(8,128)S(1)}, u32[]{:S(2)}, u32[]{:S(2)}) collective-permute-start(f32[8,128]{1,0:T(8,128)S(1)} %get-tuple-element.29), channel_id=1, source_target_pairs={{1,2},{2,1},{5,6},{6,5},{9,10},{10,9},{13,14},{14,13},{17,18},{18,... | collective-permute-start | bytes 12296 | tf_op jit(solution)/shard_map/ppermute | solution.py:314
  14.2 1.4 %collective-permute-done.5.refs_5_ = f32[8,128]{1,0:T(8,128)S(1)} collective-permute-done((f32[8,128]{1,0:T(8,128)S(1)}, f32[8,128]{1,0:T(8,128)S(1)}, u32[]{:S(2)}, u32[]{:S(2)}) %collective-permute-start.5) | collective-permute-done | bytes 4128 | tf_op jit(solution)/shard_map/ppermute | solution.py:314
  15.6 0.0 collective-permute-done.refs_0_
  15.6 0.0 collective-permute-done.1.refs_1_
  15.6 0.0 collective-permute-done.2.refs_2_
  15.6 0.0 collective-permute-done.3.refs_3_
  15.6 2.6 %shard_map.123 = (f32[3,8,8,128]{3,2,1,0:T(8,128)S(1)}, f32[3,8,128]{2,1,0:T(8,128)S(1)}, f32[3,8,128]{2,1,0:T(8,128)S(1)}, f32[24,128]{1,0:T(8,128)S(1)}, f32[2...) custom-call(f32[5,3,5]{2,1,0:T(4,128)} %bitcast.9, f32[3,5]{1,0:T(4,128)} %map_any.1, ...), custom_call_target="tpu_custom_call" | custom-call | tf_op jit(solution)/shard_map/pallas_call | solution.py:284
  18.2 4.9 %collective-permute-start.6 = (f32[3,8,128]{2,1,0:T(8,128)S(1)}, f32[3,8,128]{2,1,0:T(8,128)S(1)}, u32[]{:S(2)}, u32[]{:S(2)}) collective-permute-start(f32[3,8,128]{2,1,0:T(8,128)S(1)} %get-tuple-element.31), channel_id=1, source_target_pairs={{0,16},{32,48},{64,80},{96,112},{128,144},{160,176},{192,208},{224... | collective-permute-start | bytes 36872 | tf_op jit(solution)/shard_map/ppermute | solution.py:314
  23.1 0.7 collective-permute-start.7
  23.8 3.7 %collective-permute-start.8 = (f32[24,128]{1,0:T(8,128)S(1)}, f32[24,128]{1,0:T(8,128)S(1)}, u32[]{:S(2)}, u32[]{:S(2)}) collective-permute-start(f32[24,128]{1,0:T(8,128)S(1)} %get-tuple-element.33), channel_id=1, source_target_pairs={{0,4},{8,12},{4,0},{12,8},{1,5},{9,13},{5,1},{13,9},{2,6},{10,14},... | collective-permute-start | bytes 36872 | tf_op jit(solution)/shard_map/ppermute | solution.py:314
  27.5 0.7 collective-permute-start.9
  28.2 0.1 collective-permute-start.10
  28.3 1.2 %collective-permute-done.10.refs_4_ = f32[8,128]{1,0:T(8,128)S(1)} collective-permute-done((f32[8,128]{1,0:T(8,128)S(1)}, f32[8,128]{1,0:T(8,128)S(1)}, u32[]{:S(2)}, u32[]{:S(2)}) %collective-permute-start.10) | collective-permute-done | bytes 4128 | tf_op jit(solution)/shard_map/ppermute | solution.py:314
  29.4 5.6 %collective-permute-start.11 = (f32[8,128]{1,0:T(8,128)S(1)}, f32[8,128]{1,0:T(8,128)S(1)}, u32[]{:S(2)}, u32[]{:S(2)}) collective-permute-start(f32[8,128]{1,0:T(8,128)S(1)} %get-tuple-element.36), channel_id=1, source_target_pairs={{1,2},{2,1},{5,6},{6,5},{9,10},{10,9},{13,14},{14,13},{17,18},{18,... | collective-permute-start | bytes 12296 | tf_op jit(solution)/shard_map/ppermute | solution.py:314
  35.1 1.3 %collective-permute-done.11.refs_5_ = f32[8,128]{1,0:T(8,128)S(1)} collective-permute-done((f32[8,128]{1,0:T(8,128)S(1)}, f32[8,128]{1,0:T(8,128)S(1)}, u32[]{:S(2)}, u32[]{:S(2)}) %collective-permute-start.11) | collective-permute-done | bytes 4128 | tf_op jit(solution)/shard_map/ppermute | solution.py:314
  36.3 0.0 collective-permute-done.6.refs_0_
  36.3 0.0 collective-permute-done.7.refs_1_
  36.3 0.0 collective-permute-done.8.refs_2_
  36.3 0.0 collective-permute-done.9.refs_3_
  36.4 0.3 shard_map.124
  36.6 5.2 %collective-permute-start.12 = (f32[3,8,128]{2,1,0:T(8,128)S(1)}, f32[3,8,128]{2,1,0:T(8,128)S(1)}, u32[]{:S(2)}, u32[]{:S(2)}) collective-permute-start(f32[3,8,128]{2,1,0:T(8,128)S(1)} %get-tuple-element.38), channel_id=1, source_target_pairs={{0,16},{32,48},{64,80},{96,112},{128,144},{160,176},{192,208},{224... | collective-permute-start | bytes 36872 | tf_op jit(solution)/shard_map/ppermute | solution.py:314
  41.8 0.7 collective-permute-start.13
  42.5 1.1 %collective-permute-start.14 = (f32[24,128]{1,0:T(8,128)S(1)}, f32[24,128]{1,0:T(8,128)S(1)}, u32[]{:S(2)}, u32[]{:S(2)}) collective-permute-start(f32[24,128]{1,0:T(8,128)S(1)} %get-tuple-element.40), channel_id=1, source_target_pairs={{0,4},{8,12},{4,0},{12,8},{1,5},{9,13},{5,1},{13,9},{2,6},{10,14},... | collective-permute-start | bytes 36872 | tf_op jit(solution)/shard_map/ppermute | solution.py:314
  43.6 0.7 collective-permute-start.15
  44.3 0.1 collective-permute-start.16
  44.4 1.2 %collective-permute-done.16.refs_4_ = f32[8,128]{1,0:T(8,128)S(1)} collective-permute-done((f32[8,128]{1,0:T(8,128)S(1)}, f32[8,128]{1,0:T(8,128)S(1)}, u32[]{:S(2)}, u32[]{:S(2)}) %collective-permute-start.16) | collective-permute-done | bytes 4128 | tf_op jit(solution)/shard_map/ppermute | solution.py:314
  45.5 5.7 %collective-permute-start.17 = (f32[8,128]{1,0:T(8,128)S(1)}, f32[8,128]{1,0:T(8,128)S(1)}, u32[]{:S(2)}, u32[]{:S(2)}) collective-permute-start(f32[8,128]{1,0:T(8,128)S(1)} %get-tuple-element.43), channel_id=1, source_target_pairs={{1,2},{2,1},{5,6},{6,5},{9,10},{10,9},{13,14},{14,13},{17,18},{18,... | collective-permute-start | bytes 12296 | tf_op jit(solution)/shard_map/ppermute | solution.py:314
  51.9 0.6 collective-permute-done.17.refs_5_
  52.5 0.0 collective-permute-done.12.refs_0_
  52.5 0.0 collective-permute-done.13.refs_1_
  52.5 0.0 collective-permute-done.14.refs_2_
  52.5 0.0 collective-permute-done.15.refs_3_
  52.5 1.4 %shard_map.125 = (f32[3,8,8,128]{3,2,1,0:T(8,128)}, f32[32,16,128]{2,1,0:T(8,128)S(1)}) custom-call(s32[1]{0:T(128)} %bitcast.5.box_ref, s32[3]{0:T(128)S(1)} %bitcast.7, f32[3,8,8,128]{3,2,1,0:T(8,128)S(1)} %get-tuple-element.37.now_ref, f32[3,8,8,128]{3,2,1,0:T(8,128)S(1)} %get-tuple-element.30.start_ref, f32[7,8,8,128]{3,2,1,0:T(8,128)S(1)} %copy-done, ...), custom_call_target="tpu_custom_call" | custom-call | tf_op jit(solution)/shard_map/pallas_call | solution.py:284
  53.9 17.6 %all_to_all.10 = f32[32,16,128]{2,1,0:T(8,128)S(1)} all-to-all(f32[32,16,128]{2,1,0:T(8,128)S(1)} %get-tuple-element.45), channel_id=1, replica_groups={{0,2,16,18,32,34,48,50,64,66,80,82,96,98,112,114,128,130,144,146,160,16..., dimensions={0} | all-to-all | bytes 524288 | tf_op jit(solution)/shard_map/all_to_all | solution.py:361
  71.5 1.1 %shard_map.126 = f32[8,72,128]{2,1,0:T(8,128)S(1)} custom-call(f32[512,128]{1,0:T(8,128)S(1)} %bitcast.6), custom_call_target="tpu_custom_call" | custom-call | tf_op jit(solution)/shard_map/pallas_call | solution.py:284
  72.6 16.7 %all_to_all.11.got_ref = f32[8,72,128]{2,1,0:T(8,128)S(1)} all-to-all(f32[8,72,128]{2,1,0:T(8,128)S(1)} %shard_map.126), channel_id=1, replica_groups={{0,1,4,5,8,9,12,13},{2,3,6,7,10,11,14,15},{16,17,20,21,24,25,28,29},{18..., dimensions={0} | all-to-all | bytes 589824 | tf_op jit(solution)/shard_map/all_to_all | solution.py:363
  89.3 0.7 shard_map.127
  (6 shorter events, 0.0 us)
Async XLA Ops:
  0.6 51.9 %copy-start.2 = (f32[32,192]{1,0:T(8,128)S(1)}, f32[32,192]{1,0:T(8,128)}, u32[]{:S(2)}) copy-start(f32[32,192]{1,0:T(8,128)} %constant.8.clone.bx_ref) | copy-start | bytes 73732
  0.6 51.9 %copy-start.3 = (f32[8,128]{1,0:T(8,128)S(1)}, f32[8,128]{1,0:T(8,128)}, u32[]{:S(2)}) copy-start(f32[8,128]{1,0:T(8,128)} %constant.7.clone.by_ref) | copy-start | bytes 12292
  0.7 51.9 %copy-start.1 = (f32[128,128]{1,0:T(8,128)S(1)}, f32[128,128]{1,0:T(8,128)}, u32[]{:S(2)}) copy-start(f32[128,128]{1,0:T(8,128)} %constant.6.clone.bz_ref) | copy-start | bytes 196612
  0.7 35.7 %copy-start = (f32[7,8,8,128]{3,2,1,0:T(8,128)S(1)}, f32[7,8,8,128]{3,2,1,0:T(8,128)}, u32[]{:S(2)}) copy-start(f32[7,8,8,128]{3,2,1,0:T(8,128)} %stiff_ref.3) | copy-start | bytes 688132
  0.7 51.9 %copy-start.4 = (s32[1,1,1,3]{3,2,1,0:T(1,128)S(1)}, s32[1,1,1,3]{3,2,1,0:T(1,128)}, u32[]{:S(2)}) copy-start(s32[1,1,1,3]{3,2,1,0:T(1,128)} %param.18) | copy-start | bytes 40
  1.9 13.7 %collective-permute-start = (f32[5,8,128]{2,1,0:T(8,128)S(1)}, f32[5,8,128]{2,1,0:T(8,128)S(1)}, u32[]{:S(2)}, u32[]{:S(2)}) collective-permute-start(f32[5,8,128]{2,1,0:T(8,128)S(1)} %get-tuple-element.24), channel_id=1, source_target_pairs={{0,16},{32,48},{64,80},{96,112},{128,144},{160,176},{192,208},{224... | collective-permute-start | bytes 61448 | tf_op jit(solution)/shard_map/ppermute | solution.py:314
  4.4 11.2 %collective-permute-start.1 = (f32[5,8,128]{2,1,0:T(8,128)S(1)}, f32[5,8,128]{2,1,0:T(8,128)S(1)}, u32[]{:S(2)}, u32[]{:S(2)}) collective-permute-start(f32[5,8,128]{2,1,0:T(8,128)S(1)} %get-tuple-element.25), channel_id=1, source_target_pairs={{16,32},{48,64},{80,96},{112,128},{144,160},{176,192},{208,224},{3... | collective-permute-start | bytes 61448 | tf_op jit(solution)/shard_map/ppermute | solution.py:314
  5.1 10.5 %collective-permute-start.2 = (f32[40,128]{1,0:T(8,128)S(1)}, f32[40,128]{1,0:T(8,128)S(1)}, u32[]{:S(2)}, u32[]{:S(2)}) collective-permute-start(f32[40,128]{1,0:T(8,128)S(1)} %get-tuple-element.26), channel_id=1, source_target_pairs={{0,4},{8,12},{4,0},{12,8},{1,5},{9,13},{5,1},{13,9},{2,6},{10,14},... | collective-permute-start | bytes 61448 | tf_op jit(solution)/shard_map/ppermute | solution.py:314
  6.3 9.2 %collective-permute-start.3 = (f32[40,128]{1,0:T(8,128)S(1)}, f32[40,128]{1,0:T(8,128)S(1)}, u32[]{:S(2)}, u32[]{:S(2)}) collective-permute-start(f32[40,128]{1,0:T(8,128)S(1)} %get-tuple-element.27), channel_id=1, source_target_pairs={{4,8},{8,4},{5,9},{9,5},{6,10},{10,6},{7,11},{11,7},{20,24},{24,20... | collective-permute-start | bytes 61448 | tf_op jit(solution)/shard_map/ppermute | solution.py:314
  7.0 2.1 %collective-permute-start.4 = (f32[8,128]{1,0:T(8,128)S(1)}, f32[8,128]{1,0:T(8,128)S(1)}, u32[]{:S(2)}, u32[]{:S(2)}) collective-permute-start(f32[8,128]{1,0:T(8,128)S(1)} %get-tuple-element.28), channel_id=1, source_target_pairs={{0,1},{2,3},{1,0},{3,2},{4,5},{6,7},{5,4},{7,6},{8,9},{10,11},{9,8... | collective-permute-start | bytes 12296 | tf_op jit(solution)/shard_map/ppermute | solution.py:314
  9.2 6.4 %collective-permute-start.5 = (f32[8,128]{1,0:T(8,128)S(1)}, f32[8,128]{1,0:T(8,128)S(1)}, u32[]{:S(2)}, u32[]{:S(2)}) collective-permute-start(f32[8,128]{1,0:T(8,128)S(1)} %get-tuple-element.29), channel_id=1, source_target_pairs={{1,2},{2,1},{5,6},{6,5},{9,10},{10,9},{13,14},{14,13},{17,18},{18,... | collective-permute-start | bytes 12296 | tf_op jit(solution)/shard_map/ppermute | solution.py:314
  18.2 18.1 %collective-permute-start.6 = (f32[3,8,128]{2,1,0:T(8,128)S(1)}, f32[3,8,128]{2,1,0:T(8,128)S(1)}, u32[]{:S(2)}, u32[]{:S(2)}) collective-permute-start(f32[3,8,128]{2,1,0:T(8,128)S(1)} %get-tuple-element.31), channel_id=1, source_target_pairs={{0,16},{32,48},{64,80},{96,112},{128,144},{160,176},{192,208},{224... | collective-permute-start | bytes 36872 | tf_op jit(solution)/shard_map/ppermute | solution.py:314
  23.1 13.2 %collective-permute-start.7 = (f32[3,8,128]{2,1,0:T(8,128)S(1)}, f32[3,8,128]{2,1,0:T(8,128)S(1)}, u32[]{:S(2)}, u32[]{:S(2)}) collective-permute-start(f32[3,8,128]{2,1,0:T(8,128)S(1)} %get-tuple-element.32), channel_id=1, source_target_pairs={{16,32},{48,64},{80,96},{112,128},{144,160},{176,192},{208,224},{3... | collective-permute-start | bytes 36872 | tf_op jit(solution)/shard_map/ppermute | solution.py:314
  23.8 12.5 %collective-permute-start.8 = (f32[24,128]{1,0:T(8,128)S(1)}, f32[24,128]{1,0:T(8,128)S(1)}, u32[]{:S(2)}, u32[]{:S(2)}) collective-permute-start(f32[24,128]{1,0:T(8,128)S(1)} %get-tuple-element.33), channel_id=1, source_target_pairs={{0,4},{8,12},{4,0},{12,8},{1,5},{9,13},{5,1},{13,9},{2,6},{10,14},... | collective-permute-start | bytes 36872 | tf_op jit(solution)/shard_map/ppermute | solution.py:314
  27.5 8.8 %collective-permute-start.9 = (f32[24,128]{1,0:T(8,128)S(1)}, f32[24,128]{1,0:T(8,128)S(1)}, u32[]{:S(2)}, u32[]{:S(2)}) collective-permute-start(f32[24,128]{1,0:T(8,128)S(1)} %get-tuple-element.34), channel_id=1, source_target_pairs={{4,8},{8,4},{5,9},{9,5},{6,10},{10,6},{7,11},{11,7},{20,24},{24,20... | collective-permute-start | bytes 36872 | tf_op jit(solution)/shard_map/ppermute | solution.py:314
  28.2 1.3 %collective-permute-start.10 = (f32[8,128]{1,0:T(8,128)S(1)}, f32[8,128]{1,0:T(8,128)S(1)}, u32[]{:S(2)}, u32[]{:S(2)}) collective-permute-start(f32[8,128]{1,0:T(8,128)S(1)} %get-tuple-element.35), channel_id=1, source_target_pairs={{0,1},{2,3},{1,0},{3,2},{4,5},{6,7},{5,4},{7,6},{8,9},{10,11},{9,8... | collective-permute-start | bytes 12296 | tf_op jit(solution)/shard_map/ppermute | solution.py:314
  29.4 6.9 %collective-permute-start.11 = (f32[8,128]{1,0:T(8,128)S(1)}, f32[8,128]{1,0:T(8,128)S(1)}, u32[]{:S(2)}, u32[]{:S(2)}) collective-permute-start(f32[8,128]{1,0:T(8,128)S(1)} %get-tuple-element.36), channel_id=1, source_target_pairs={{1,2},{2,1},{5,6},{6,5},{9,10},{10,9},{13,14},{14,13},{17,18},{18,... | collective-permute-start | bytes 12296 | tf_op jit(solution)/shard_map/ppermute | solution.py:314
  36.6 15.8 %collective-permute-start.12 = (f32[3,8,128]{2,1,0:T(8,128)S(1)}, f32[3,8,128]{2,1,0:T(8,128)S(1)}, u32[]{:S(2)}, u32[]{:S(2)}) collective-permute-start(f32[3,8,128]{2,1,0:T(8,128)S(1)} %get-tuple-element.38), channel_id=1, source_target_pairs={{0,16},{32,48},{64,80},{96,112},{128,144},{160,176},{192,208},{224... | collective-permute-start | bytes 36872 | tf_op jit(solution)/shard_map/ppermute | solution.py:314
  41.8 10.6 %collective-permute-start.13 = (f32[3,8,128]{2,1,0:T(8,128)S(1)}, f32[3,8,128]{2,1,0:T(8,128)S(1)}, u32[]{:S(2)}, u32[]{:S(2)}) collective-permute-start(f32[3,8,128]{2,1,0:T(8,128)S(1)} %get-tuple-element.39), channel_id=1, source_target_pairs={{16,32},{48,64},{80,96},{112,128},{144,160},{176,192},{208,224},{3... | collective-permute-start | bytes 36872 | tf_op jit(solution)/shard_map/ppermute | solution.py:314
  42.5 10.0 %collective-permute-start.14 = (f32[24,128]{1,0:T(8,128)S(1)}, f32[24,128]{1,0:T(8,128)S(1)}, u32[]{:S(2)}, u32[]{:S(2)}) collective-permute-start(f32[24,128]{1,0:T(8,128)S(1)} %get-tuple-element.40), channel_id=1, source_target_pairs={{0,4},{8,12},{4,0},{12,8},{1,5},{9,13},{5,1},{13,9},{2,6},{10,14},... | collective-permute-start | bytes 36872 | tf_op jit(solution)/shard_map/ppermute | solution.py:314
  43.6 8.9 %collective-permute-start.15 = (f32[24,128]{1,0:T(8,128)S(1)}, f32[24,128]{1,0:T(8,128)S(1)}, u32[]{:S(2)}, u32[]{:S(2)}) collective-permute-start(f32[24,128]{1,0:T(8,128)S(1)} %get-tuple-element.41), channel_id=1, source_target_pairs={{4,8},{8,4},{5,9},{9,5},{6,10},{10,6},{7,11},{11,7},{20,24},{24,20... | collective-permute-start | bytes 36872 | tf_op jit(solution)/shard_map/ppermute | solution.py:314
  44.3 1.3 %collective-permute-start.16 = (f32[8,128]{1,0:T(8,128)S(1)}, f32[8,128]{1,0:T(8,128)S(1)}, u32[]{:S(2)}, u32[]{:S(2)}) collective-permute-start(f32[8,128]{1,0:T(8,128)S(1)} %get-tuple-element.42), channel_id=1, source_target_pairs={{0,1},{2,3},{1,0},{3,2},{4,5},{6,7},{5,4},{7,6},{8,9},{10,11},{9,8... | collective-permute-start | bytes 12296 | tf_op jit(solution)/shard_map/ppermute | solution.py:314
  45.5 7.0 %collective-permute-start.17 = (f32[8,128]{1,0:T(8,128)S(1)}, f32[8,128]{1,0:T(8,128)S(1)}, u32[]{:S(2)}, u32[]{:S(2)}) collective-permute-start(f32[8,128]{1,0:T(8,128)S(1)} %get-tuple-element.43), channel_id=1, source_target_pairs={{1,2},{2,1},{5,6},{6,5},{9,10},{10,9},{13,14},{14,13},{17,18},{18,... | collective-permute-start | bytes 12296 | tf_op jit(solution)/shard_map/ppermute | solution.py:314
where the time goes:
time: 90.4 us; the launch traced here: 90 us
  starting transfers between devices  40.5 us (45%)
  blocking collectives  34.3 us (38%)
  Pallas kernels  7.24 us (8%)
  waiting for transfers between devices  6.44 us (7%)
  between operations  1.51 us (2%)
    ppermute x18, starting transfers between devices, swap(): got.append(lax.ppermute(one, AXES[name], pairing(AXES[name], at % 2)))  40.5 us
    all_to_all x1, blocking collectives, local(): lax.all_to_all(windows, ALL, 0, 0, axis_index_groups=owners, tiled=True)  17.6 us
    all_to_all x1, blocking collectives, local(): lax.all_to_all(chunks, ALL, 0, 0, axis_index_groups=sharers, tiled=True)  16.7 us
    pallas_call x6, Pallas kernels, call(): pl.pallas_call(body, out_shape=outs, in_specs=specs, out_specs=jax.tree.m...  7.24 us
    ppermute x18, waiting for transfers between devices, swap(): got.append(lax.ppermute(one, AXES[name], pairing(AXES[name], at % 2)))  6.44 us
  transfers between devices with their start and end apart: 18, of which 6 were waited for; matrix products, arithmetic and copies ran while one was open for 0% of the time, Pallas kernels for 0%

commit v1 on v0

--- a/solution.py
+++ b/solution.py
@@ -74,14 +74,19 @@
     zb[...] = pick(by_z, high, low)
 
 
+def inner(axis, low, high):
+    at = lax.axis_index(axis)
+    last = lax.axis_size(axis) - 1
+    zero = jnp.zeros(low.shape, F32)
+    return pick(at > 0, low, zero), pick(at < last, high, zero)
+
+
 def unpack(halo, planes_ref, rows_ref):
-    xa, xb, ya, yb, za, zb = halo
+    xa, xb, ya, yb, za, zb = (one[...] for one in halo)
     by_x, by_y, by_z = odd("span"), odd("chord"), odd("normal")
-    planes_ref[0] = pick(by_x, xa[...], xb[...])
-    planes_ref[1] = pick(by_x, xb[...], xa[...])
-    rows_ref[0] = pick(by_y, ya[...], yb[...])
-    rows_ref[1] = pick(by_y, yb[...], ya[...])
-    return pick(by_z, za[...], zb[...]), pick(by_z, zb[...], za[...])
+    planes_ref[0], planes_ref[1] = inner("span", pick(by_x, xa, xb), pick(by_x, xb, xa))
+    rows_ref[0], rows_ref[1] = inner("chord", pick(by_y, ya, yb), pick(by_y, yb, ya))
+    return inner("normal", pick(by_z, za, zb), pick(by_z, zb, za))
 
 
 def neighbour(e, tile_of, v, x, planes_ref, rows_ref, low, high):
@@ -303,7 +308,8 @@
 
 
 def pairing(axis, start):
-    pairs = [(i, i + 1) for i in range(start, lax.axis_size(axis) - 1, 2)]
+    count = lax.axis_size(axis)
+    pairs = [(i, (i + 1) % count) for i in range(start, count, 2)]
     return pairs + [(j, i) for i, j in pairs]
 
 

time: 90.4 us -> 77.6 us (0.86)
  starting transfers between devices: 40.5 us -> 31.4 us
  blocking collectives: 34.3 us -> 30.3 us
    ppermute x18, starting transfers between devices: 40.5 us -> 31.4 us  [swap(): got.append(lax.ppermute(one, AXES[name], pairing(AXES[name], at % 2)))]
    all_to_all x1, blocking collectives: 16.7 us -> 11.9 us  [local(): lax.all_to_all(chunks, ALL, 0, 0, axis_index_groups=sharers, tiled=True)]
where the time goes in v1:
time: 77.6 us; the launch traced here: 77.4 us
  starting transfers between devices  31.4 us (40%)
  blocking collectives  30.3 us (39%)
  Pallas kernels  7.25 us (9%)
  waiting for transfers between devices  6.91 us (9%)
  between operations  1.45 us (2%)
    ppermute x18, starting transfers between devices, swap(): got.append(lax.ppermute(one, AXES[name], pairing(AXES[name], at % 2)))  31.4 us
    all_to_all x1, blocking collectives, local(): lax.all_to_all(windows, ALL, 0, 0, axis_index_groups=owners, tiled=True)  18.4 us
    all_to_all x1, blocking collectives, local(): lax.all_to_all(chunks, ALL, 0, 0, axis_index_groups=sharers, tiled=True)  11.9 us
    pallas_call x6, Pallas kernels, call(): pl.pallas_call(body, out_shape=outs, in_specs=specs, out_specs=jax.tree.m...  7.25 us
    ppermute x18, waiting for transfers between devices, swap(): got.append(lax.ppermute(one, AXES[name], pairing(AXES[name], at % 2)))  6.91 us
  transfers between devices with their start and end apart: 18, of which 6 were waited for; matrix products, arithmetic and copies ran while one was open for 0% of the time, Pallas kernels for 0%

profile of v1, /device:TPU:1, one launch (start us, length us, event | category | flops | bytes accessed | tf_op | source)
XLA Modules:
  0.0 77.4 jit_solution(7283846689720464916)
XLA Ops:
  0.6 0.0 copy-start.2
  0.6 0.0 copy-start.3
  0.7 0.0 copy-start.1
  0.7 0.0 copy-start
  0.7 1.2 %shard_map.122 = (f32[5,8,128]{2,1,0:T(8,128)S(1)}, f32[5,8,128]{2,1,0:T(8,128)S(1)}, f32[40,128]{1,0:T(8,128)S(1)}, f32[40,128]{1,0:T(8,128)S(1)}, f32[8,128]{1,0:T(8,128)S(1)}, /*index=5*/f32[8,128]{1,0:T(8,128)S(1)}) custom-call(f32[5,8,8,128]{3,2,1,0:T(8,128)} %adjoint_any.3), custom_call_target="tpu_custom_call" | custom-call | tf_op jit(solution)/shard_map/pallas_call | solution.py:289
  1.9 2.5 %collective-permute-start = (f32[5,8,128]{2,1,0:T(8,128)S(1)}, f32[5,8,128]{2,1,0:T(8,128)S(1)}, u32[]{:S(2)}, u32[]{:S(2)}) collective-permute-start(f32[5,8,128]{2,1,0:T(8,128)S(1)} %get-tuple-element.24), channel_id=1, source_target_pairs={{0,16},{32,48},{64,80},{96,112},{128,144},{160,176},{192,208},{224... | collective-permute-start | bytes 61448 | tf_op jit(solution)/shard_map/ppermute | solution.py:320
  4.4 5.7 %collective-permute-start.1 = (f32[5,8,128]{2,1,0:T(8,128)S(1)}, f32[5,8,128]{2,1,0:T(8,128)S(1)}, u32[]{:S(2)}, u32[]{:S(2)}) collective-permute-start(f32[5,8,128]{2,1,0:T(8,128)S(1)} %get-tuple-element.25), channel_id=1, source_target_pairs={{16,32},{48,64},{80,96},{112,128},{144,160},{176,192},{208,224},{2... | collective-permute-start | bytes 61448 | tf_op jit(solution)/shard_map/ppermute | solution.py:320
  10.1 1.2 %collective-permute-start.2 = (f32[40,128]{1,0:T(8,128)S(1)}, f32[40,128]{1,0:T(8,128)S(1)}, u32[]{:S(2)}, u32[]{:S(2)}) collective-permute-start(f32[40,128]{1,0:T(8,128)S(1)} %get-tuple-element.26), channel_id=1, source_target_pairs={{0,4},{8,12},{4,0},{12,8},{1,5},{9,13},{5,1},{13,9},{2,6},{10,14},... | collective-permute-start | bytes 61448 | tf_op jit(solution)/shard_map/ppermute | solution.py:320
  11.3 1.8 %collective-permute-start.3 = (f32[40,128]{1,0:T(8,128)S(1)}, f32[40,128]{1,0:T(8,128)S(1)}, u32[]{:S(2)}, u32[]{:S(2)}) collective-permute-start(f32[40,128]{1,0:T(8,128)S(1)} %get-tuple-element.27), channel_id=1, source_target_pairs={{4,8},{12,0},{8,4},{0,12},{5,9},{13,1},{9,5},{1,13},{6,10},{14,2},... | collective-permute-start | bytes 61448 | tf_op jit(solution)/shard_map/ppermute | solution.py:320
  13.1 1.8 %collective-permute-start.4 = (f32[8,128]{1,0:T(8,128)S(1)}, f32[8,128]{1,0:T(8,128)S(1)}, u32[]{:S(2)}, u32[]{:S(2)}) collective-permute-start(f32[8,128]{1,0:T(8,128)S(1)} %get-tuple-element.28), channel_id=1, source_target_pairs={{0,1},{2,3},{1,0},{3,2},{4,5},{6,7},{5,4},{7,6},{8,9},{10,11},{9,8... | collective-permute-start | bytes 12296 | tf_op jit(solution)/shard_map/ppermute | solution.py:320
  14.9 0.8 %collective-permute-done.4.refs_4_ = f32[8,128]{1,0:T(8,128)S(1)} collective-permute-done((f32[8,128]{1,0:T(8,128)S(1)}, f32[8,128]{1,0:T(8,128)S(1)}, u32[]{:S(2)}, u32[]{:S(2)}) %collective-permute-start.4) | collective-permute-done | bytes 4128 | tf_op jit(solution)/shard_map/ppermute | solution.py:320
  15.7 2.8 %collective-permute-start.5 = (f32[8,128]{1,0:T(8,128)S(1)}, f32[8,128]{1,0:T(8,128)S(1)}, u32[]{:S(2)}, u32[]{:S(2)}) collective-permute-start(f32[8,128]{1,0:T(8,128)S(1)} %get-tuple-element.29), channel_id=1, source_target_pairs={{1,2},{3,0},{2,1},{0,3},{5,6},{7,4},{6,5},{4,7},{9,10},{11,8},{10,... | collective-permute-start | bytes 12296 | tf_op jit(solution)/shard_map/ppermute | solution.py:320
  18.6 1.7 %collective-permute-done.5.refs_5_ = f32[8,128]{1,0:T(8,128)S(1)} collective-permute-done((f32[8,128]{1,0:T(8,128)S(1)}, f32[8,128]{1,0:T(8,128)S(1)}, u32[]{:S(2)}, u32[]{:S(2)}) %collective-permute-start.5) | collective-permute-done | bytes 4128 | tf_op jit(solution)/shard_map/ppermute | solution.py:320
  20.3 0.0 collective-permute-done.refs_0_
  20.3 0.0 collective-permute-done.1.refs_1_
  20.3 0.0 collective-permute-done.2.refs_2_
  20.3 0.0 collective-permute-done.3.refs_3_
  20.3 2.6 %shard_map.123 = (f32[3,8,8,128]{3,2,1,0:T(8,128)S(1)}, f32[3,8,128]{2,1,0:T(8,128)S(1)}, f32[3,8,128]{2,1,0:T(8,128)S(1)}, f32[24,128]{1,0:T(8,128)S(1)}, f32[2...) custom-call(f32[5,3,5]{2,1,0:T(4,128)} %bitcast.9, f32[3,5]{1,0:T(4,128)} %map_any.1, ...), custom_call_target="tpu_custom_call" | custom-call | tf_op jit(solution)/shard_map/pallas_call | solution.py:289
  22.9 0.1 collective-permute-start.6
  23.0 1.4 %collective-permute-start.7 = (f32[3,8,128]{2,1,0:T(8,128)S(1)}, f32[3,8,128]{2,1,0:T(8,128)S(1)}, u32[]{:S(2)}, u32[]{:S(2)}) collective-permute-start(f32[3,8,128]{2,1,0:T(8,128)S(1)} %get-tuple-element.32), channel_id=1, source_target_pairs={{16,32},{48,64},{80,96},{112,128},{144,160},{176,192},{208,224},{2... | collective-permute-start | bytes 36872 | tf_op jit(solution)/shard_map/ppermute | solution.py:320
  24.5 0.3 collective-permute-start.8
  24.8 0.6 collective-permute-start.9
  25.3 1.2 %collective-permute-start.10 = (f32[8,128]{1,0:T(8,128)S(1)}, f32[8,128]{1,0:T(8,128)S(1)}, u32[]{:S(2)}, u32[]{:S(2)}) collective-permute-start(f32[8,128]{1,0:T(8,128)S(1)} %get-tuple-element.35), channel_id=1, source_target_pairs={{0,1},{2,3},{1,0},{3,2},{4,5},{6,7},{5,4},{7,6},{8,9},{10,11},{9,8... | collective-permute-start | bytes 12296 | tf_op jit(solution)/shard_map/ppermute | solution.py:320
  26.6 0.8 %collective-permute-done.10.refs_4_ = f32[8,128]{1,0:T(8,128)S(1)} collective-permute-done((f32[8,128]{1,0:T(8,128)S(1)}, f32[8,128]{1,0:T(8,128)S(1)}, u32[]{:S(2)}, u32[]{:S(2)}) %collective-permute-start.10) | collective-permute-done | bytes 4128 | tf_op jit(solution)/shard_map/ppermute | solution.py:320
  27.4 2.8 %collective-permute-start.11 = (f32[8,128]{1,0:T(8,128)S(1)}, f32[8,128]{1,0:T(8,128)S(1)}, u32[]{:S(2)}, u32[]{:S(2)}) collective-permute-start(f32[8,128]{1,0:T(8,128)S(1)} %get-tuple-element.36), channel_id=1, source_target_pairs={{1,2},{3,0},{2,1},{0,3},{5,6},{7,4},{6,5},{4,7},{9,10},{11,8},{10,... | collective-permute-start | bytes 12296 | tf_op jit(solution)/shard_map/ppermute | solution.py:320
  30.3 1.7 %collective-permute-done.11.refs_5_ = f32[8,128]{1,0:T(8,128)S(1)} collective-permute-done((f32[8,128]{1,0:T(8,128)S(1)}, f32[8,128]{1,0:T(8,128)S(1)}, u32[]{:S(2)}, u32[]{:S(2)}) %collective-permute-start.11) | collective-permute-done | bytes 4128 | tf_op jit(solution)/shard_map/ppermute | solution.py:320
  31.9 0.0 collective-permute-done.6.refs_0_
  31.9 0.0 collective-permute-done.7.refs_1_
  31.9 0.0 collective-permute-done.8.refs_2_
  32.0 0.0 collective-permute-done.9.refs_3_
  32.0 0.3 shard_map.124
  32.3 0.1 collective-permute-start.12
  32.4 2.0 %collective-permute-start.13 = (f32[3,8,128]{2,1,0:T(8,128)S(1)}, f32[3,8,128]{2,1,0:T(8,128)S(1)}, u32[]{:S(2)}, u32[]{:S(2)}) collective-permute-start(f32[3,8,128]{2,1,0:T(8,128)S(1)} %get-tuple-element.39), channel_id=1, source_target_pairs={{16,32},{48,64},{80,96},{112,128},{144,160},{176,192},{208,224},{2... | collective-permute-start | bytes 36872 | tf_op jit(solution)/shard_map/ppermute | solution.py:320
  34.4 1.1 %collective-permute-start.14 = (f32[24,128]{1,0:T(8,128)S(1)}, f32[24,128]{1,0:T(8,128)S(1)}, u32[]{:S(2)}, u32[]{:S(2)}) collective-permute-start(f32[24,128]{1,0:T(8,128)S(1)} %get-tuple-element.40), channel_id=1, source_target_pairs={{0,4},{8,12},{4,0},{12,8},{1,5},{9,13},{5,1},{13,9},{2,6},{10,14},... | collective-permute-start | bytes 36872 | tf_op jit(solution)/shard_map/ppermute | solution.py:320
  35.5 1.8 %collective-permute-start.15 = (f32[24,128]{1,0:T(8,128)S(1)}, f32[24,128]{1,0:T(8,128)S(1)}, u32[]{:S(2)}, u32[]{:S(2)}) collective-permute-start(f32[24,128]{1,0:T(8,128)S(1)} %get-tuple-element.41), channel_id=1, source_target_pairs={{4,8},{12,0},{8,4},{0,12},{5,9},{13,1},{9,5},{1,13},{6,10},{14,2},... | collective-permute-start | bytes 36872 | tf_op jit(solution)/shard_map/ppermute | solution.py:320
  37.3 1.2 %collective-permute-start.16 = (f32[8,128]{1,0:T(8,128)S(1)}, f32[8,128]{1,0:T(8,128)S(1)}, u32[]{:S(2)}, u32[]{:S(2)}) collective-permute-start(f32[8,128]{1,0:T(8,128)S(1)} %get-tuple-element.42), channel_id=1, source_target_pairs={{0,1},{2,3},{1,0},{3,2},{4,5},{6,7},{5,4},{7,6},{8,9},{10,11},{9,8... | collective-permute-start | bytes 12296 | tf_op jit(solution)/shard_map/ppermute | solution.py:320
  38.5 0.8 %collective-permute-done.16.refs_4_ = f32[8,128]{1,0:T(8,128)S(1)} collective-permute-done((f32[8,128]{1,0:T(8,128)S(1)}, f32[8,128]{1,0:T(8,128)S(1)}, u32[]{:S(2)}, u32[]{:S(2)}) %collective-permute-start.16) | collective-permute-done | bytes 4128 | tf_op jit(solution)/shard_map/ppermute | solution.py:320
  39.3 2.8 %collective-permute-start.17 = (f32[8,128]{1,0:T(8,128)S(1)}, f32[8,128]{1,0:T(8,128)S(1)}, u32[]{:S(2)}, u32[]{:S(2)}) collective-permute-start(f32[8,128]{1,0:T(8,128)S(1)} %get-tuple-element.43), channel_id=1, source_target_pairs={{1,2},{3,0},{2,1},{0,3},{5,6},{7,4},{6,5},{4,7},{9,10},{11,8},{10,... | collective-permute-start | bytes 12296 | tf_op jit(solution)/shard_map/ppermute | solution.py:320
  42.8 1.0 %collective-permute-done.17.refs_5_ = f32[8,128]{1,0:T(8,128)S(1)} collective-permute-done((f32[8,128]{1,0:T(8,128)S(1)}, f32[8,128]{1,0:T(8,128)S(1)}, u32[]{:S(2)}, u32[]{:S(2)}) %collective-permute-start.17) | collective-permute-done | bytes 4128 | tf_op jit(solution)/shard_map/ppermute | solution.py:320
  43.8 0.0 collective-permute-done.12.refs_0_
  43.8 0.0 collective-permute-done.13.refs_1_
  43.8 0.0 collective-permute-done.14.refs_2_
  43.8 0.0 collective-permute-done.15.refs_3_
  43.9 1.4 %shard_map.125 = (f32[3,8,8,128]{3,2,1,0:T(8,128)}, f32[32,16,128]{2,1,0:T(8,128)S(1)}) custom-call(s32[1]{0:T(128)} %bitcast.5.box_ref, s32[3]{0:T(128)S(1)} %bitcast.7, f32[3,8,8,128]{3,2,1,0:T(8,128)S(1)} %get-tuple-element.37.now_ref, f32[3,8,8,128]{3,2,1,0:T(8,128)S(1)} %get-tuple-element.30.start_ref, f32[7,8,8,128]{3,2,1,0:T(8,128)S(1)} %copy-done, ...), custom_call_target="tpu_custom_call" | custom-call | tf_op jit(solution)/shard_map/pallas_call | solution.py:289
  45.3 18.4 %all_to_all.10 = f32[32,16,128]{2,1,0:T(8,128)S(1)} all-to-all(f32[32,16,128]{2,1,0:T(8,128)S(1)} %get-tuple-element.45), channel_id=1, replica_groups={{0,2,16,18,32,34,48,50,64,66,80,82,96,98,112,114,128,130,144,146,160,16..., dimensions={0} | all-to-all | bytes 524288 | tf_op jit(solution)/shard_map/all_to_all | solution.py:367
  63.7 1.1 %shard_map.126 = f32[8,72,128]{2,1,0:T(8,128)S(1)} custom-call(f32[512,128]{1,0:T(8,128)S(1)} %bitcast.6), custom_call_target="tpu_custom_call" | custom-call | tf_op jit(solution)/shard_map/pallas_call | solution.py:289
  64.8 11.9 %all_to_all.11.got_ref = f32[8,72,128]{2,1,0:T(8,128)S(1)} all-to-all(f32[8,72,128]{2,1,0:T(8,128)S(1)} %shard_map.126), channel_id=1, replica_groups={{0,1,4,5,8,9,12,13},{2,3,6,7,10,11,14,15},{16,17,20,21,24,25,28,29},{18..., dimensions={0} | all-to-all | bytes 589824 | tf_op jit(solution)/shard_map/all_to_all | solution.py:369
  76.7 0.7 shard_map.127
  (6 shorter events, 0.0 us)
Async XLA Ops:
  0.6 43.2 %copy-start.2 = (f32[32,192]{1,0:T(8,128)S(1)}, f32[32,192]{1,0:T(8,128)}, u32[]{:S(2)}) copy-start(f32[32,192]{1,0:T(8,128)} %constant.8.clone.bx_ref) | copy-start | bytes 73732
  0.6 43.2 %copy-start.3 = (f32[8,128]{1,0:T(8,128)S(1)}, f32[8,128]{1,0:T(8,128)}, u32[]{:S(2)}) copy-start(f32[8,128]{1,0:T(8,128)} %constant.7.clone.by_ref) | copy-start | bytes 12292
  0.7 43.2 %copy-start.1 = (f32[128,128]{1,0:T(8,128)S(1)}, f32[128,128]{1,0:T(8,128)}, u32[]{:S(2)}) copy-start(f32[128,128]{1,0:T(8,128)} %constant.6.clone.bz_ref) | copy-start | bytes 196612
  0.7 31.3 %copy-start = (f32[7,8,8,128]{3,2,1,0:T(8,128)S(1)}, f32[7,8,8,128]{3,2,1,0:T(8,128)}, u32[]{:S(2)}) copy-start(f32[7,8,8,128]{3,2,1,0:T(8,128)} %stiff_ref.3) | copy-start | bytes 688132
  0.7 43.2 %copy-start.4 = (s32[1,1,1,3]{3,2,1,0:T(1,128)S(1)}, s32[1,1,1,3]{3,2,1,0:T(1,128)}, u32[]{:S(2)}) copy-start(s32[1,1,1,3]{3,2,1,0:T(1,128)} %param.18) | copy-start | bytes 40
  1.9 18.4 %collective-permute-start = (f32[5,8,128]{2,1,0:T(8,128)S(1)}, f32[5,8,128]{2,1,0:T(8,128)S(1)}, u32[]{:S(2)}, u32[]{:S(2)}) collective-permute-start(f32[5,8,128]{2,1,0:T(8,128)S(1)} %get-tuple-element.24), channel_id=1, source_target_pairs={{0,16},{32,48},{64,80},{96,112},{128,144},{160,176},{192,208},{224... | collective-permute-start | bytes 61448 | tf_op jit(solution)/shard_map/ppermute | solution.py:320
  4.4 15.9 %collective-permute-start.1 = (f32[5,8,128]{2,1,0:T(8,128)S(1)}, f32[5,8,128]{2,1,0:T(8,128)S(1)}, u32[]{:S(2)}, u32[]{:S(2)}) collective-permute-start(f32[5,8,128]{2,1,0:T(8,128)S(1)} %get-tuple-element.25), channel_id=1, source_target_pairs={{16,32},{48,64},{80,96},{112,128},{144,160},{176,192},{208,224},{2... | collective-permute-start | bytes 61448 | tf_op jit(solution)/shard_map/ppermute | solution.py:320
  10.1 10.2 %collective-permute-start.2 = (f32[40,128]{1,0:T(8,128)S(1)}, f32[40,128]{1,0:T(8,128)S(1)}, u32[]{:S(2)}, u32[]{:S(2)}) collective-permute-start(f32[40,128]{1,0:T(8,128)S(1)} %get-tuple-element.26), channel_id=1, source_target_pairs={{0,4},{8,12},{4,0},{12,8},{1,5},{9,13},{5,1},{13,9},{2,6},{10,14},... | collective-permute-start | bytes 61448 | tf_op jit(solution)/shard_map/ppermute | solution.py:320
  11.3 9.0 %collective-permute-start.3 = (f32[40,128]{1,0:T(8,128)S(1)}, f32[40,128]{1,0:T(8,128)S(1)}, u32[]{:S(2)}, u32[]{:S(2)}) collective-permute-start(f32[40,128]{1,0:T(8,128)S(1)} %get-tuple-element.27), channel_id=1, source_target_pairs={{4,8},{12,0},{8,4},{0,12},{5,9},{13,1},{9,5},{1,13},{6,10},{14,2},... | collective-permute-start | bytes 61448 | tf_op jit(solution)/shard_map/ppermute | solution.py:320
  13.1 2.6 %collective-permute-start.4 = (f32[8,128]{1,0:T(8,128)S(1)}, f32[8,128]{1,0:T(8,128)S(1)}, u32[]{:S(2)}, u32[]{:S(2)}) collective-permute-start(f32[8,128]{1,0:T(8,128)S(1)} %get-tuple-element.28), channel_id=1, source_target_pairs={{0,1},{2,3},{1,0},{3,2},{4,5},{6,7},{5,4},{7,6},{8,9},{10,11},{9,8... | collective-permute-start | bytes 12296 | tf_op jit(solution)/shard_map/ppermute | solution.py:320
  15.7 4.5 %collective-permute-start.5 = (f32[8,128]{1,0:T(8,128)S(1)}, f32[8,128]{1,0:T(8,128)S(1)}, u32[]{:S(2)}, u32[]{:S(2)}) collective-permute-start(f32[8,128]{1,0:T(8,128)S(1)} %get-tuple-element.29), channel_id=1, source_target_pairs={{1,2},{3,0},{2,1},{0,3},{5,6},{7,4},{6,5},{4,7},{9,10},{11,8},{10,... | collective-permute-start | bytes 12296 | tf_op jit(solution)/shard_map/ppermute | solution.py:320
  22.9 9.0 %collective-permute-start.6 = (f32[3,8,128]{2,1,0:T(8,128)S(1)}, f32[3,8,128]{2,1,0:T(8,128)S(1)}, u32[]{:S(2)}, u32[]{:S(2)}) collective-permute-start(f32[3,8,128]{2,1,0:T(8,128)S(1)} %get-tuple-element.31), channel_id=1, source_target_pairs={{0,16},{32,48},{64,80},{96,112},{128,144},{160,176},{192,208},{224... | collective-permute-start | bytes 36872 | tf_op jit(solution)/shard_map/ppermute | solution.py:320
  23.0 8.9 %collective-permute-start.7 = (f32[3,8,128]{2,1,0:T(8,128)S(1)}, f32[3,8,128]{2,1,0:T(8,128)S(1)}, u32[]{:S(2)}, u32[]{:S(2)}) collective-permute-start(f32[3,8,128]{2,1,0:T(8,128)S(1)} %get-tuple-element.32), channel_id=1, source_target_pairs={{16,32},{48,64},{80,96},{112,128},{144,160},{176,192},{208,224},{2... | collective-permute-start | bytes 36872 | tf_op jit(solution)/shard_map/ppermute | solution.py:320
  24.5 7.5 %collective-permute-start.8 = (f32[24,128]{1,0:T(8,128)S(1)}, f32[24,128]{1,0:T(8,128)S(1)}, u32[]{:S(2)}, u32[]{:S(2)}) collective-permute-start(f32[24,128]{1,0:T(8,128)S(1)} %get-tuple-element.33), channel_id=1, source_target_pairs={{0,4},{8,12},{4,0},{12,8},{1,5},{9,13},{5,1},{13,9},{2,6},{10,14},... | collective-permute-start | bytes 36872 | tf_op jit(solution)/shard_map/ppermute | solution.py:320
  24.8 7.2 %collective-permute-start.9 = (f32[24,128]{1,0:T(8,128)S(1)}, f32[24,128]{1,0:T(8,128)S(1)}, u32[]{:S(2)}, u32[]{:S(2)}) collective-permute-start(f32[24,128]{1,0:T(8,128)S(1)} %get-tuple-element.34), channel_id=1, source_target_pairs={{4,8},{12,0},{8,4},{0,12},{5,9},{13,1},{9,5},{1,13},{6,10},{14,2},... | collective-permute-start | bytes 36872 | tf_op jit(solution)/shard_map/ppermute | solution.py:320
  25.3 2.1 %collective-permute-start.10 = (f32[8,128]{1,0:T(8,128)S(1)}, f32[8,128]{1,0:T(8,128)S(1)}, u32[]{:S(2)}, u32[]{:S(2)}) collective-permute-start(f32[8,128]{1,0:T(8,128)S(1)} %get-tuple-element.35), channel_id=1, source_target_pairs={{0,1},{2,3},{1,0},{3,2},{4,5},{6,7},{5,4},{7,6},{8,9},{10,11},{9,8... | collective-permute-start | bytes 12296 | tf_op jit(solution)/shard_map/ppermute | solution.py:320
  27.4 4.5 %collective-permute-start.11 = (f32[8,128]{1,0:T(8,128)S(1)}, f32[8,128]{1,0:T(8,128)S(1)}, u32[]{:S(2)}, u32[]{:S(2)}) collective-permute-start(f32[8,128]{1,0:T(8,128)S(1)} %get-tuple-element.36), channel_id=1, source_target_pairs={{1,2},{3,0},{2,1},{0,3},{5,6},{7,4},{6,5},{4,7},{9,10},{11,8},{10,... | collective-permute-start | bytes 12296 | tf_op jit(solution)/shard_map/ppermute | solution.py:320
  32.3 11.6 %collective-permute-start.12 = (f32[3,8,128]{2,1,0:T(8,128)S(1)}, f32[3,8,128]{2,1,0:T(8,128)S(1)}, u32[]{:S(2)}, u32[]{:S(2)}) collective-permute-start(f32[3,8,128]{2,1,0:T(8,128)S(1)} %get-tuple-element.38), channel_id=1, source_target_pairs={{0,16},{32,48},{64,80},{96,112},{128,144},{160,176},{192,208},{224... | collective-permute-start | bytes 36872 | tf_op jit(solution)/shard_map/ppermute | solution.py:320
  32.4 11.5 %collective-permute-start.13 = (f32[3,8,128]{2,1,0:T(8,128)S(1)}, f32[3,8,128]{2,1,0:T(8,128)S(1)}, u32[]{:S(2)}, u32[]{:S(2)}) collective-permute-start(f32[3,8,128]{2,1,0:T(8,128)S(1)} %get-tuple-element.39), channel_id=1, source_target_pairs={{16,32},{48,64},{80,96},{112,128},{144,160},{176,192},{208,224},{2... | collective-permute-start | bytes 36872 | tf_op jit(solution)/shard_map/ppermute | solution.py:320
  34.4 9.5 %collective-permute-start.14 = (f32[24,128]{1,0:T(8,128)S(1)}, f32[24,128]{1,0:T(8,128)S(1)}, u32[]{:S(2)}, u32[]{:S(2)}) collective-permute-start(f32[24,128]{1,0:T(8,128)S(1)} %get-tuple-element.40), channel_id=1, source_target_pairs={{0,4},{8,12},{4,0},{12,8},{1,5},{9,13},{5,1},{13,9},{2,6},{10,14},... | collective-permute-start | bytes 36872 | tf_op jit(solution)/shard_map/ppermute | solution.py:320
  35.5 8.4 %collective-permute-start.15 = (f32[24,128]{1,0:T(8,128)S(1)}, f32[24,128]{1,0:T(8,128)S(1)}, u32[]{:S(2)}, u32[]{:S(2)}) collective-permute-start(f32[24,128]{1,0:T(8,128)S(1)} %get-tuple-element.41), channel_id=1, source_target_pairs={{4,8},{12,0},{8,4},{0,12},{5,9},{13,1},{9,5},{1,13},{6,10},{14,2},... | collective-permute-start | bytes 36872 | tf_op jit(solution)/shard_map/ppermute | solution.py:320
  37.3 2.0 %collective-permute-start.16 = (f32[8,128]{1,0:T(8,128)S(1)}, f32[8,128]{1,0:T(8,128)S(1)}, u32[]{:S(2)}, u32[]{:S(2)}) collective-permute-start(f32[8,128]{1,0:T(8,128)S(1)} %get-tuple-element.42), channel_id=1, source_target_pairs={{0,1},{2,3},{1,0},{3,2},{4,5},{6,7},{5,4},{7,6},{8,9},{10,11},{9,8... | collective-permute-start | bytes 12296 | tf_op jit(solution)/shard_map/ppermute | solution.py:320
  39.3 4.5 %collective-permute-start.17 = (f32[8,128]{1,0:T(8,128)S(1)}, f32[8,128]{1,0:T(8,128)S(1)}, u32[]{:S(2)}, u32[]{:S(2)}) collective-permute-start(f32[8,128]{1,0:T(8,128)S(1)} %get-tuple-element.43), channel_id=1, source_target_pairs={{1,2},{3,0},{2,1},{0,3},{5,6},{7,4},{6,5},{4,7},{9,10},{11,8},{10,... | collective-permute-start | bytes 12296 | tf_op jit(solution)/shard_map/ppermute | solution.py:320

commit v2 on v1

--- a/solution.py
+++ b/solution.py
@@ -225,7 +225,8 @@
         send_ref[2 * s + 1] = there
 
 
-def place_kernel(got_ref, send_ref, wide_ref):
+def place_kernel(got_ref, *refs):
+    keep_ref, give_ref, wide_ref, chunk_ref = refs
     half = lax.div(lax.axis_index("normal"), 2)
     where = got_ref[pl.ds(12, WINDOWS, stride=SLOT), :]
     start = got_ref[pl.ds(13, WINDOWS, stride=SLOT), :]
@@ -256,15 +257,27 @@
         for i in range(8):
             for block in range(4):
                 base = (r * 4 + block) * ROWS
-                send_ref[i, base : base + ROWS, :] = placed[
+                chunk_ref[i, base : base + ROWS, :] = placed[
                     i * 8 : i * 8 + ROWS, block * 128 : block * 128 + 128
                 ]
-
-
-def sum_kernel(got_ref, out_ref, total_ref):
-    total = got_ref[0]
-    for j in range(1, 8):
-        total = total + got_ref[j]
+    near = lax.rem(lax.axis_index("normal"), 2)
+    for c in range(4):
+        keep_ref[c] = chunk_ref[c * 2 + near]
+        give_ref[c] = chunk_ref[c * 2 + 1 - near]
+
+
+def join_kernel(keep_ref, got_ref, *sends):
+    mine = lax.axis_index("chord")
+    for d in range(4):
+        at = lax.bitwise_xor(mine, d)
+        sends[d][...] = keep_ref[at] + got_ref[at]
+
+
+def sum_kernel(*refs):
+    got, (out_ref, total_ref) = refs[:4], refs[4:]
+    total = got[0][...]
+    for one in got[1:]:
+        total = total + one[...]
     total_ref[...] = total
     for r in range(3):
         for block in range(4):
@@ -321,11 +334,9 @@
     return got
 
 
-def ffd_groups():
+def owners():
     index = np.arange(256).reshape(16, 4, 2, 2)
-    owners = index.transpose(1, 3, 0, 2).reshape(8, 32).tolist()
-    sharers = index.transpose(0, 2, 1, 3).reshape(32, 8).tolist()
-    return owners, sharers
+    return index.transpose(1, 3, 0, 2).reshape(8, 32).tolist()
 
 
 def ends(v):
@@ -363,11 +374,17 @@
         scratch=(*kept, (192, 128)),
         scalars=2,
     )
-    owners, sharers = ffd_groups()
-    got = lax.all_to_all(windows, ALL, 0, 0, axis_index_groups=owners, tiled=True)
-    chunks = call(place_kernel, shape(8, 72, 128), (got.reshape(WINDOWS * SLOT, 128),), scratch=((3, 256, 512),))
-    got = lax.all_to_all(chunks, ALL, 0, 0, axis_index_groups=sharers, tiled=True)
-    grad = call(sum_kernel, shape(3, 1, 3072), (got,), scratch=((72, 128),))
+    got = lax.all_to_all(windows, ALL, 0, 0, axis_index_groups=owners(), tiled=True)
+    keep, give = call(
+        place_kernel,
+        (shape(4, 72, 128),) * 2,
+        (got.reshape(WINDOWS * SLOT, 128),),
+        scratch=((3, 256, 512), (8, 72, 128)),
+    )
+    got = lax.ppermute(give, "normal", pairing("normal", 0))
+    mine, *chunks = call(join_kernel, (shape(72, 128),) * 4, (keep, got))
+    got = [lax.ppermute(one, "chord", [(i, i ^ d) for i in range(4)]) for d, one in enumerate(chunks, 1)]
+    grad = call(sum_kernel, shape(3, 1, 3072), (mine, *got), scratch=((72, 128),))
     return final, grad.reshape(1, 3, 3072)
 
 

time: 77.6 us -> 75.3 us (0.970)
  blocking collectives: 30.3 us -> 18.4 us
  starting transfers between devices: 31.4 us -> 37.7 us
  waiting for transfers between devices: 6.91 us -> 10.2 us
    all_to_all x2 -> x1, blocking collectives: 30.3 us -> 18.4 us  [local(): lax.all_to_all(windows, ALL, 0, 0, axis_index_groups=owners(), tiled=True)]
    ppermute x0 -> x4, starting transfers between devices: none -> 6.32 us  [the longest x3 3.95 us: local(): lax.ppermute(one, 'chord', [(i, i ^ d) for i in range(4)])]
    ppermute x0 -> x4, waiting for transfers between devices: none -> 3.28 us  [the longest x3 2.27 us: local(): lax.ppermute(one, 'chord', [(i, i ^ d) for i in range(4)])]
    pallas_call x6 -> x7, Pallas kernels: 7.25 us -> 7.29 us  [call(): pl.pallas_call(body, out_shape=outs, in_specs=specs, out_specs=jax.tree.m...]
  transfers between devices with their start and end apart: 18 -> 22, of which waited for: 6 -> 9; matrix products, arithmetic and copies ran while one was open for 0% -> 0% of each run, Pallas kernels for 0% -> 0%
where the time goes in v2:
time: 75.3 us; the launch traced here: 75.1 us
  starting transfers between devices  37.7 us (50%)
  blocking collectives  18.4 us (24%)
  waiting for transfers between devices  10.2 us (14%)
  Pallas kernels  7.29 us (10%)
  between operations  1.46 us (2%)
    ppermute x18, starting transfers between devices, swap(): got.append(lax.ppermute(one, AXES[name], pairing(AXES[name], at % 2)))  31.4 us
    all_to_all x1, blocking collectives, local(): lax.all_to_all(windows, ALL, 0, 0, axis_index_groups=owners(), tiled=True)  18.4 us
    pallas_call x7, Pallas kernels, call(): pl.pallas_call(body, out_shape=outs, in_specs=specs, out_specs=jax.tree.m...  7.29 us
    ppermute x18, waiting for transfers between devices, swap(): got.append(lax.ppermute(one, AXES[name], pairing(AXES[name], at % 2)))  6.91 us
    ppermute x3, starting transfers between devices, local(): lax.ppermute(one, 'chord', [(i, i ^ d) for i in range(4)])  3.95 us
    ppermute x1, starting transfers between devices, local(): got = lax.ppermute(give, 'normal', pairing('normal', 0))  2.37 us
    ppermute x3, waiting for transfers between devices, local(): lax.ppermute(one, 'chord', [(i, i ^ d) for i in range(4)])  2.27 us
  transfers between devices with their start and end apart: 22, of which 9 were waited for; matrix products, arithmetic and copies ran while one was open for 0% of the time, Pallas kernels for 0%

profile of v2, /device:TPU:1, one launch (start us, length us, event | category | flops | bytes accessed | tf_op | source)
XLA Modules:
  0.0 75.1 jit_solution(4756976010347252880)
XLA Ops:
  0.6 0.0 copy-start.2
  0.6 0.0 copy-start.3
  0.7 0.0 copy-start.1
  0.7 0.0 copy-start
  0.7 1.2 %shard_map.122 = (f32[5,8,128]{2,1,0:T(8,128)S(1)}, f32[5,8,128]{2,1,0:T(8,128)S(1)}, f32[40,128]{1,0:T(8,128)S(1)}, f32[40,128]{1,0:T(8,128)S(1)}, f32[8,128]{1,0:T(8,128)S(1)}, /*index=5*/f32[8,128]{1,0:T(8,128)S(1)}) custom-call(f32[5,8,8,128]{3,2,1,0:T(8,128)} %adjoint_any.3), custom_call_target="tpu_custom_call" | custom-call | tf_op jit(solution)/shard_map/pallas_call | solution.py:302
  1.9 2.5 %collective-permute-start = (f32[5,8,128]{2,1,0:T(8,128)S(1)}, f32[5,8,128]{2,1,0:T(8,128)S(1)}, u32[]{:S(2)}, u32[]{:S(2)}) collective-permute-start(f32[5,8,128]{2,1,0:T(8,128)S(1)} %get-tuple-element.30), channel_id=1, source_target_pairs={{0,16},{32,48},{64,80},{96,112},{128,144},{160,176},{192,208},{224... | collective-permute-start | bytes 61448 | tf_op jit(solution)/shard_map/ppermute | solution.py:333
  4.4 5.7 %collective-permute-start.1 = (f32[5,8,128]{2,1,0:T(8,128)S(1)}, f32[5,8,128]{2,1,0:T(8,128)S(1)}, u32[]{:S(2)}, u32[]{:S(2)}) collective-permute-start(f32[5,8,128]{2,1,0:T(8,128)S(1)} %get-tuple-element.31), channel_id=1, source_target_pairs={{16,32},{48,64},{80,96},{112,128},{144,160},{176,192},{208,224},{2... | collective-permute-start | bytes 61448 | tf_op jit(solution)/shard_map/ppermute | solution.py:333
  10.1 1.2 %collective-permute-start.2 = (f32[40,128]{1,0:T(8,128)S(1)}, f32[40,128]{1,0:T(8,128)S(1)}, u32[]{:S(2)}, u32[]{:S(2)}) collective-permute-start(f32[40,128]{1,0:T(8,128)S(1)} %get-tuple-element.32), channel_id=1, source_target_pairs={{0,4},{8,12},{4,0},{12,8},{1,5},{9,13},{5,1},{13,9},{2,6},{10,14},... | collective-permute-start | bytes 61448 | tf_op jit(solution)/shard_map/ppermute | solution.py:333
  11.3 1.8 %collective-permute-start.3 = (f32[40,128]{1,0:T(8,128)S(1)}, f32[40,128]{1,0:T(8,128)S(1)}, u32[]{:S(2)}, u32[]{:S(2)}) collective-permute-start(f32[40,128]{1,0:T(8,128)S(1)} %get-tuple-element.33), channel_id=1, source_target_pairs={{4,8},{12,0},{8,4},{0,12},{5,9},{13,1},{9,5},{1,13},{6,10},{14,2},... | collective-permute-start | bytes 61448 | tf_op jit(solution)/shard_map/ppermute | solution.py:333
  13.1 1.8 %collective-permute-start.4 = (f32[8,128]{1,0:T(8,128)S(1)}, f32[8,128]{1,0:T(8,128)S(1)}, u32[]{:S(2)}, u32[]{:S(2)}) collective-permute-start(f32[8,128]{1,0:T(8,128)S(1)} %get-tuple-element.34), channel_id=1, source_target_pairs={{0,1},{2,3},{1,0},{3,2},{4,5},{6,7},{5,4},{7,6},{8,9},{10,11},{9,8... | collective-permute-start | bytes 12296 | tf_op jit(solution)/shard_map/ppermute | solution.py:333
  14.9 0.8 %collective-permute-done.4.refs_4_ = f32[8,128]{1,0:T(8,128)S(1)} collective-permute-done((f32[8,128]{1,0:T(8,128)S(1)}, f32[8,128]{1,0:T(8,128)S(1)}, u32[]{:S(2)}, u32[]{:S(2)}) %collective-permute-start.4) | collective-permute-done | bytes 4128 | tf_op jit(solution)/shard_map/ppermute | solution.py:333
  15.7 2.8 %collective-permute-start.5 = (f32[8,128]{1,0:T(8,128)S(1)}, f32[8,128]{1,0:T(8,128)S(1)}, u32[]{:S(2)}, u32[]{:S(2)}) collective-permute-start(f32[8,128]{1,0:T(8,128)S(1)} %get-tuple-element.35), channel_id=1, source_target_pairs={{1,2},{3,0},{2,1},{0,3},{5,6},{7,4},{6,5},{4,7},{9,10},{11,8},{10,... | collective-permute-start | bytes 12296 | tf_op jit(solution)/shard_map/ppermute | solution.py:333
  18.6 1.7 %collective-permute-done.5.refs_5_ = f32[8,128]{1,0:T(8,128)S(1)} collective-permute-done((f32[8,128]{1,0:T(8,128)S(1)}, f32[8,128]{1,0:T(8,128)S(1)}, u32[]{:S(2)}, u32[]{:S(2)}) %collective-permute-start.5) | collective-permute-done | bytes 4128 | tf_op jit(solution)/shard_map/ppermute | solution.py:333
  20.3 0.0 collective-permute-done.refs_0_
  20.3 0.0 collective-permute-done.1.refs_1_
  20.3 0.0 collective-permute-done.3.refs_3_
  20.3 2.6 %shard_map.123 = (f32[3,8,8,128]{3,2,1,0:T(8,128)S(1)}, f32[3,8,128]{2,1,0:T(8,128)S(1)}, f32[3,8,128]{2,1,0:T(8,128)S(1)}, f32[24,128]{1,0:T(8,128)S(1)}, f32[2...) custom-call(f32[5,3,5]{2,1,0:T(4,128)} %bitcast.9, f32[3,5]{1,0:T(4,128)} %map_any.1, ...), custom_call_target="tpu_custom_call" | custom-call | tf_op jit(solution)/shard_map/pallas_call | solution.py:302
  22.9 0.1 collective-permute-start.6
  23.0 1.4 %collective-permute-start.7 = (f32[3,8,128]{2,1,0:T(8,128)S(1)}, f32[3,8,128]{2,1,0:T(8,128)S(1)}, u32[]{:S(2)}, u32[]{:S(2)}) collective-permute-start(f32[3,8,128]{2,1,0:T(8,128)S(1)} %get-tuple-element.38), channel_id=1, source_target_pairs={{16,32},{48,64},{80,96},{112,128},{144,160},{176,192},{208,224},{2... | collective-permute-start | bytes 36872 | tf_op jit(solution)/shard_map/ppermute | solution.py:333
  24.5 0.3 collective-permute-start.8
  24.8 0.6 collective-permute-start.9
  25.3 1.2 %collective-permute-start.10 = (f32[8,128]{1,0:T(8,128)S(1)}, f32[8,128]{1,0:T(8,128)S(1)}, u32[]{:S(2)}, u32[]{:S(2)}) collective-permute-start(f32[8,128]{1,0:T(8,128)S(1)} %get-tuple-element.41), channel_id=1, source_target_pairs={{0,1},{2,3},{1,0},{3,2},{4,5},{6,7},{5,4},{7,6},{8,9},{10,11},{9,8... | collective-permute-start | bytes 12296 | tf_op jit(solution)/shard_map/ppermute | solution.py:333
  26.6 0.8 %collective-permute-done.10.refs_4_ = f32[8,128]{1,0:T(8,128)S(1)} collective-permute-done((f32[8,128]{1,0:T(8,128)S(1)}, f32[8,128]{1,0:T(8,128)S(1)}, u32[]{:S(2)}, u32[]{:S(2)}) %collective-permute-start.10) | collective-permute-done | bytes 4128 | tf_op jit(solution)/shard_map/ppermute | solution.py:333
  27.4 2.8 %collective-permute-start.11 = (f32[8,128]{1,0:T(8,128)S(1)}, f32[8,128]{1,0:T(8,128)S(1)}, u32[]{:S(2)}, u32[]{:S(2)}) collective-permute-start(f32[8,128]{1,0:T(8,128)S(1)} %get-tuple-element.42), channel_id=1, source_target_pairs={{1,2},{3,0},{2,1},{0,3},{5,6},{7,4},{6,5},{4,7},{9,10},{11,8},{10,... | collective-permute-start | bytes 12296 | tf_op jit(solution)/shard_map/ppermute | solution.py:333
  30.3 1.7 %collective-permute-done.11.refs_5_ = f32[8,128]{1,0:T(8,128)S(1)} collective-permute-done((f32[8,128]{1,0:T(8,128)S(1)}, f32[8,128]{1,0:T(8,128)S(1)}, u32[]{:S(2)}, u32[]{:S(2)}) %collective-permute-start.11) | collective-permute-done | bytes 4128 | tf_op jit(solution)/shard_map/ppermute | solution.py:333
  31.9 0.0 collective-permute-done.6.refs_0_
  32.0 0.3 shard_map.124
  32.3 0.1 collective-permute-start.12
  32.4 2.0 %collective-permute-start.13 = (f32[3,8,128]{2,1,0:T(8,128)S(1)}, f32[3,8,128]{2,1,0:T(8,128)S(1)}, u32[]{:S(2)}, u32[]{:S(2)}) collective-permute-start(f32[3,8,128]{2,1,0:T(8,128)S(1)} %get-tuple-element.45), channel_id=1, source_target_pairs={{16,32},{48,64},{80,96},{112,128},{144,160},{176,192},{208,224},{2... | collective-permute-start | bytes 36872 | tf_op jit(solution)/shard_map/ppermute | solution.py:333
  34.4 1.1 %collective-permute-start.14 = (f32[24,128]{1,0:T(8,128)S(1)}, f32[24,128]{1,0:T(8,128)S(1)}, u32[]{:S(2)}, u32[]{:S(2)}) collective-permute-start(f32[24,128]{1,0:T(8,128)S(1)} %get-tuple-element.46), channel_id=1, source_target_pairs={{0,4},{8,12},{4,0},{12,8},{1,5},{9,13},{5,1},{13,9},{2,6},{10,14},... | collective-permute-start | bytes 36872 | tf_op jit(solution)/shard_map/ppermute | solution.py:333
  35.5 1.8 %collective-permute-start.15 = (f32[24,128]{1,0:T(8,128)S(1)}, f32[24,128]{1,0:T(8,128)S(1)}, u32[]{:S(2)}, u32[]{:S(2)}) collective-permute-start(f32[24,128]{1,0:T(8,128)S(1)} %get-tuple-element.47), channel_id=1, source_target_pairs={{4,8},{12,0},{8,4},{0,12},{5,9},{13,1},{9,5},{1,13},{6,10},{14,2},... | collective-permute-start | bytes 36872 | tf_op jit(solution)/shard_map/ppermute | solution.py:333
  37.3 1.2 %collective-permute-start.16 = (f32[8,128]{1,0:T(8,128)S(1)}, f32[8,128]{1,0:T(8,128)S(1)}, u32[]{:S(2)}, u32[]{:S(2)}) collective-permute-start(f32[8,128]{1,0:T(8,128)S(1)} %get-tuple-element.48), channel_id=1, source_target_pairs={{0,1},{2,3},{1,0},{3,2},{4,5},{6,7},{5,4},{7,6},{8,9},{10,11},{9,8... | collective-permute-start | bytes 12296 | tf_op jit(solution)/shard_map/ppermute | solution.py:333
  38.5 0.8 %collective-permute-done.16.refs_4_ = f32[8,128]{1,0:T(8,128)S(1)} collective-permute-done((f32[8,128]{1,0:T(8,128)S(1)}, f32[8,128]{1,0:T(8,128)S(1)}, u32[]{:S(2)}, u32[]{:S(2)}) %collective-permute-start.16) | collective-permute-done | bytes 4128 | tf_op jit(solution)/shard_map/ppermute | solution.py:333
  39.3 2.8 %collective-permute-start.17 = (f32[8,128]{1,0:T(8,128)S(1)}, f32[8,128]{1,0:T(8,128)S(1)}, u32[]{:S(2)}, u32[]{:S(2)}) collective-permute-start(f32[8,128]{1,0:T(8,128)S(1)} %get-tuple-element.49), channel_id=1, source_target_pairs={{1,2},{3,0},{2,1},{0,3},{5,6},{7,4},{6,5},{4,7},{9,10},{11,8},{10,... | collective-permute-start | bytes 12296 | tf_op jit(solution)/shard_map/ppermute | solution.py:333
  42.8 1.0 %collective-permute-done.17.refs_5_ = f32[8,128]{1,0:T(8,128)S(1)} collective-permute-done((f32[8,128]{1,0:T(8,128)S(1)}, f32[8,128]{1,0:T(8,128)S(1)}, u32[]{:S(2)}, u32[]{:S(2)}) %collective-permute-start.17) | collective-permute-done | bytes 4128 | tf_op jit(solution)/shard_map/ppermute | solution.py:333
  43.8 0.0 collective-permute-done.14.refs_2_
  43.8 0.0 collective-permute-done.15.refs_3_
  43.9 1.4 %shard_map.125 = (f32[3,8,8,128]{3,2,1,0:T(8,128)}, f32[32,16,128]{2,1,0:T(8,128)S(1)}) custom-call(s32[1]{0:T(128)} %bitcast.5.box_ref, s32[3]{0:T(128)S(1)} %bitcast.7, f32[3,8,8,128]{3,2,1,0:T(8,128)S(1)} %get-tuple-element.43.now_ref, f32[3,8,8,128]{3,2,1,0:T(8,128)S(1)} %get-tuple-element.36.start_ref, f32[7,8,8,128]{3,2,1,0:T(8,128)S(1)} %copy-done, ...), custom_call_target="tpu_custom_call" | custom-call | tf_op jit(solution)/shard_map/pallas_call | solution.py:302
  45.3 18.4 %all_to_all.5 = f32[32,16,128]{2,1,0:T(8,128)S(1)} all-to-all(f32[32,16,128]{2,1,0:T(8,128)S(1)} %get-tuple-element.51), channel_id=1, replica_groups={{0,2,16,18,32,34,48,50,64,66,80,82,96,98,112,114,128,130,144,146,160,16..., dimensions={0} | all-to-all | bytes 524288 | tf_op jit(solution)/shard_map/all_to_all | solution.py:377
  63.7 1.2 %shard_map.126 = (f32[4,72,128]{2,1,0:T(8,128)S(1)}, f32[4,72,128]{2,1,0:T(8,128)S(1)}) custom-call(f32[512,128]{1,0:T(8,128)S(1)} %bitcast.6), custom_call_target="tpu_custom_call" | custom-call | tf_op jit(solution)/shard_map/pallas_call | solution.py:302
  64.8 2.4 %collective-permute-start.18 = (f32[4,72,128]{2,1,0:T(8,128)S(1)}, f32[4,72,128]{2,1,0:T(8,128)S(1)}, u32[]{:S(2)}, u32[]{:S(2)}) collective-permute-start(f32[4,72,128]{2,1,0:T(8,128)S(1)} %get-tuple-element.53), channel_id=1, source_target_pairs={{0,1},{2,3},{1,0},{3,2},{4,5},{6,7},{5,4},{7,6},{8,9},{10,11},{9,8... | collective-permute-start | bytes 442376 | tf_op jit(solution)/shard_map/ppermute | solution.py:384
  67.2 1.0 %collective-permute-done.18.got_ref = f32[4,72,128]{2,1,0:T(8,128)S(1)} collective-permute-done((f32[4,72,128]{2,1,0:T(8,128)S(1)}, f32[4,72,128]{2,1,0:T(8,128)S(1)}, u32[]{:S(2)}, u32[]{:S(2)}) %collective-permute-start.18) | collective-permute-done | bytes 147488 | tf_op jit(solution)/shard_map/ppermute | solution.py:384
  68.2 0.4 collective-permute-start.19
  68.6 1.7 %collective-permute-start.20 = (f32[72,128]{1,0:T(8,128)S(1)}, f32[72,128]{1,0:T(8,128)S(1)}, u32[]{:S(2)}, u32[]{:S(2)}) collective-permute-start(f32[72,128]{1,0:T(8,128)S(1)} %get-tuple-element.56), channel_id=1, source_target_pairs={{0,8},{4,12},{8,0},{12,4},{1,9},{5,13},{9,1},{13,5},{2,10},{6,14},... | collective-permute-start | bytes 110600 | tf_op jit(solution)/shard_map/ppermute | solution.py:386
  70.4 1.8 %collective-permute-start.21 = (f32[72,128]{1,0:T(8,128)S(1)}, f32[72,128]{1,0:T(8,128)S(1)}, u32[]{:S(2)}, u32[]{:S(2)}) collective-permute-start(f32[72,128]{1,0:T(8,128)S(1)} %get-tuple-element.57), channel_id=1, source_target_pairs={{0,12},{4,8},{8,4},{12,0},{1,13},{5,9},{9,5},{13,1},{2,14},{6,10},... | collective-permute-start | bytes 110600 | tf_op jit(solution)/shard_map/ppermute | solution.py:386
  72.2 0.8 %collective-permute-done.20.refs_2_ = f32[72,128]{1,0:T(8,128)S(1)} collective-permute-done((f32[72,128]{1,0:T(8,128)S(1)}, f32[72,128]{1,0:T(8,128)S(1)}, u32[]{:S(2)}, u32[]{:S(2)}) %collective-permute-start.20) | collective-permute-done | bytes 36896 | tf_op jit(solution)/shard_map/ppermute | solution.py:386
  73.0 1.5 %collective-permute-done.21.refs_3_ = f32[72,128]{1,0:T(8,128)S(1)} collective-permute-done((f32[72,128]{1,0:T(8,128)S(1)}, f32[72,128]{1,0:T(8,128)S(1)}, u32[]{:S(2)}, u32[]{:S(2)}) %collective-permute-start.21) | collective-permute-done | bytes 36896 | tf_op jit(solution)/shard_map/ppermute | solution.py:386
  74.5 0.7 shard_map.128
  (14 shorter events, 0.0 us)
Async XLA Ops:
  0.6 43.2 %copy-start.2 = (f32[32,192]{1,0:T(8,128)S(1)}, f32[32,192]{1,0:T(8,128)}, u32[]{:S(2)}) copy-start(f32[32,192]{1,0:T(8,128)} %constant.8.clone.bx_ref) | copy-start | bytes 73732
  0.6 43.2 %copy-start.3 = (f32[8,128]{1,0:T(8,128)S(1)}, f32[8,128]{1,0:T(8,128)}, u32[]{:S(2)}) copy-start(f32[8,128]{1,0:T(8,128)} %constant.7.clone.by_ref) | copy-start | bytes 12292
  0.7 43.2 %copy-start.1 = (f32[128,128]{1,0:T(8,128)S(1)}, f32[128,128]{1,0:T(8,128)}, u32[]{:S(2)}) copy-start(f32[128,128]{1,0:T(8,128)} %constant.6.clone.bz_ref) | copy-start | bytes 196612
  0.7 31.3 %copy-start = (f32[7,8,8,128]{3,2,1,0:T(8,128)S(1)}, f32[7,8,8,128]{3,2,1,0:T(8,128)}, u32[]{:S(2)}) copy-start(f32[7,8,8,128]{3,2,1,0:T(8,128)} %stiff_ref.3) | copy-start | bytes 688132
  0.7 43.2 %copy-start.4 = (s32[1,1,1,3]{3,2,1,0:T(1,128)S(1)}, s32[1,1,1,3]{3,2,1,0:T(1,128)}, u32[]{:S(2)}) copy-start(s32[1,1,1,3]{3,2,1,0:T(1,128)} %param.18) | copy-start | bytes 40
  1.9 18.4 %collective-permute-start = (f32[5,8,128]{2,1,0:T(8,128)S(1)}, f32[5,8,128]{2,1,0:T(8,128)S(1)}, u32[]{:S(2)}, u32[]{:S(2)}) collective-permute-start(f32[5,8,128]{2,1,0:T(8,128)S(1)} %get-tuple-element.30), channel_id=1, source_target_pairs={{0,16},{32,48},{64,80},{96,112},{128,144},{160,176},{192,208},{224... | collective-permute-start | bytes 61448 | tf_op jit(solution)/shard_map/ppermute | solution.py:333
  4.4 15.9 %collective-permute-start.1 = (f32[5,8,128]{2,1,0:T(8,128)S(1)}, f32[5,8,128]{2,1,0:T(8,128)S(1)}, u32[]{:S(2)}, u32[]{:S(2)}) collective-permute-start(f32[5,8,128]{2,1,0:T(8,128)S(1)} %get-tuple-element.31), channel_id=1, source_target_pairs={{16,32},{48,64},{80,96},{112,128},{144,160},{176,192},{208,224},{2... | collective-permute-start | bytes 61448 | tf_op jit(solution)/shard_map/ppermute | solution.py:333
  10.1 10.2 %collective-permute-start.2 = (f32[40,128]{1,0:T(8,128)S(1)}, f32[40,128]{1,0:T(8,128)S(1)}, u32[]{:S(2)}, u32[]{:S(2)}) collective-permute-start(f32[40,128]{1,0:T(8,128)S(1)} %get-tuple-element.32), channel_id=1, source_target_pairs={{0,4},{8,12},{4,0},{12,8},{1,5},{9,13},{5,1},{13,9},{2,6},{10,14},... | collective-permute-start | bytes 61448 | tf_op jit(solution)/shard_map/ppermute | solution.py:333
  11.3 9.0 %collective-permute-start.3 = (f32[40,128]{1,0:T(8,128)S(1)}, f32[40,128]{1,0:T(8,128)S(1)}, u32[]{:S(2)}, u32[]{:S(2)}) collective-permute-start(f32[40,128]{1,0:T(8,128)S(1)} %get-tuple-element.33), channel_id=1, source_target_pairs={{4,8},{12,0},{8,4},{0,12},{5,9},{13,1},{9,5},{1,13},{6,10},{14,2},... | collective-permute-start | bytes 61448 | tf_op jit(solution)/shard_map/ppermute | solution.py:333
  13.1 2.6 %collective-permute-start.4 = (f32[8,128]{1,0:T(8,128)S(1)}, f32[8,128]{1,0:T(8,128)S(1)}, u32[]{:S(2)}, u32[]{:S(2)}) collective-permute-start(f32[8,128]{1,0:T(8,128)S(1)} %get-tuple-element.34), channel_id=1, source_target_pairs={{0,1},{2,3},{1,0},{3,2},{4,5},{6,7},{5,4},{7,6},{8,9},{10,11},{9,8... | collective-permute-start | bytes 12296 | tf_op jit(solution)/shard_map/ppermute | solution.py:333
  15.7 4.5 %collective-permute-start.5 = (f32[8,128]{1,0:T(8,128)S(1)}, f32[8,128]{1,0:T(8,128)S(1)}, u32[]{:S(2)}, u32[]{:S(2)}) collective-permute-start(f32[8,128]{1,0:T(8,128)S(1)} %get-tuple-element.35), channel_id=1, source_target_pairs={{1,2},{3,0},{2,1},{0,3},{5,6},{7,4},{6,5},{4,7},{9,10},{11,8},{10,... | collective-permute-start | bytes 12296 | tf_op jit(solution)/shard_map/ppermute | solution.py:333
  22.9 9.0 %collective-permute-start.6 = (f32[3,8,128]{2,1,0:T(8,128)S(1)}, f32[3,8,128]{2,1,0:T(8,128)S(1)}, u32[]{:S(2)}, u32[]{:S(2)}) collective-permute-start(f32[3,8,128]{2,1,0:T(8,128)S(1)} %get-tuple-element.37), channel_id=1, source_target_pairs={{0,16},{32,48},{64,80},{96,112},{128,144},{160,176},{192,208},{224... | collective-permute-start | bytes 36872 | tf_op jit(solution)/shard_map/ppermute | solution.py:333
  23.0 8.9 %collective-permute-start.7 = (f32[3,8,128]{2,1,0:T(8,128)S(1)}, f32[3,8,128]{2,1,0:T(8,128)S(1)}, u32[]{:S(2)}, u32[]{:S(2)}) collective-permute-start(f32[3,8,128]{2,1,0:T(8,128)S(1)} %get-tuple-element.38), channel_id=1, source_target_pairs={{16,32},{48,64},{80,96},{112,128},{144,160},{176,192},{208,224},{2... | collective-permute-start | bytes 36872 | tf_op jit(solution)/shard_map/ppermute | solution.py:333
  24.5 7.5 %collective-permute-start.8 = (f32[24,128]{1,0:T(8,128)S(1)}, f32[24,128]{1,0:T(8,128)S(1)}, u32[]{:S(2)}, u32[]{:S(2)}) collective-permute-start(f32[24,128]{1,0:T(8,128)S(1)} %get-tuple-element.39), channel_id=1, source_target_pairs={{0,4},{8,12},{4,0},{12,8},{1,5},{9,13},{5,1},{13,9},{2,6},{10,14},... | collective-permute-start | bytes 36872 | tf_op jit(solution)/shard_map/ppermute | solution.py:333
  24.8 7.2 %collective-permute-start.9 = (f32[24,128]{1,0:T(8,128)S(1)}, f32[24,128]{1,0:T(8,128)S(1)}, u32[]{:S(2)}, u32[]{:S(2)}) collective-permute-start(f32[24,128]{1,0:T(8,128)S(1)} %get-tuple-element.40), channel_id=1, source_target_pairs={{4,8},{12,0},{8,4},{0,12},{5,9},{13,1},{9,5},{1,13},{6,10},{14,2},... | collective-permute-start | bytes 36872 | tf_op jit(solution)/shard_map/ppermute | solution.py:333
  25.3 2.1 %collective-permute-start.10 = (f32[8,128]{1,0:T(8,128)S(1)}, f32[8,128]{1,0:T(8,128)S(1)}, u32[]{:S(2)}, u32[]{:S(2)}) collective-permute-start(f32[8,128]{1,0:T(8,128)S(1)} %get-tuple-element.41), channel_id=1, source_target_pairs={{0,1},{2,3},{1,0},{3,2},{4,5},{6,7},{5,4},{7,6},{8,9},{10,11},{9,8... | collective-permute-start | bytes 12296 | tf_op jit(solution)/shard_map/ppermute | solution.py:333
  27.4 4.5 %collective-permute-start.11 = (f32[8,128]{1,0:T(8,128)S(1)}, f32[8,128]{1,0:T(8,128)S(1)}, u32[]{:S(2)}, u32[]{:S(2)}) collective-permute-start(f32[8,128]{1,0:T(8,128)S(1)} %get-tuple-element.42), channel_id=1, source_target_pairs={{1,2},{3,0},{2,1},{0,3},{5,6},{7,4},{6,5},{4,7},{9,10},{11,8},{10,... | collective-permute-start | bytes 12296 | tf_op jit(solution)/shard_map/ppermute | solution.py:333
  32.3 11.6 %collective-permute-start.12 = (f32[3,8,128]{2,1,0:T(8,128)S(1)}, f32[3,8,128]{2,1,0:T(8,128)S(1)}, u32[]{:S(2)}, u32[]{:S(2)}) collective-permute-start(f32[3,8,128]{2,1,0:T(8,128)S(1)} %get-tuple-element.44), channel_id=1, source_target_pairs={{0,16},{32,48},{64,80},{96,112},{128,144},{160,176},{192,208},{224... | collective-permute-start | bytes 36872 | tf_op jit(solution)/shard_map/ppermute | solution.py:333
  32.4 11.5 %collective-permute-start.13 = (f32[3,8,128]{2,1,0:T(8,128)S(1)}, f32[3,8,128]{2,1,0:T(8,128)S(1)}, u32[]{:S(2)}, u32[]{:S(2)}) collective-permute-start(f32[3,8,128]{2,1,0:T(8,128)S(1)} %get-tuple-element.45), channel_id=1, source_target_pairs={{16,32},{48,64},{80,96},{112,128},{144,160},{176,192},{208,224},{2... | collective-permute-start | bytes 36872 | tf_op jit(solution)/shard_map/ppermute | solution.py:333
  34.4 9.5 %collective-permute-start.14 = (f32[24,128]{1,0:T(8,128)S(1)}, f32[24,128]{1,0:T(8,128)S(1)}, u32[]{:S(2)}, u32[]{:S(2)}) collective-permute-start(f32[24,128]{1,0:T(8,128)S(1)} %get-tuple-element.46), channel_id=1, source_target_pairs={{0,4},{8,12},{4,0},{12,8},{1,5},{9,13},{5,1},{13,9},{2,6},{10,14},... | collective-permute-start | bytes 36872 | tf_op jit(solution)/shard_map/ppermute | solution.py:333
  35.5 8.4 %collective-permute-start.15 = (f32[24,128]{1,0:T(8,128)S(1)}, f32[24,128]{1,0:T(8,128)S(1)}, u32[]{:S(2)}, u32[]{:S(2)}) collective-permute-start(f32[24,128]{1,0:T(8,128)S(1)} %get-tuple-element.47), channel_id=1, source_target_pairs={{4,8},{12,0},{8,4},{0,12},{5,9},{13,1},{9,5},{1,13},{6,10},{14,2},... | collective-permute-start | bytes 36872 | tf_op jit(solution)/shard_map/ppermute | solution.py:333
  37.3 2.0 %collective-permute-start.16 = (f32[8,128]{1,0:T(8,128)S(1)}, f32[8,128]{1,0:T(8,128)S(1)}, u32[]{:S(2)}, u32[]{:S(2)}) collective-permute-start(f32[8,128]{1,0:T(8,128)S(1)} %get-tuple-element.48), channel_id=1, source_target_pairs={{0,1},{2,3},{1,0},{3,2},{4,5},{6,7},{5,4},{7,6},{8,9},{10,11},{9,8... | collective-permute-start | bytes 12296 | tf_op jit(solution)/shard_map/ppermute | solution.py:333
  39.3 4.5 %collective-permute-start.17 = (f32[8,128]{1,0:T(8,128)S(1)}, f32[8,128]{1,0:T(8,128)S(1)}, u32[]{:S(2)}, u32[]{:S(2)}) collective-permute-start(f32[8,128]{1,0:T(8,128)S(1)} %get-tuple-element.49), channel_id=1, source_target_pairs={{1,2},{3,0},{2,1},{0,3},{5,6},{7,4},{6,5},{4,7},{9,10},{11,8},{10,... | collective-permute-start | bytes 12296 | tf_op jit(solution)/shard_map/ppermute | solution.py:333
  64.8 3.4 %collective-permute-start.18 = (f32[4,72,128]{2,1,0:T(8,128)S(1)}, f32[4,72,128]{2,1,0:T(8,128)S(1)}, u32[]{:S(2)}, u32[]{:S(2)}) collective-permute-start(f32[4,72,128]{2,1,0:T(8,128)S(1)} %get-tuple-element.53), channel_id=1, source_target_pairs={{0,1},{2,3},{1,0},{3,2},{4,5},{6,7},{5,4},{7,6},{8,9},{10,11},{9,8... | collective-permute-start | bytes 442376 | tf_op jit(solution)/shard_map/ppermute | solution.py:384
  68.2 3.9 %collective-permute-start.19 = (f32[72,128]{1,0:T(8,128)S(1)}, f32[72,128]{1,0:T(8,128)S(1)}, u32[]{:S(2)}, u32[]{:S(2)}) collective-permute-start(f32[72,128]{1,0:T(8,128)S(1)} %get-tuple-element.55), channel_id=1, source_target_pairs={{0,4},{4,0},{8,12},{12,8},{1,5},{5,1},{9,13},{13,9},{2,6},{6,2},{1... | collective-permute-start | bytes 110600 | tf_op jit(solution)/shard_map/ppermute | solution.py:386
  68.6 4.3 %collective-permute-start.20 = (f32[72,128]{1,0:T(8,128)S(1)}, f32[72,128]{1,0:T(8,128)S(1)}, u32[]{:S(2)}, u32[]{:S(2)}) collective-permute-start(f32[72,128]{1,0:T(8,128)S(1)} %get-tuple-element.56), channel_id=1, source_target_pairs={{0,8},{4,12},{8,0},{12,4},{1,9},{5,13},{9,1},{13,5},{2,10},{6,14},... | collective-permute-start | bytes 110600 | tf_op jit(solution)/shard_map/ppermute | solution.py:386
  70.4 4.1 %collective-permute-start.21 = (f32[72,128]{1,0:T(8,128)S(1)}, f32[72,128]{1,0:T(8,128)S(1)}, u32[]{:S(2)}, u32[]{:S(2)}) collective-permute-start(f32[72,128]{1,0:T(8,128)S(1)} %get-tuple-element.57), channel_id=1, source_target_pairs={{0,12},{4,8},{8,4},{12,0},{1,13},{5,9},{9,5},{13,1},{2,14},{6,10},... | collective-permute-start | bytes 110600 | tf_op jit(solution)/shard_map/ppermute | solution.py:386

commit v3 on v2

--- a/solution.py
+++ b/solution.py
@@ -225,6 +225,15 @@
         send_ref[2 * s + 1] = there
 
 
+def split(one, count):
+    parts = []
+    for _ in range(count):
+        part = one.astype(jnp.bfloat16)
+        parts.append(part)
+        one = one - part.astype(F32)
+    return parts
+
+
 def place_kernel(got_ref, *refs):
     keep_ref, give_ref, wide_ref, chunk_ref = refs
     half = lax.div(lax.axis_index("normal"), 2)
@@ -242,6 +251,7 @@
     hits = jnp.concatenate(
         [jnp.where(point == jnp.broadcast_to(first + 4.0 * h, (64, 128)), 1.0, 0.0) for h in range(2)], axis=1
     )
+    hits = hits.astype(jnp.bfloat16)
     masks = [where == float(block) for block in range(4)]
     for r in range(3):
         for a in range(4):
@@ -253,7 +263,7 @@
                     wide_ref[r, base : base + WINDOWS, block * 128 : block * 128 + 128] = jnp.where(
                         masks[block], view, 0.0
                     )
-        placed = jnp.dot(hits, wide_ref[r], precision=HIGHEST, preferred_element_type=F32)
+        placed = sum(jnp.dot(hits, part, preferred_element_type=F32) for part in split(wide_ref[r], 3))
         for i in range(8):
             for block in range(4):
                 base = (r * 4 + block) * ROWS
@@ -383,7 +393,9 @@
     )
     got = lax.ppermute(give, "normal", pairing("normal", 0))
     mine, *chunks = call(join_kernel, (shape(72, 128),) * 4, (keep, got))
-    got = [lax.ppermute(one, "chord", [(i, i ^ d) for i in range(4)]) for d, one in enumerate(chunks, 1)]
+    got = []
+    for d, one in enumerate(chunks, 1):
+        got.append(lax.ppermute(one, "chord", [(i, i ^ d) for i in range(4)]))
     grad = call(sum_kernel, shape(3, 1, 3072), (mine, *got), scratch=((72, 128),))
     return final, grad.reshape(1, 3, 3072)
 

time: 75.3 us -> 74.9 us (level)
  no operation moved by 1% of the time
where the time goes in v3:
time: 74.9 us; the launch traced here: 74.7 us
  starting transfers between devices  37.8 us (50%)
  blocking collectives  18.4 us (25%)
  waiting for transfers between devices  10.2 us (14%)
  Pallas kernels  6.88 us (9%)
  between operations  1.46 us (2%)
    ppermute x18, starting transfers between devices, swap(): got.append(lax.ppermute(one, AXES[name], pairing(AXES[name], at % 2)))  31.4 us
    all_to_all x1, blocking collectives, local(): lax.all_to_all(windows, ALL, 0, 0, axis_index_groups=owners(), tiled=True)  18.4 us
    ppermute x18, waiting for transfers between devices, swap(): got.append(lax.ppermute(one, AXES[name], pairing(AXES[name], at % 2)))  6.91 us
    pallas_call x7, Pallas kernels, call(): pl.pallas_call(body, out_shape=outs, in_specs=specs, out_specs=jax.tree.m...  6.88 us
    ppermute x3, starting transfers between devices, local(): got.append(lax.ppermute(one, 'chord', [(i, i ^ d) for i in range(4)]))  3.95 us
    ppermute x1, starting transfers between devices, local(): got = lax.ppermute(give, 'normal', pairing('normal', 0))  2.38 us
    ppermute x3, waiting for transfers between devices, local(): got.append(lax.ppermute(one, 'chord', [(i, i ^ d) for i in range(4)]))  2.27 us
  transfers between devices with their start and end apart: 22, of which 9 were waited for; matrix products, arithmetic and copies ran while one was open for 0% of the time, Pallas kernels for 0%

profile of v3, /device:TPU:1, one launch (start us, length us, event | category | flops | bytes accessed | tf_op | source)
XLA Modules:
  0.0 74.7 jit_solution(8801911853511269223)
XLA Ops:
  0.6 0.0 copy-start.2
  0.6 0.0 copy-start.3
  0.7 0.0 copy-start.1
  0.7 0.0 copy-start
  0.7 1.2 %shard_map.122 = (f32[5,8,128]{2,1,0:T(8,128)S(1)}, f32[5,8,128]{2,1,0:T(8,128)S(1)}, f32[40,128]{1,0:T(8,128)S(1)}, f32[40,128]{1,0:T(8,128)S(1)}, f32[8,128]{1,0:T(8,128)S(1)}, /*index=5*/f32[8,128]{1,0:T(8,128)S(1)}) custom-call(f32[5,8,8,128]{3,2,1,0:T(8,128)} %adjoint_any.3), custom_call_target="tpu_custom_call" | custom-call | tf_op jit(solution)/shard_map/pallas_call | solution.py:312
  1.9 2.5 %collective-permute-start = (f32[5,8,128]{2,1,0:T(8,128)S(1)}, f32[5,8,128]{2,1,0:T(8,128)S(1)}, u32[]{:S(2)}, u32[]{:S(2)}) collective-permute-start(f32[5,8,128]{2,1,0:T(8,128)S(1)} %get-tuple-element.30), channel_id=1, source_target_pairs={{0,16},{32,48},{64,80},{96,112},{128,144},{160,176},{192,208},{224... | collective-permute-start | bytes 61448 | tf_op jit(solution)/shard_map/ppermute | solution.py:343
  4.4 5.7 %collective-permute-start.1 = (f32[5,8,128]{2,1,0:T(8,128)S(1)}, f32[5,8,128]{2,1,0:T(8,128)S(1)}, u32[]{:S(2)}, u32[]{:S(2)}) collective-permute-start(f32[5,8,128]{2,1,0:T(8,128)S(1)} %get-tuple-element.31), channel_id=1, source_target_pairs={{16,32},{48,64},{80,96},{112,128},{144,160},{176,192},{208,224},{2... | collective-permute-start | bytes 61448 | tf_op jit(solution)/shard_map/ppermute | solution.py:343
  10.1 1.2 %collective-permute-start.2 = (f32[40,128]{1,0:T(8,128)S(1)}, f32[40,128]{1,0:T(8,128)S(1)}, u32[]{:S(2)}, u32[]{:S(2)}) collective-permute-start(f32[40,128]{1,0:T(8,128)S(1)} %get-tuple-element.32), channel_id=1, source_target_pairs={{0,4},{8,12},{4,0},{12,8},{1,5},{9,13},{5,1},{13,9},{2,6},{10,14},... | collective-permute-start | bytes 61448 | tf_op jit(solution)/shard_map/ppermute | solution.py:343
  11.3 1.8 %collective-permute-start.3 = (f32[40,128]{1,0:T(8,128)S(1)}, f32[40,128]{1,0:T(8,128)S(1)}, u32[]{:S(2)}, u32[]{:S(2)}) collective-permute-start(f32[40,128]{1,0:T(8,128)S(1)} %get-tuple-element.33), channel_id=1, source_target_pairs={{4,8},{12,0},{8,4},{0,12},{5,9},{13,1},{9,5},{1,13},{6,10},{14,2},... | collective-permute-start | bytes 61448 | tf_op jit(solution)/shard_map/ppermute | solution.py:343
  13.1 1.8 %collective-permute-start.4 = (f32[8,128]{1,0:T(8,128)S(1)}, f32[8,128]{1,0:T(8,128)S(1)}, u32[]{:S(2)}, u32[]{:S(2)}) collective-permute-start(f32[8,128]{1,0:T(8,128)S(1)} %get-tuple-element.34), channel_id=1, source_target_pairs={{0,1},{2,3},{1,0},{3,2},{4,5},{6,7},{5,4},{7,6},{8,9},{10,11},{9,8... | collective-permute-start | bytes 12296 | tf_op jit(solution)/shard_map/ppermute | solution.py:343
  14.9 0.8 %collective-permute-done.4.refs_4_ = f32[8,128]{1,0:T(8,128)S(1)} collective-permute-done((f32[8,128]{1,0:T(8,128)S(1)}, f32[8,128]{1,0:T(8,128)S(1)}, u32[]{:S(2)}, u32[]{:S(2)}) %collective-permute-start.4) | collective-permute-done | bytes 4128 | tf_op jit(solution)/shard_map/ppermute | solution.py:343
  15.7 2.8 %collective-permute-start.5 = (f32[8,128]{1,0:T(8,128)S(1)}, f32[8,128]{1,0:T(8,128)S(1)}, u32[]{:S(2)}, u32[]{:S(2)}) collective-permute-start(f32[8,128]{1,0:T(8,128)S(1)} %get-tuple-element.35), channel_id=1, source_target_pairs={{1,2},{3,0},{2,1},{0,3},{5,6},{7,4},{6,5},{4,7},{9,10},{11,8},{10,... | collective-permute-start | bytes 12296 | tf_op jit(solution)/shard_map/ppermute | solution.py:343
  18.6 1.7 %collective-permute-done.5.refs_5_ = f32[8,128]{1,0:T(8,128)S(1)} collective-permute-done((f32[8,128]{1,0:T(8,128)S(1)}, f32[8,128]{1,0:T(8,128)S(1)}, u32[]{:S(2)}, u32[]{:S(2)}) %collective-permute-start.5) | collective-permute-done | bytes 4128 | tf_op jit(solution)/shard_map/ppermute | solution.py:343
  20.3 0.0 collective-permute-done.refs_0_
  20.3 0.0 collective-permute-done.1.refs_1_
  20.3 0.0 collective-permute-done.3.refs_3_
  20.3 2.6 %shard_map.123 = (f32[3,8,8,128]{3,2,1,0:T(8,128)S(1)}, f32[3,8,128]{2,1,0:T(8,128)S(1)}, f32[3,8,128]{2,1,0:T(8,128)S(1)}, f32[24,128]{1,0:T(8,128)S(1)}, f32[2...) custom-call(f32[5,3,5]{2,1,0:T(4,128)} %bitcast.9, f32[3,5]{1,0:T(4,128)} %map_any.1, ...), custom_call_target="tpu_custom_call" | custom-call | tf_op jit(solution)/shard_map/pallas_call | solution.py:312
  22.9 0.1 collective-permute-start.6
  23.0 1.4 %collective-permute-start.7 = (f32[3,8,128]{2,1,0:T(8,128)S(1)}, f32[3,8,128]{2,1,0:T(8,128)S(1)}, u32[]{:S(2)}, u32[]{:S(2)}) collective-permute-start(f32[3,8,128]{2,1,0:T(8,128)S(1)} %get-tuple-element.38), channel_id=1, source_target_pairs={{16,32},{48,64},{80,96},{112,128},{144,160},{176,192},{208,224},{2... | collective-permute-start | bytes 36872 | tf_op jit(solution)/shard_map/ppermute | solution.py:343
  24.5 0.3 collective-permute-start.8
  24.8 0.6 collective-permute-start.9
  25.3 1.2 %collective-permute-start.10 = (f32[8,128]{1,0:T(8,128)S(1)}, f32[8,128]{1,0:T(8,128)S(1)}, u32[]{:S(2)}, u32[]{:S(2)}) collective-permute-start(f32[8,128]{1,0:T(8,128)S(1)} %get-tuple-element.41), channel_id=1, source_target_pairs={{0,1},{2,3},{1,0},{3,2},{4,5},{6,7},{5,4},{7,6},{8,9},{10,11},{9,8... | collective-permute-start | bytes 12296 | tf_op jit(solution)/shard_map/ppermute | solution.py:343
  26.6 0.8 %collective-permute-done.10.refs_4_ = f32[8,128]{1,0:T(8,128)S(1)} collective-permute-done((f32[8,128]{1,0:T(8,128)S(1)}, f32[8,128]{1,0:T(8,128)S(1)}, u32[]{:S(2)}, u32[]{:S(2)}) %collective-permute-start.10) | collective-permute-done | bytes 4128 | tf_op jit(solution)/shard_map/ppermute | solution.py:343
  27.4 2.8 %collective-permute-start.11 = (f32[8,128]{1,0:T(8,128)S(1)}, f32[8,128]{1,0:T(8,128)S(1)}, u32[]{:S(2)}, u32[]{:S(2)}) collective-permute-start(f32[8,128]{1,0:T(8,128)S(1)} %get-tuple-element.42), channel_id=1, source_target_pairs={{1,2},{3,0},{2,1},{0,3},{5,6},{7,4},{6,5},{4,7},{9,10},{11,8},{10,... | collective-permute-start | bytes 12296 | tf_op jit(solution)/shard_map/ppermute | solution.py:343
  30.3 1.7 %collective-permute-done.11.refs_5_ = f32[8,128]{1,0:T(8,128)S(1)} collective-permute-done((f32[8,128]{1,0:T(8,128)S(1)}, f32[8,128]{1,0:T(8,128)S(1)}, u32[]{:S(2)}, u32[]{:S(2)}) %collective-permute-start.11) | collective-permute-done | bytes 4128 | tf_op jit(solution)/shard_map/ppermute | solution.py:343
  31.9 0.0 collective-permute-done.6.refs_0_
  32.0 0.3 shard_map.124
  32.3 0.1 collective-permute-start.12
  32.4 2.0 %collective-permute-start.13 = (f32[3,8,128]{2,1,0:T(8,128)S(1)}, f32[3,8,128]{2,1,0:T(8,128)S(1)}, u32[]{:S(2)}, u32[]{:S(2)}) collective-permute-start(f32[3,8,128]{2,1,0:T(8,128)S(1)} %get-tuple-element.45), channel_id=1, source_target_pairs={{16,32},{48,64},{80,96},{112,128},{144,160},{176,192},{208,224},{2... | collective-permute-start | bytes 36872 | tf_op jit(solution)/shard_map/ppermute | solution.py:343
  34.4 1.1 %collective-permute-start.14 = (f32[24,128]{1,0:T(8,128)S(1)}, f32[24,128]{1,0:T(8,128)S(1)}, u32[]{:S(2)}, u32[]{:S(2)}) collective-permute-start(f32[24,128]{1,0:T(8,128)S(1)} %get-tuple-element.46), channel_id=1, source_target_pairs={{0,4},{8,12},{4,0},{12,8},{1,5},{9,13},{5,1},{13,9},{2,6},{10,14},... | collective-permute-start | bytes 36872 | tf_op jit(solution)/shard_map/ppermute | solution.py:343
  35.5 1.8 %collective-permute-start.15 = (f32[24,128]{1,0:T(8,128)S(1)}, f32[24,128]{1,0:T(8,128)S(1)}, u32[]{:S(2)}, u32[]{:S(2)}) collective-permute-start(f32[24,128]{1,0:T(8,128)S(1)} %get-tuple-element.47), channel_id=1, source_target_pairs={{4,8},{12,0},{8,4},{0,12},{5,9},{13,1},{9,5},{1,13},{6,10},{14,2},... | collective-permute-start | bytes 36872 | tf_op jit(solution)/shard_map/ppermute | solution.py:343
  37.3 1.2 %collective-permute-start.16 = (f32[8,128]{1,0:T(8,128)S(1)}, f32[8,128]{1,0:T(8,128)S(1)}, u32[]{:S(2)}, u32[]{:S(2)}) collective-permute-start(f32[8,128]{1,0:T(8,128)S(1)} %get-tuple-element.48), channel_id=1, source_target_pairs={{0,1},{2,3},{1,0},{3,2},{4,5},{6,7},{5,4},{7,6},{8,9},{10,11},{9,8... | collective-permute-start | bytes 12296 | tf_op jit(solution)/shard_map/ppermute | solution.py:343
  38.5 0.8 %collective-permute-done.16.refs_4_ = f32[8,128]{1,0:T(8,128)S(1)} collective-permute-done((f32[8,128]{1,0:T(8,128)S(1)}, f32[8,128]{1,0:T(8,128)S(1)}, u32[]{:S(2)}, u32[]{:S(2)}) %collective-permute-start.16) | collective-permute-done | bytes 4128 | tf_op jit(solution)/shard_map/ppermute | solution.py:343
  39.3 2.8 %collective-permute-start.17 = (f32[8,128]{1,0:T(8,128)S(1)}, f32[8,128]{1,0:T(8,128)S(1)}, u32[]{:S(2)}, u32[]{:S(2)}) collective-permute-start(f32[8,128]{1,0:T(8,128)S(1)} %get-tuple-element.49), channel_id=1, source_target_pairs={{1,2},{3,0},{2,1},{0,3},{5,6},{7,4},{6,5},{4,7},{9,10},{11,8},{10,... | collective-permute-start | bytes 12296 | tf_op jit(solution)/shard_map/ppermute | solution.py:343
  42.8 1.0 %collective-permute-done.17.refs_5_ = f32[8,128]{1,0:T(8,128)S(1)} collective-permute-done((f32[8,128]{1,0:T(8,128)S(1)}, f32[8,128]{1,0:T(8,128)S(1)}, u32[]{:S(2)}, u32[]{:S(2)}) %collective-permute-start.17) | collective-permute-done | bytes 4128 | tf_op jit(solution)/shard_map/ppermute | solution.py:343
  43.8 0.0 collective-permute-done.14.refs_2_
  43.8 0.0 collective-permute-done.15.refs_3_
  43.9 1.4 %shard_map.125 = (f32[3,8,8,128]{3,2,1,0:T(8,128)}, f32[32,16,128]{2,1,0:T(8,128)S(1)}) custom-call(s32[1]{0:T(128)} %bitcast.5.box_ref, s32[3]{0:T(128)S(1)} %bitcast.7, f32[3,8,8,128]{3,2,1,0:T(8,128)S(1)} %get-tuple-element.43.now_ref, f32[3,8,8,128]{3,2,1,0:T(8,128)S(1)} %get-tuple-element.36.start_ref, f32[7,8,8,128]{3,2,1,0:T(8,128)S(1)} %copy-done, ...), custom_call_target="tpu_custom_call" | custom-call | tf_op jit(solution)/shard_map/pallas_call | solution.py:312
  45.3 18.4 %all_to_all.5 = f32[32,16,128]{2,1,0:T(8,128)S(1)} all-to-all(f32[32,16,128]{2,1,0:T(8,128)S(1)} %get-tuple-element.51), channel_id=1, replica_groups={{0,2,16,18,32,34,48,50,64,66,80,82,96,98,112,114,128,130,144,146,160,16..., dimensions={0} | all-to-all | bytes 524288 | tf_op jit(solution)/shard_map/all_to_all | solution.py:387
  63.7 0.8 %shard_map.126 = (f32[4,72,128]{2,1,0:T(8,128)S(1)}, f32[4,72,128]{2,1,0:T(8,128)S(1)}) custom-call(f32[512,128]{1,0:T(8,128)S(1)} %bitcast.6), custom_call_target="tpu_custom_call" | custom-call | tf_op jit(solution)/shard_map/pallas_call | solution.py:312
  64.4 2.4 %collective-permute-start.18 = (f32[4,72,128]{2,1,0:T(8,128)S(1)}, f32[4,72,128]{2,1,0:T(8,128)S(1)}, u32[]{:S(2)}, u32[]{:S(2)}) collective-permute-start(f32[4,72,128]{2,1,0:T(8,128)S(1)} %get-tuple-element.53), channel_id=1, source_target_pairs={{0,1},{2,3},{1,0},{3,2},{4,5},{6,7},{5,4},{7,6},{8,9},{10,11},{9,8... | collective-permute-start | bytes 442376 | tf_op jit(solution)/shard_map/ppermute | solution.py:394
  66.8 1.0 %collective-permute-done.18.got_ref = f32[4,72,128]{2,1,0:T(8,128)S(1)} collective-permute-done((f32[4,72,128]{2,1,0:T(8,128)S(1)}, f32[4,72,128]{2,1,0:T(8,128)S(1)}, u32[]{:S(2)}, u32[]{:S(2)}) %collective-permute-start.18) | collective-permute-done | bytes 147488 | tf_op jit(solution)/shard_map/ppermute | solution.py:394
  67.8 0.4 collective-permute-start.19
  68.2 1.7 %collective-permute-start.20 = (f32[72,128]{1,0:T(8,128)S(1)}, f32[72,128]{1,0:T(8,128)S(1)}, u32[]{:S(2)}, u32[]{:S(2)}) collective-permute-start(f32[72,128]{1,0:T(8,128)S(1)} %get-tuple-element.56), channel_id=1, source_target_pairs={{0,8},{4,12},{8,0},{12,4},{1,9},{5,13},{9,1},{13,5},{2,10},{6,14},... | collective-permute-start | bytes 110600 | tf_op jit(solution)/shard_map/ppermute | solution.py:398
  70.0 1.8 %collective-permute-start.21 = (f32[72,128]{1,0:T(8,128)S(1)}, f32[72,128]{1,0:T(8,128)S(1)}, u32[]{:S(2)}, u32[]{:S(2)}) collective-permute-start(f32[72,128]{1,0:T(8,128)S(1)} %get-tuple-element.57), channel_id=1, source_target_pairs={{0,12},{4,8},{8,4},{12,0},{1,13},{5,9},{9,5},{13,1},{2,14},{6,10},... | collective-permute-start | bytes 110600 | tf_op jit(solution)/shard_map/ppermute | solution.py:398
  71.8 0.8 %collective-permute-done.20.refs_2_ = f32[72,128]{1,0:T(8,128)S(1)} collective-permute-done((f32[72,128]{1,0:T(8,128)S(1)}, f32[72,128]{1,0:T(8,128)S(1)}, u32[]{:S(2)}, u32[]{:S(2)}) %collective-permute-start.20) | collective-permute-done | bytes 36896 | tf_op jit(solution)/shard_map/ppermute | solution.py:398
  72.6 1.5 %collective-permute-done.21.refs_3_ = f32[72,128]{1,0:T(8,128)S(1)} collective-permute-done((f32[72,128]{1,0:T(8,128)S(1)}, f32[72,128]{1,0:T(8,128)S(1)}, u32[]{:S(2)}, u32[]{:S(2)}) %collective-permute-start.21) | collective-permute-done | bytes 36896 | tf_op jit(solution)/shard_map/ppermute | solution.py:398
  74.1 0.7 shard_map.128
  (14 shorter events, 0.0 us)
Async XLA Ops:
  0.6 43.2 %copy-start.2 = (f32[32,192]{1,0:T(8,128)S(1)}, f32[32,192]{1,0:T(8,128)}, u32[]{:S(2)}) copy-start(f32[32,192]{1,0:T(8,128)} %constant.8.clone.bx_ref) | copy-start | bytes 73732
  0.6 43.2 %copy-start.3 = (f32[8,128]{1,0:T(8,128)S(1)}, f32[8,128]{1,0:T(8,128)}, u32[]{:S(2)}) copy-start(f32[8,128]{1,0:T(8,128)} %constant.7.clone.by_ref) | copy-start | bytes 12292
  0.7 43.2 %copy-start.1 = (f32[128,128]{1,0:T(8,128)S(1)}, f32[128,128]{1,0:T(8,128)}, u32[]{:S(2)}) copy-start(f32[128,128]{1,0:T(8,128)} %constant.6.clone.bz_ref) | copy-start | bytes 196612
  0.7 31.3 %copy-start = (f32[7,8,8,128]{3,2,1,0:T(8,128)S(1)}, f32[7,8,8,128]{3,2,1,0:T(8,128)}, u32[]{:S(2)}) copy-start(f32[7,8,8,128]{3,2,1,0:T(8,128)} %stiff_ref.3) | copy-start | bytes 688132
  0.7 43.2 %copy-start.4 = (s32[1,1,1,3]{3,2,1,0:T(1,128)S(1)}, s32[1,1,1,3]{3,2,1,0:T(1,128)}, u32[]{:S(2)}) copy-start(s32[1,1,1,3]{3,2,1,0:T(1,128)} %param.18) | copy-start | bytes 40
  1.9 18.4 %collective-permute-start = (f32[5,8,128]{2,1,0:T(8,128)S(1)}, f32[5,8,128]{2,1,0:T(8,128)S(1)}, u32[]{:S(2)}, u32[]{:S(2)}) collective-permute-start(f32[5,8,128]{2,1,0:T(8,128)S(1)} %get-tuple-element.30), channel_id=1, source_target_pairs={{0,16},{32,48},{64,80},{96,112},{128,144},{160,176},{192,208},{224... | collective-permute-start | bytes 61448 | tf_op jit(solution)/shard_map/ppermute | solution.py:343
  4.4 15.9 %collective-permute-start.1 = (f32[5,8,128]{2,1,0:T(8,128)S(1)}, f32[5,8,128]{2,1,0:T(8,128)S(1)}, u32[]{:S(2)}, u32[]{:S(2)}) collective-permute-start(f32[5,8,128]{2,1,0:T(8,128)S(1)} %get-tuple-element.31), channel_id=1, source_target_pairs={{16,32},{48,64},{80,96},{112,128},{144,160},{176,192},{208,224},{2... | collective-permute-start | bytes 61448 | tf_op jit(solution)/shard_map/ppermute | solution.py:343
  10.1 10.2 %collective-permute-start.2 = (f32[40,128]{1,0:T(8,128)S(1)}, f32[40,128]{1,0:T(8,128)S(1)}, u32[]{:S(2)}, u32[]{:S(2)}) collective-permute-start(f32[40,128]{1,0:T(8,128)S(1)} %get-tuple-element.32), channel_id=1, source_target_pairs={{0,4},{8,12},{4,0},{12,8},{1,5},{9,13},{5,1},{13,9},{2,6},{10,14},... | collective-permute-start | bytes 61448 | tf_op jit(solution)/shard_map/ppermute | solution.py:343
  11.3 9.0 %collective-permute-start.3 = (f32[40,128]{1,0:T(8,128)S(1)}, f32[40,128]{1,0:T(8,128)S(1)}, u32[]{:S(2)}, u32[]{:S(2)}) collective-permute-start(f32[40,128]{1,0:T(8,128)S(1)} %get-tuple-element.33), channel_id=1, source_target_pairs={{4,8},{12,0},{8,4},{0,12},{5,9},{13,1},{9,5},{1,13},{6,10},{14,2},... | collective-permute-start | bytes 61448 | tf_op jit(solution)/shard_map/ppermute | solution.py:343
  13.1 2.6 %collective-permute-start.4 = (f32[8,128]{1,0:T(8,128)S(1)}, f32[8,128]{1,0:T(8,128)S(1)}, u32[]{:S(2)}, u32[]{:S(2)}) collective-permute-start(f32[8,128]{1,0:T(8,128)S(1)} %get-tuple-element.34), channel_id=1, source_target_pairs={{0,1},{2,3},{1,0},{3,2},{4,5},{6,7},{5,4},{7,6},{8,9},{10,11},{9,8... | collective-permute-start | bytes 12296 | tf_op jit(solution)/shard_map/ppermute | solution.py:343
  15.7 4.5 %collective-permute-start.5 = (f32[8,128]{1,0:T(8,128)S(1)}, f32[8,128]{1,0:T(8,128)S(1)}, u32[]{:S(2)}, u32[]{:S(2)}) collective-permute-start(f32[8,128]{1,0:T(8,128)S(1)} %get-tuple-element.35), channel_id=1, source_target_pairs={{1,2},{3,0},{2,1},{0,3},{5,6},{7,4},{6,5},{4,7},{9,10},{11,8},{10,... | collective-permute-start | bytes 12296 | tf_op jit(solution)/shard_map/ppermute | solution.py:343
  22.9 9.0 %collective-permute-start.6 = (f32[3,8,128]{2,1,0:T(8,128)S(1)}, f32[3,8,128]{2,1,0:T(8,128)S(1)}, u32[]{:S(2)}, u32[]{:S(2)}) collective-permute-start(f32[3,8,128]{2,1,0:T(8,128)S(1)} %get-tuple-element.37), channel_id=1, source_target_pairs={{0,16},{32,48},{64,80},{96,112},{128,144},{160,176},{192,208},{224... | collective-permute-start | bytes 36872 | tf_op jit(solution)/shard_map/ppermute | solution.py:343
  23.0 8.9 %collective-permute-start.7 = (f32[3,8,128]{2,1,0:T(8,128)S(1)}, f32[3,8,128]{2,1,0:T(8,128)S(1)}, u32[]{:S(2)}, u32[]{:S(2)}) collective-permute-start(f32[3,8,128]{2,1,0:T(8,128)S(1)} %get-tuple-element.38), channel_id=1, source_target_pairs={{16,32},{48,64},{80,96},{112,128},{144,160},{176,192},{208,224},{2... | collective-permute-start | bytes 36872 | tf_op jit(solution)/shard_map/ppermute | solution.py:343
  24.5 7.5 %collective-permute-start.8 = (f32[24,128]{1,0:T(8,128)S(1)}, f32[24,128]{1,0:T(8,128)S(1)}, u32[]{:S(2)}, u32[]{:S(2)}) collective-permute-start(f32[24,128]{1,0:T(8,128)S(1)} %get-tuple-element.39), channel_id=1, source_target_pairs={{0,4},{8,12},{4,0},{12,8},{1,5},{9,13},{5,1},{13,9},{2,6},{10,14},... | collective-permute-start | bytes 36872 | tf_op jit(solution)/shard_map/ppermute | solution.py:343
  24.8 7.2 %collective-permute-start.9 = (f32[24,128]{1,0:T(8,128)S(1)}, f32[24,128]{1,0:T(8,128)S(1)}, u32[]{:S(2)}, u32[]{:S(2)}) collective-permute-start(f32[24,128]{1,0:T(8,128)S(1)} %get-tuple-element.40), channel_id=1, source_target_pairs={{4,8},{12,0},{8,4},{0,12},{5,9},{13,1},{9,5},{1,13},{6,10},{14,2},... | collective-permute-start | bytes 36872 | tf_op jit(solution)/shard_map/ppermute | solution.py:343
  25.3 2.1 %collective-permute-start.10 = (f32[8,128]{1,0:T(8,128)S(1)}, f32[8,128]{1,0:T(8,128)S(1)}, u32[]{:S(2)}, u32[]{:S(2)}) collective-permute-start(f32[8,128]{1,0:T(8,128)S(1)} %get-tuple-element.41), channel_id=1, source_target_pairs={{0,1},{2,3},{1,0},{3,2},{4,5},{6,7},{5,4},{7,6},{8,9},{10,11},{9,8... | collective-permute-start | bytes 12296 | tf_op jit(solution)/shard_map/ppermute | solution.py:343
  27.4 4.5 %collective-permute-start.11 = (f32[8,128]{1,0:T(8,128)S(1)}, f32[8,128]{1,0:T(8,128)S(1)}, u32[]{:S(2)}, u32[]{:S(2)}) collective-permute-start(f32[8,128]{1,0:T(8,128)S(1)} %get-tuple-element.42), channel_id=1, source_target_pairs={{1,2},{3,0},{2,1},{0,3},{5,6},{7,4},{6,5},{4,7},{9,10},{11,8},{10,... | collective-permute-start | bytes 12296 | tf_op jit(solution)/shard_map/ppermute | solution.py:343
  32.3 11.6 %collective-permute-start.12 = (f32[3,8,128]{2,1,0:T(8,128)S(1)}, f32[3,8,128]{2,1,0:T(8,128)S(1)}, u32[]{:S(2)}, u32[]{:S(2)}) collective-permute-start(f32[3,8,128]{2,1,0:T(8,128)S(1)} %get-tuple-element.44), channel_id=1, source_target_pairs={{0,16},{32,48},{64,80},{96,112},{128,144},{160,176},{192,208},{224... | collective-permute-start | bytes 36872 | tf_op jit(solution)/shard_map/ppermute | solution.py:343
  32.4 11.5 %collective-permute-start.13 = (f32[3,8,128]{2,1,0:T(8,128)S(1)}, f32[3,8,128]{2,1,0:T(8,128)S(1)}, u32[]{:S(2)}, u32[]{:S(2)}) collective-permute-start(f32[3,8,128]{2,1,0:T(8,128)S(1)} %get-tuple-element.45), channel_id=1, source_target_pairs={{16,32},{48,64},{80,96},{112,128},{144,160},{176,192},{208,224},{2... | collective-permute-start | bytes 36872 | tf_op jit(solution)/shard_map/ppermute | solution.py:343
  34.4 9.5 %collective-permute-start.14 = (f32[24,128]{1,0:T(8,128)S(1)}, f32[24,128]{1,0:T(8,128)S(1)}, u32[]{:S(2)}, u32[]{:S(2)}) collective-permute-start(f32[24,128]{1,0:T(8,128)S(1)} %get-tuple-element.46), channel_id=1, source_target_pairs={{0,4},{8,12},{4,0},{12,8},{1,5},{9,13},{5,1},{13,9},{2,6},{10,14},... | collective-permute-start | bytes 36872 | tf_op jit(solution)/shard_map/ppermute | solution.py:343
  35.5 8.4 %collective-permute-start.15 = (f32[24,128]{1,0:T(8,128)S(1)}, f32[24,128]{1,0:T(8,128)S(1)}, u32[]{:S(2)}, u32[]{:S(2)}) collective-permute-start(f32[24,128]{1,0:T(8,128)S(1)} %get-tuple-element.47), channel_id=1, source_target_pairs={{4,8},{12,0},{8,4},{0,12},{5,9},{13,1},{9,5},{1,13},{6,10},{14,2},... | collective-permute-start | bytes 36872 | tf_op jit(solution)/shard_map/ppermute | solution.py:343
  37.3 2.0 %collective-permute-start.16 = (f32[8,128]{1,0:T(8,128)S(1)}, f32[8,128]{1,0:T(8,128)S(1)}, u32[]{:S(2)}, u32[]{:S(2)}) collective-permute-start(f32[8,128]{1,0:T(8,128)S(1)} %get-tuple-element.48), channel_id=1, source_target_pairs={{0,1},{2,3},{1,0},{3,2},{4,5},{6,7},{5,4},{7,6},{8,9},{10,11},{9,8... | collective-permute-start | bytes 12296 | tf_op jit(solution)/shard_map/ppermute | solution.py:343
  39.3 4.5 %collective-permute-start.17 = (f32[8,128]{1,0:T(8,128)S(1)}, f32[8,128]{1,0:T(8,128)S(1)}, u32[]{:S(2)}, u32[]{:S(2)}) collective-permute-start(f32[8,128]{1,0:T(8,128)S(1)} %get-tuple-element.49), channel_id=1, source_target_pairs={{1,2},{3,0},{2,1},{0,3},{5,6},{7,4},{6,5},{4,7},{9,10},{11,8},{10,... | collective-permute-start | bytes 12296 | tf_op jit(solution)/shard_map/ppermute | solution.py:343
  64.4 3.4 %collective-permute-start.18 = (f32[4,72,128]{2,1,0:T(8,128)S(1)}, f32[4,72,128]{2,1,0:T(8,128)S(1)}, u32[]{:S(2)}, u32[]{:S(2)}) collective-permute-start(f32[4,72,128]{2,1,0:T(8,128)S(1)} %get-tuple-element.53), channel_id=1, source_target_pairs={{0,1},{2,3},{1,0},{3,2},{4,5},{6,7},{5,4},{7,6},{8,9},{10,11},{9,8... | collective-permute-start | bytes 442376 | tf_op jit(solution)/shard_map/ppermute | solution.py:394
  67.8 3.9 %collective-permute-start.19 = (f32[72,128]{1,0:T(8,128)S(1)}, f32[72,128]{1,0:T(8,128)S(1)}, u32[]{:S(2)}, u32[]{:S(2)}) collective-permute-start(f32[72,128]{1,0:T(8,128)S(1)} %get-tuple-element.55), channel_id=1, source_target_pairs={{0,4},{4,0},{8,12},{12,8},{1,5},{5,1},{9,13},{13,9},{2,6},{6,2},{1... | collective-permute-start | bytes 110600 | tf_op jit(solution)/shard_map/ppermute | solution.py:398
  68.2 4.3 %collective-permute-start.20 = (f32[72,128]{1,0:T(8,128)S(1)}, f32[72,128]{1,0:T(8,128)S(1)}, u32[]{:S(2)}, u32[]{:S(2)}) collective-permute-start(f32[72,128]{1,0:T(8,128)S(1)} %get-tuple-element.56), channel_id=1, source_target_pairs={{0,8},{4,12},{8,0},{12,4},{1,9},{5,13},{9,1},{13,5},{2,10},{6,14},... | collective-permute-start | bytes 110600 | tf_op jit(solution)/shard_map/ppermute | solution.py:398
  70.0 4.1 %collective-permute-start.21 = (f32[72,128]{1,0:T(8,128)S(1)}, f32[72,128]{1,0:T(8,128)S(1)}, u32[]{:S(2)}, u32[]{:S(2)}) collective-permute-start(f32[72,128]{1,0:T(8,128)S(1)} %get-tuple-element.57), channel_id=1, source_target_pairs={{0,12},{4,8},{8,4},{12,0},{1,13},{5,9},{9,5},{13,1},{2,14},{6,10},... | collective-permute-start | bytes 110600 | tf_op jit(solution)/shard_map/ppermute | solution.py:398

commit v4 on v3

--- a/solution.py
+++ b/solution.py
@@ -217,12 +217,10 @@
     window = pltpu.roll(window, shift, 1)
     inside = lax.rem(lane - shift + 128, 16) < 8
     block = jnp.where(inside, lax.div(ob, 8) + jnp.where(lane < shift, 1, 0), -1)
-    for s in range(16):
-        where = jnp.where(box == s, block, -1)
-        there = jnp.where(row == 12, where, oa).astype(F32)
-        there = jnp.where(row < 12, window, there)
-        send_ref[2 * s] = there
-        send_ref[2 * s + 1] = there
+    there = jnp.where(row == 12, block, jnp.where(row == 13, oa, box)).astype(F32)
+    there = jnp.where(row < 12, window, there)
+    for at in range(WINDOWS):
+        send_ref[at] = there
 
 
 def split(one, count):
@@ -237,19 +235,24 @@
 def place_kernel(got_ref, *refs):
     keep_ref, give_ref, wide_ref, chunk_ref = refs
     half = lax.div(lax.axis_index("normal"), 2)
+    span = lax.axis_index("span")
+    nearest = lax.div(span, 8) * 8 + lax.rem(span, 2)
     where = got_ref[pl.ds(12, WINDOWS, stride=SLOT), :]
     start = got_ref[pl.ds(13, WINDOWS, stride=SLOT), :]
     lane = lax.broadcasted_iota(jnp.int32, (WINDOWS, 128), 1)
     row = lax.broadcasted_iota(jnp.int32, (WINDOWS, 128), 0)
+    boxes = got_ref[pl.ds(14, WINDOWS, stride=SLOT), :]
+    boxes = jnp.sum(jnp.where(lax.rem(lane, WINDOWS) == row, boxes, 0.0), axis=0, keepdims=True)
     start = jnp.sum(jnp.where(lax.rem(lane, WINDOWS) == row, start, 0.0), axis=0, keepdims=True)
     step = lax.div(lax.broadcasted_iota(jnp.int32, (1, 128), 1), WINDOWS).astype(F32)
     first = start + step
     line = lax.broadcasted_iota(jnp.int32, (64, 128), 0)
     chunk = lax.div(line, 8)
-    owner = lax.div(chunk, 2) * 4 + half * 2 + lax.rem(chunk, 2)
+    owner = lax.axis_index("chord") * 4 + half * 2 + lax.rem(chunk, 2)
+    same = (nearest + 2 * lax.div(chunk, 2)).astype(F32) == jnp.broadcast_to(boxes, (64, 128))
     point = jnp.where(lax.rem(line, 8) < ROWS, owner * ROWS + lax.rem(line, 8), -1).astype(F32)
     hits = jnp.concatenate(
-        [jnp.where(point == jnp.broadcast_to(first + 4.0 * h, (64, 128)), 1.0, 0.0) for h in range(2)], axis=1
+        [jnp.where(same & (point == jnp.broadcast_to(first + 4.0 * h, (64, 128))), 1.0, 0.0) for h in range(2)], axis=1
     )
     hits = hits.astype(jnp.bfloat16)
     masks = [where == float(block) for block in range(4)]
@@ -277,7 +280,7 @@
 
 
 def join_kernel(keep_ref, got_ref, *sends):
-    mine = lax.axis_index("chord")
+    mine = lax.div(lax.rem(lax.axis_index("span"), 8), 2)
     for d in range(4):
         at = lax.bitwise_xor(mine, d)
         sends[d][...] = keep_ref[at] + got_ref[at]
@@ -345,8 +348,8 @@
 
 
 def owners():
-    index = np.arange(256).reshape(16, 4, 2, 2)
-    return index.transpose(1, 3, 0, 2).reshape(8, 32).tolist()
+    index = np.arange(256).reshape(2, 4, 2, 4, 2, 2)
+    return index.transpose(1, 5, 0, 2, 3, 4).reshape(8, 32).tolist()
 
 
 def ends(v):
@@ -395,7 +398,7 @@
     mine, *chunks = call(join_kernel, (shape(72, 128),) * 4, (keep, got))
     got = []
     for d, one in enumerate(chunks, 1):
-        got.append(lax.ppermute(one, "chord", [(i, i ^ d) for i in range(4)]))
+        got.append(lax.ppermute(one, "span", [(i, i ^ (2 * d)) for i in range(16)]))
     grad = call(sum_kernel, shape(3, 1, 3072), (mine, *got), scratch=((72, 128),))
     return final, grad.reshape(1, 3, 3072)
 

time: 74.9 us -> 72.6 us (0.969)
  blocking collectives: 18.4 us -> 13.5 us
  waiting for transfers between devices: 10.2 us -> 11.8 us
  starting transfers between devices: 37.8 us -> 38.7 us
    all_to_all x1, blocking collectives: 18.4 us -> 13.5 us  [local(): lax.all_to_all(windows, ALL, 0, 0, axis_index_groups=owners(), tiled=True)]
    ppermute x3, starting transfers between devices: 3.95 us -> 5.74 us  [local(): got.append(lax.ppermute(one, 'span', [(i, i ^ 2 * d) for i in range(16)]))]
    ppermute x3, waiting for transfers between devices: 2.27 us -> 3.9 us  [local(): got.append(lax.ppermute(one, 'span', [(i, i ^ 2 * d) for i in range(16)]))]
    ppermute x1, starting transfers between devices: 2.38 us -> 1.57 us  [local(): got = lax.ppermute(give, 'normal', pairing('normal', 0))]
where the time goes in v4:
time: 72.6 us; the launch traced here: 72.4 us
  starting transfers between devices  38.7 us (53%)
  blocking collectives  13.5 us (19%)
  waiting for transfers between devices  11.8 us (16%)
  Pallas kernels  6.86 us (9%)
  between operations  1.46 us (2%)
    ppermute x18, starting transfers between devices, swap(): got.append(lax.ppermute(one, AXES[name], pairing(AXES[name], at % 2)))  31.4 us
    all_to_all x1, blocking collectives, local(): lax.all_to_all(windows, ALL, 0, 0, axis_index_groups=owners(), tiled=True)  13.5 us
    ppermute x18, waiting for transfers between devices, swap(): got.append(lax.ppermute(one, AXES[name], pairing(AXES[name], at % 2)))  6.91 us
    pallas_call x7, Pallas kernels, call(): pl.pallas_call(body, out_shape=outs, in_specs=specs, out_specs=jax.tree.m...  6.86 us
    ppermute x3, starting transfers between devices, local(): got.append(lax.ppermute(one, 'span', [(i, i ^ 2 * d) for i in range(16)]))  5.74 us
    ppermute x3, waiting for transfers between devices, local(): got.append(lax.ppermute(one, 'span', [(i, i ^ 2 * d) for i in range(16)]))  3.9 us
    ppermute x1, starting transfers between devices, local(): got = lax.ppermute(give, 'normal', pairing('normal', 0))  1.57 us
  transfers between devices with their start and end apart: 22, of which 9 were waited for; matrix products, arithmetic and copies ran while one was open for 0% of the time, Pallas kernels for 0%

profile of v4, /device:TPU:1, one launch (start us, length us, event | category | flops | bytes accessed | tf_op | source)
XLA Modules:
  0.0 72.4 jit_solution(7224781283770912960)
XLA Ops:
  0.6 0.0 copy-start.2
  0.6 0.0 copy-start.3
  0.7 0.0 copy-start.1
  0.7 0.0 copy-start
  0.7 1.2 %shard_map.122 = (f32[5,8,128]{2,1,0:T(8,128)S(1)}, f32[5,8,128]{2,1,0:T(8,128)S(1)}, f32[40,128]{1,0:T(8,128)S(1)}, f32[40,128]{1,0:T(8,128)S(1)}, f32[8,128]{1,0:T(8,128)S(1)}, /*index=5*/f32[8,128]{1,0:T(8,128)S(1)}) custom-call(f32[5,8,8,128]{3,2,1,0:T(8,128)} %adjoint_any.3), custom_call_target="tpu_custom_call" | custom-call | tf_op jit(solution)/shard_map/pallas_call | solution.py:315
  1.9 2.5 %collective-permute-start = (f32[5,8,128]{2,1,0:T(8,128)S(1)}, f32[5,8,128]{2,1,0:T(8,128)S(1)}, u32[]{:S(2)}, u32[]{:S(2)}) collective-permute-start(f32[5,8,128]{2,1,0:T(8,128)S(1)} %get-tuple-element.30), channel_id=1, source_target_pairs={{0,16},{32,48},{64,80},{96,112},{128,144},{160,176},{192,208},{224... | collective-permute-start | bytes 61448 | tf_op jit(solution)/shard_map/ppermute | solution.py:346
  4.4 5.7 %collective-permute-start.1 = (f32[5,8,128]{2,1,0:T(8,128)S(1)}, f32[5,8,128]{2,1,0:T(8,128)S(1)}, u32[]{:S(2)}, u32[]{:S(2)}) collective-permute-start(f32[5,8,128]{2,1,0:T(8,128)S(1)} %get-tuple-element.31), channel_id=1, source_target_pairs={{16,32},{48,64},{80,96},{112,128},{144,160},{176,192},{208,224},{2... | collective-permute-start | bytes 61448 | tf_op jit(solution)/shard_map/ppermute | solution.py:346
  10.1 1.2 %collective-permute-start.2 = (f32[40,128]{1,0:T(8,128)S(1)}, f32[40,128]{1,0:T(8,128)S(1)}, u32[]{:S(2)}, u32[]{:S(2)}) collective-permute-start(f32[40,128]{1,0:T(8,128)S(1)} %get-tuple-element.32), channel_id=1, source_target_pairs={{0,4},{8,12},{4,0},{12,8},{1,5},{9,13},{5,1},{13,9},{2,6},{10,14},... | collective-permute-start | bytes 61448 | tf_op jit(solution)/shard_map/ppermute | solution.py:346
  11.3 1.8 %collective-permute-start.3 = (f32[40,128]{1,0:T(8,128)S(1)}, f32[40,128]{1,0:T(8,128)S(1)}, u32[]{:S(2)}, u32[]{:S(2)}) collective-permute-start(f32[40,128]{1,0:T(8,128)S(1)} %get-tuple-element.33), channel_id=1, source_target_pairs={{4,8},{12,0},{8,4},{0,12},{5,9},{13,1},{9,5},{1,13},{6,10},{14,2},... | collective-permute-start | bytes 61448 | tf_op jit(solution)/shard_map/ppermute | solution.py:346
  13.1 1.8 %collective-permute-start.4 = (f32[8,128]{1,0:T(8,128)S(1)}, f32[8,128]{1,0:T(8,128)S(1)}, u32[]{:S(2)}, u32[]{:S(2)}) collective-permute-start(f32[8,128]{1,0:T(8,128)S(1)} %get-tuple-element.34), channel_id=1, source_target_pairs={{0,1},{2,3},{1,0},{3,2},{4,5},{6,7},{5,4},{7,6},{8,9},{10,11},{9,8... | collective-permute-start | bytes 12296 | tf_op jit(solution)/shard_map/ppermute | solution.py:346
  14.9 0.8 %collective-permute-done.4.refs_4_ = f32[8,128]{1,0:T(8,128)S(1)} collective-permute-done((f32[8,128]{1,0:T(8,128)S(1)}, f32[8,128]{1,0:T(8,128)S(1)}, u32[]{:S(2)}, u32[]{:S(2)}) %collective-permute-start.4) | collective-permute-done | bytes 4128 | tf_op jit(solution)/shard_map/ppermute | solution.py:346
  15.7 2.8 %collective-permute-start.5 = (f32[8,128]{1,0:T(8,128)S(1)}, f32[8,128]{1,0:T(8,128)S(1)}, u32[]{:S(2)}, u32[]{:S(2)}) collective-permute-start(f32[8,128]{1,0:T(8,128)S(1)} %get-tuple-element.35), channel_id=1, source_target_pairs={{1,2},{3,0},{2,1},{0,3},{5,6},{7,4},{6,5},{4,7},{9,10},{11,8},{10,... | collective-permute-start | bytes 12296 | tf_op jit(solution)/shard_map/ppermute | solution.py:346
  18.6 1.7 %collective-permute-done.5.refs_5_ = f32[8,128]{1,0:T(8,128)S(1)} collective-permute-done((f32[8,128]{1,0:T(8,128)S(1)}, f32[8,128]{1,0:T(8,128)S(1)}, u32[]{:S(2)}, u32[]{:S(2)}) %collective-permute-start.5) | collective-permute-done | bytes 4128 | tf_op jit(solution)/shard_map/ppermute | solution.py:346
  20.3 0.0 collective-permute-done.refs_0_
  20.3 0.0 collective-permute-done.1.refs_1_
  20.3 0.0 collective-permute-done.3.refs_3_
  20.3 2.6 %shard_map.123 = (f32[3,8,8,128]{3,2,1,0:T(8,128)S(1)}, f32[3,8,128]{2,1,0:T(8,128)S(1)}, f32[3,8,128]{2,1,0:T(8,128)S(1)}, f32[24,128]{1,0:T(8,128)S(1)}, f32[2...) custom-call(f32[5,3,5]{2,1,0:T(4,128)} %bitcast.9, f32[3,5]{1,0:T(4,128)} %map_any.1, ...), custom_call_target="tpu_custom_call" | custom-call | tf_op jit(solution)/shard_map/pallas_call | solution.py:315
  22.9 0.1 collective-permute-start.6
  23.0 1.4 %collective-permute-start.7 = (f32[3,8,128]{2,1,0:T(8,128)S(1)}, f32[3,8,128]{2,1,0:T(8,128)S(1)}, u32[]{:S(2)}, u32[]{:S(2)}) collective-permute-start(f32[3,8,128]{2,1,0:T(8,128)S(1)} %get-tuple-element.38), channel_id=1, source_target_pairs={{16,32},{48,64},{80,96},{112,128},{144,160},{176,192},{208,224},{2... | collective-permute-start | bytes 36872 | tf_op jit(solution)/shard_map/ppermute | solution.py:346
  24.5 0.3 collective-permute-start.8
  24.8 0.6 collective-permute-start.9
  25.3 1.2 %collective-permute-start.10 = (f32[8,128]{1,0:T(8,128)S(1)}, f32[8,128]{1,0:T(8,128)S(1)}, u32[]{:S(2)}, u32[]{:S(2)}) collective-permute-start(f32[8,128]{1,0:T(8,128)S(1)} %get-tuple-element.41), channel_id=1, source_target_pairs={{0,1},{2,3},{1,0},{3,2},{4,5},{6,7},{5,4},{7,6},{8,9},{10,11},{9,8... | collective-permute-start | bytes 12296 | tf_op jit(solution)/shard_map/ppermute | solution.py:346
  26.6 0.8 %collective-permute-done.10.refs_4_ = f32[8,128]{1,0:T(8,128)S(1)} collective-permute-done((f32[8,128]{1,0:T(8,128)S(1)}, f32[8,128]{1,0:T(8,128)S(1)}, u32[]{:S(2)}, u32[]{:S(2)}) %collective-permute-start.10) | collective-permute-done | bytes 4128 | tf_op jit(solution)/shard_map/ppermute | solution.py:346
  27.4 2.8 %collective-permute-start.11 = (f32[8,128]{1,0:T(8,128)S(1)}, f32[8,128]{1,0:T(8,128)S(1)}, u32[]{:S(2)}, u32[]{:S(2)}) collective-permute-start(f32[8,128]{1,0:T(8,128)S(1)} %get-tuple-element.42), channel_id=1, source_target_pairs={{1,2},{3,0},{2,1},{0,3},{5,6},{7,4},{6,5},{4,7},{9,10},{11,8},{10,... | collective-permute-start | bytes 12296 | tf_op jit(solution)/shard_map/ppermute | solution.py:346
  30.3 1.7 %collective-permute-done.11.refs_5_ = f32[8,128]{1,0:T(8,128)S(1)} collective-permute-done((f32[8,128]{1,0:T(8,128)S(1)}, f32[8,128]{1,0:T(8,128)S(1)}, u32[]{:S(2)}, u32[]{:S(2)}) %collective-permute-start.11) | collective-permute-done | bytes 4128 | tf_op jit(solution)/shard_map/ppermute | solution.py:346
  31.9 0.0 collective-permute-done.6.refs_0_
  32.0 0.3 shard_map.124
  32.3 0.1 collective-permute-start.12
  32.4 2.0 %collective-permute-start.13 = (f32[3,8,128]{2,1,0:T(8,128)S(1)}, f32[3,8,128]{2,1,0:T(8,128)S(1)}, u32[]{:S(2)}, u32[]{:S(2)}) collective-permute-start(f32[3,8,128]{2,1,0:T(8,128)S(1)} %get-tuple-element.45), channel_id=1, source_target_pairs={{16,32},{48,64},{80,96},{112,128},{144,160},{176,192},{208,224},{2... | collective-permute-start | bytes 36872 | tf_op jit(solution)/shard_map/ppermute | solution.py:346
  34.4 1.1 %collective-permute-start.14 = (f32[24,128]{1,0:T(8,128)S(1)}, f32[24,128]{1,0:T(8,128)S(1)}, u32[]{:S(2)}, u32[]{:S(2)}) collective-permute-start(f32[24,128]{1,0:T(8,128)S(1)} %get-tuple-element.46), channel_id=1, source_target_pairs={{0,4},{8,12},{4,0},{12,8},{1,5},{9,13},{5,1},{13,9},{2,6},{10,14},... | collective-permute-start | bytes 36872 | tf_op jit(solution)/shard_map/ppermute | solution.py:346
  35.5 1.8 %collective-permute-start.15 = (f32[24,128]{1,0:T(8,128)S(1)}, f32[24,128]{1,0:T(8,128)S(1)}, u32[]{:S(2)}, u32[]{:S(2)}) collective-permute-start(f32[24,128]{1,0:T(8,128)S(1)} %get-tuple-element.47), channel_id=1, source_target_pairs={{4,8},{12,0},{8,4},{0,12},{5,9},{13,1},{9,5},{1,13},{6,10},{14,2},... | collective-permute-start | bytes 36872 | tf_op jit(solution)/shard_map/ppermute | solution.py:346
  37.3 1.2 %collective-permute-start.16 = (f32[8,128]{1,0:T(8,128)S(1)}, f32[8,128]{1,0:T(8,128)S(1)}, u32[]{:S(2)}, u32[]{:S(2)}) collective-permute-start(f32[8,128]{1,0:T(8,128)S(1)} %get-tuple-element.48), channel_id=1, source_target_pairs={{0,1},{2,3},{1,0},{3,2},{4,5},{6,7},{5,4},{7,6},{8,9},{10,11},{9,8... | collective-permute-start | bytes 12296 | tf_op jit(solution)/shard_map/ppermute | solution.py:346
  38.5 0.8 %collective-permute-done.16.refs_4_ = f32[8,128]{1,0:T(8,128)S(1)} collective-permute-done((f32[8,128]{1,0:T(8,128)S(1)}, f32[8,128]{1,0:T(8,128)S(1)}, u32[]{:S(2)}, u32[]{:S(2)}) %collective-permute-start.16) | collective-permute-done | bytes 4128 | tf_op jit(solution)/shard_map/ppermute | solution.py:346
  39.3 2.8 %collective-permute-start.17 = (f32[8,128]{1,0:T(8,128)S(1)}, f32[8,128]{1,0:T(8,128)S(1)}, u32[]{:S(2)}, u32[]{:S(2)}) collective-permute-start(f32[8,128]{1,0:T(8,128)S(1)} %get-tuple-element.49), channel_id=1, source_target_pairs={{1,2},{3,0},{2,1},{0,3},{5,6},{7,4},{6,5},{4,7},{9,10},{11,8},{10,... | collective-permute-start | bytes 12296 | tf_op jit(solution)/shard_map/ppermute | solution.py:346
  42.8 1.0 %collective-permute-done.17.refs_5_ = f32[8,128]{1,0:T(8,128)S(1)} collective-permute-done((f32[8,128]{1,0:T(8,128)S(1)}, f32[8,128]{1,0:T(8,128)S(1)}, u32[]{:S(2)}, u32[]{:S(2)}) %collective-permute-start.17) | collective-permute-done | bytes 4128 | tf_op jit(solution)/shard_map/ppermute | solution.py:346
  43.8 0.0 collective-permute-done.14.refs_2_
  43.8 0.0 collective-permute-done.15.refs_3_
  43.9 1.4 %shard_map.125 = (f32[3,8,8,128]{3,2,1,0:T(8,128)}, f32[32,16,128]{2,1,0:T(8,128)S(1)}) custom-call(s32[1]{0:T(128)} %bitcast.5.box_ref, s32[3]{0:T(128)S(1)} %bitcast.7, f32[3,8,8,128]{3,2,1,0:T(8,128)S(1)} %get-tuple-element.43.now_ref, f32[3,8,8,128]{3,2,1,0:T(8,128)S(1)} %get-tuple-element.36.start_ref, f32[7,8,8,128]{3,2,1,0:T(8,128)S(1)} %copy-done, ...), custom_call_target="tpu_custom_call" | custom-call | tf_op jit(solution)/shard_map/pallas_call | solution.py:315
  45.3 13.5 %all_to_all.5 = f32[32,16,128]{2,1,0:T(8,128)S(1)} all-to-all(f32[32,16,128]{2,1,0:T(8,128)S(1)} %get-tuple-element.51), channel_id=1, replica_groups={{0,2,4,6,8,10,12,14,16,18,20,22,24,26,28,30,128,130,132,134,136,138,140..., dimensions={0} | all-to-all | bytes 524288 | tf_op jit(solution)/shard_map/all_to_all | solution.py:390
  58.8 0.7 %shard_map.126 = (f32[4,72,128]{2,1,0:T(8,128)S(1)}, f32[4,72,128]{2,1,0:T(8,128)S(1)}) custom-call(f32[512,128]{1,0:T(8,128)S(1)} %bitcast.6), custom_call_target="tpu_custom_call" | custom-call | tf_op jit(solution)/shard_map/pallas_call | solution.py:315
  59.6 1.6 %collective-permute-start.18 = (f32[4,72,128]{2,1,0:T(8,128)S(1)}, f32[4,72,128]{2,1,0:T(8,128)S(1)}, u32[]{:S(2)}, u32[]{:S(2)}) collective-permute-start(f32[4,72,128]{2,1,0:T(8,128)S(1)} %get-tuple-element.53), channel_id=1, source_target_pairs={{0,1},{2,3},{1,0},{3,2},{4,5},{6,7},{5,4},{7,6},{8,9},{10,11},{9,8... | collective-permute-start | bytes 442376 | tf_op jit(solution)/shard_map/ppermute | solution.py:397
  61.1 1.0 %collective-permute-done.18.got_ref = f32[4,72,128]{2,1,0:T(8,128)S(1)} collective-permute-done((f32[4,72,128]{2,1,0:T(8,128)S(1)}, f32[4,72,128]{2,1,0:T(8,128)S(1)}, u32[]{:S(2)}, u32[]{:S(2)}) %collective-permute-start.18) | collective-permute-done | bytes 147488 | tf_op jit(solution)/shard_map/ppermute | solution.py:397
  62.1 1.0 %collective-permute-start.19 = (f32[72,128]{1,0:T(8,128)S(1)}, f32[72,128]{1,0:T(8,128)S(1)}, u32[]{:S(2)}, u32[]{:S(2)}) collective-permute-start(f32[72,128]{1,0:T(8,128)S(1)} %get-tuple-element.55), channel_id=1, source_target_pairs={{0,32},{16,48},{32,0},{48,16},{64,96},{80,112},{96,64},{112,80},{1... | collective-permute-start | bytes 110600 | tf_op jit(solution)/shard_map/ppermute | solution.py:401
  63.1 3.7 %collective-permute-start.20 = (f32[72,128]{1,0:T(8,128)S(1)}, f32[72,128]{1,0:T(8,128)S(1)}, u32[]{:S(2)}, u32[]{:S(2)}) collective-permute-start(f32[72,128]{1,0:T(8,128)S(1)} %get-tuple-element.56), channel_id=1, source_target_pairs={{0,64},{16,80},{32,96},{48,112},{64,0},{80,16},{96,32},{112,48},{1... | collective-permute-start | bytes 110600 | tf_op jit(solution)/shard_map/ppermute | solution.py:401
  66.9 1.0 %collective-permute-start.21 = (f32[72,128]{1,0:T(8,128)S(1)}, f32[72,128]{1,0:T(8,128)S(1)}, u32[]{:S(2)}, u32[]{:S(2)}) collective-permute-start(f32[72,128]{1,0:T(8,128)S(1)} %get-tuple-element.57), channel_id=1, source_target_pairs={{0,96},{16,112},{32,64},{48,80},{64,32},{80,48},{96,0},{112,16},{1... | collective-permute-start | bytes 110600 | tf_op jit(solution)/shard_map/ppermute | solution.py:401
  67.9 1.9 %collective-permute-done.20.refs_2_ = f32[72,128]{1,0:T(8,128)S(1)} collective-permute-done((f32[72,128]{1,0:T(8,128)S(1)}, f32[72,128]{1,0:T(8,128)S(1)}, u32[]{:S(2)}, u32[]{:S(2)}) %collective-permute-start.20) | collective-permute-done | bytes 36896 | tf_op jit(solution)/shard_map/ppermute | solution.py:401
  69.8 2.0 %collective-permute-done.21.refs_3_ = f32[72,128]{1,0:T(8,128)S(1)} collective-permute-done((f32[72,128]{1,0:T(8,128)S(1)}, f32[72,128]{1,0:T(8,128)S(1)}, u32[]{:S(2)}, u32[]{:S(2)}) %collective-permute-start.21) | collective-permute-done | bytes 36896 | tf_op jit(solution)/shard_map/ppermute | solution.py:401
  71.8 0.7 shard_map.128
  (14 shorter events, 0.0 us)
Async XLA Ops:
  0.6 43.2 %copy-start.2 = (f32[32,192]{1,0:T(8,128)S(1)}, f32[32,192]{1,0:T(8,128)}, u32[]{:S(2)}) copy-start(f32[32,192]{1,0:T(8,128)} %constant.8.clone.bx_ref) | copy-start | bytes 73732
  0.6 43.2 %copy-start.3 = (f32[8,128]{1,0:T(8,128)S(1)}, f32[8,128]{1,0:T(8,128)}, u32[]{:S(2)}) copy-start(f32[8,128]{1,0:T(8,128)} %constant.7.clone.by_ref) | copy-start | bytes 12292
  0.7 43.2 %copy-start.1 = (f32[128,128]{1,0:T(8,128)S(1)}, f32[128,128]{1,0:T(8,128)}, u32[]{:S(2)}) copy-start(f32[128,128]{1,0:T(8,128)} %constant.6.clone.bz_ref) | copy-start | bytes 196612
  0.7 31.3 %copy-start = (f32[7,8,8,128]{3,2,1,0:T(8,128)S(1)}, f32[7,8,8,128]{3,2,1,0:T(8,128)}, u32[]{:S(2)}) copy-start(f32[7,8,8,128]{3,2,1,0:T(8,128)} %stiff_ref.3) | copy-start | bytes 688132
  0.7 43.2 %copy-start.4 = (s32[1,1,1,3]{3,2,1,0:T(1,128)S(1)}, s32[1,1,1,3]{3,2,1,0:T(1,128)}, u32[]{:S(2)}) copy-start(s32[1,1,1,3]{3,2,1,0:T(1,128)} %param.18) | copy-start | bytes 40
  1.9 18.4 %collective-permute-start = (f32[5,8,128]{2,1,0:T(8,128)S(1)}, f32[5,8,128]{2,1,0:T(8,128)S(1)}, u32[]{:S(2)}, u32[]{:S(2)}) collective-permute-start(f32[5,8,128]{2,1,0:T(8,128)S(1)} %get-tuple-element.30), channel_id=1, source_target_pairs={{0,16},{32,48},{64,80},{96,112},{128,144},{160,176},{192,208},{224... | collective-permute-start | bytes 61448 | tf_op jit(solution)/shard_map/ppermute | solution.py:346
  4.4 15.9 %collective-permute-start.1 = (f32[5,8,128]{2,1,0:T(8,128)S(1)}, f32[5,8,128]{2,1,0:T(8,128)S(1)}, u32[]{:S(2)}, u32[]{:S(2)}) collective-permute-start(f32[5,8,128]{2,1,0:T(8,128)S(1)} %get-tuple-element.31), channel_id=1, source_target_pairs={{16,32},{48,64},{80,96},{112,128},{144,160},{176,192},{208,224},{2... | collective-permute-start | bytes 61448 | tf_op jit(solution)/shard_map/ppermute | solution.py:346
  10.1 10.2 %collective-permute-start.2 = (f32[40,128]{1,0:T(8,128)S(1)}, f32[40,128]{1,0:T(8,128)S(1)}, u32[]{:S(2)}, u32[]{:S(2)}) collective-permute-start(f32[40,128]{1,0:T(8,128)S(1)} %get-tuple-element.32), channel_id=1, source_target_pairs={{0,4},{8,12},{4,0},{12,8},{1,5},{9,13},{5,1},{13,9},{2,6},{10,14},... | collective-permute-start | bytes 61448 | tf_op jit(solution)/shard_map/ppermute | solution.py:346
  11.3 9.0 %collective-permute-start.3 = (f32[40,128]{1,0:T(8,128)S(1)}, f32[40,128]{1,0:T(8,128)S(1)}, u32[]{:S(2)}, u32[]{:S(2)}) collective-permute-start(f32[40,128]{1,0:T(8,128)S(1)} %get-tuple-element.33), channel_id=1, source_target_pairs={{4,8},{12,0},{8,4},{0,12},{5,9},{13,1},{9,5},{1,13},{6,10},{14,2},... | collective-permute-start | bytes 61448 | tf_op jit(solution)/shard_map/ppermute | solution.py:346
  13.1 2.6 %collective-permute-start.4 = (f32[8,128]{1,0:T(8,128)S(1)}, f32[8,128]{1,0:T(8,128)S(1)}, u32[]{:S(2)}, u32[]{:S(2)}) collective-permute-start(f32[8,128]{1,0:T(8,128)S(1)} %get-tuple-element.34), channel_id=1, source_target_pairs={{0,1},{2,3},{1,0},{3,2},{4,5},{6,7},{5,4},{7,6},{8,9},{10,11},{9,8... | collective-permute-start | bytes 12296 | tf_op jit(solution)/shard_map/ppermute | solution.py:346
  15.7 4.5 %collective-permute-start.5 = (f32[8,128]{1,0:T(8,128)S(1)}, f32[8,128]{1,0:T(8,128)S(1)}, u32[]{:S(2)}, u32[]{:S(2)}) collective-permute-start(f32[8,128]{1,0:T(8,128)S(1)} %get-tuple-element.35), channel_id=1, source_target_pairs={{1,2},{3,0},{2,1},{0,3},{5,6},{7,4},{6,5},{4,7},{9,10},{11,8},{10,... | collective-permute-start | bytes 12296 | tf_op jit(solution)/shard_map/ppermute | solution.py:346
  22.9 9.0 %collective-permute-start.6 = (f32[3,8,128]{2,1,0:T(8,128)S(1)}, f32[3,8,128]{2,1,0:T(8,128)S(1)}, u32[]{:S(2)}, u32[]{:S(2)}) collective-permute-start(f32[3,8,128]{2,1,0:T(8,128)S(1)} %get-tuple-element.37), channel_id=1, source_target_pairs={{0,16},{32,48},{64,80},{96,112},{128,144},{160,176},{192,208},{224... | collective-permute-start | bytes 36872 | tf_op jit(solution)/shard_map/ppermute | solution.py:346
  23.0 8.9 %collective-permute-start.7 = (f32[3,8,128]{2,1,0:T(8,128)S(1)}, f32[3,8,128]{2,1,0:T(8,128)S(1)}, u32[]{:S(2)}, u32[]{:S(2)}) collective-permute-start(f32[3,8,128]{2,1,0:T(8,128)S(1)} %get-tuple-element.38), channel_id=1, source_target_pairs={{16,32},{48,64},{80,96},{112,128},{144,160},{176,192},{208,224},{2... | collective-permute-start | bytes 36872 | tf_op jit(solution)/shard_map/ppermute | solution.py:346
  24.5 7.5 %collective-permute-start.8 = (f32[24,128]{1,0:T(8,128)S(1)}, f32[24,128]{1,0:T(8,128)S(1)}, u32[]{:S(2)}, u32[]{:S(2)}) collective-permute-start(f32[24,128]{1,0:T(8,128)S(1)} %get-tuple-element.39), channel_id=1, source_target_pairs={{0,4},{8,12},{4,0},{12,8},{1,5},{9,13},{5,1},{13,9},{2,6},{10,14},... | collective-permute-start | bytes 36872 | tf_op jit(solution)/shard_map/ppermute | solution.py:346
  24.8 7.2 %collective-permute-start.9 = (f32[24,128]{1,0:T(8,128)S(1)}, f32[24,128]{1,0:T(8,128)S(1)}, u32[]{:S(2)}, u32[]{:S(2)}) collective-permute-start(f32[24,128]{1,0:T(8,128)S(1)} %get-tuple-element.40), channel_id=1, source_target_pairs={{4,8},{12,0},{8,4},{0,12},{5,9},{13,1},{9,5},{1,13},{6,10},{14,2},... | collective-permute-start | bytes 36872 | tf_op jit(solution)/shard_map/ppermute | solution.py:346
  25.3 2.1 %collective-permute-start.10 = (f32[8,128]{1,0:T(8,128)S(1)}, f32[8,128]{1,0:T(8,128)S(1)}, u32[]{:S(2)}, u32[]{:S(2)}) collective-permute-start(f32[8,128]{1,0:T(8,128)S(1)} %get-tuple-element.41), channel_id=1, source_target_pairs={{0,1},{2,3},{1,0},{3,2},{4,5},{6,7},{5,4},{7,6},{8,9},{10,11},{9,8... | collective-permute-start | bytes 12296 | tf_op jit(solution)/shard_map/ppermute | solution.py:346
  27.4 4.5 %collective-permute-start.11 = (f32[8,128]{1,0:T(8,128)S(1)}, f32[8,128]{1,0:T(8,128)S(1)}, u32[]{:S(2)}, u32[]{:S(2)}) collective-permute-start(f32[8,128]{1,0:T(8,128)S(1)} %get-tuple-element.42), channel_id=1, source_target_pairs={{1,2},{3,0},{2,1},{0,3},{5,6},{7,4},{6,5},{4,7},{9,10},{11,8},{10,... | collective-permute-start | bytes 12296 | tf_op jit(solution)/shard_map/ppermute | solution.py:346
  32.3 11.6 %collective-permute-start.12 = (f32[3,8,128]{2,1,0:T(8,128)S(1)}, f32[3,8,128]{2,1,0:T(8,128)S(1)}, u32[]{:S(2)}, u32[]{:S(2)}) collective-permute-start(f32[3,8,128]{2,1,0:T(8,128)S(1)} %get-tuple-element.44), channel_id=1, source_target_pairs={{0,16},{32,48},{64,80},{96,112},{128,144},{160,176},{192,208},{224... | collective-permute-start | bytes 36872 | tf_op jit(solution)/shard_map/ppermute | solution.py:346
  32.4 11.5 %collective-permute-start.13 = (f32[3,8,128]{2,1,0:T(8,128)S(1)}, f32[3,8,128]{2,1,0:T(8,128)S(1)}, u32[]{:S(2)}, u32[]{:S(2)}) collective-permute-start(f32[3,8,128]{2,1,0:T(8,128)S(1)} %get-tuple-element.45), channel_id=1, source_target_pairs={{16,32},{48,64},{80,96},{112,128},{144,160},{176,192},{208,224},{2... | collective-permute-start | bytes 36872 | tf_op jit(solution)/shard_map/ppermute | solution.py:346
  34.4 9.5 %collective-permute-start.14 = (f32[24,128]{1,0:T(8,128)S(1)}, f32[24,128]{1,0:T(8,128)S(1)}, u32[]{:S(2)}, u32[]{:S(2)}) collective-permute-start(f32[24,128]{1,0:T(8,128)S(1)} %get-tuple-element.46), channel_id=1, source_target_pairs={{0,4},{8,12},{4,0},{12,8},{1,5},{9,13},{5,1},{13,9},{2,6},{10,14},... | collective-permute-start | bytes 36872 | tf_op jit(solution)/shard_map/ppermute | solution.py:346
  35.5 8.4 %collective-permute-start.15 = (f32[24,128]{1,0:T(8,128)S(1)}, f32[24,128]{1,0:T(8,128)S(1)}, u32[]{:S(2)}, u32[]{:S(2)}) collective-permute-start(f32[24,128]{1,0:T(8,128)S(1)} %get-tuple-element.47), channel_id=1, source_target_pairs={{4,8},{12,0},{8,4},{0,12},{5,9},{13,1},{9,5},{1,13},{6,10},{14,2},... | collective-permute-start | bytes 36872 | tf_op jit(solution)/shard_map/ppermute | solution.py:346
  37.3 2.0 %collective-permute-start.16 = (f32[8,128]{1,0:T(8,128)S(1)}, f32[8,128]{1,0:T(8,128)S(1)}, u32[]{:S(2)}, u32[]{:S(2)}) collective-permute-start(f32[8,128]{1,0:T(8,128)S(1)} %get-tuple-element.48), channel_id=1, source_target_pairs={{0,1},{2,3},{1,0},{3,2},{4,5},{6,7},{5,4},{7,6},{8,9},{10,11},{9,8... | collective-permute-start | bytes 12296 | tf_op jit(solution)/shard_map/ppermute | solution.py:346
  39.3 4.5 %collective-permute-start.17 = (f32[8,128]{1,0:T(8,128)S(1)}, f32[8,128]{1,0:T(8,128)S(1)}, u32[]{:S(2)}, u32[]{:S(2)}) collective-permute-start(f32[8,128]{1,0:T(8,128)S(1)} %get-tuple-element.49), channel_id=1, source_target_pairs={{1,2},{3,0},{2,1},{0,3},{5,6},{7,4},{6,5},{4,7},{9,10},{11,8},{10,... | collective-permute-start | bytes 12296 | tf_op jit(solution)/shard_map/ppermute | solution.py:346
  59.6 2.6 %collective-permute-start.18 = (f32[4,72,128]{2,1,0:T(8,128)S(1)}, f32[4,72,128]{2,1,0:T(8,128)S(1)}, u32[]{:S(2)}, u32[]{:S(2)}) collective-permute-start(f32[4,72,128]{2,1,0:T(8,128)S(1)} %get-tuple-element.53), channel_id=1, source_target_pairs={{0,1},{2,3},{1,0},{3,2},{4,5},{6,7},{5,4},{7,6},{8,9},{10,11},{9,8... | collective-permute-start | bytes 442376 | tf_op jit(solution)/shard_map/ppermute | solution.py:397
  62.1 5.7 %collective-permute-start.19 = (f32[72,128]{1,0:T(8,128)S(1)}, f32[72,128]{1,0:T(8,128)S(1)}, u32[]{:S(2)}, u32[]{:S(2)}) collective-permute-start(f32[72,128]{1,0:T(8,128)S(1)} %get-tuple-element.55), channel_id=1, source_target_pairs={{0,32},{16,48},{32,0},{48,16},{64,96},{80,112},{96,64},{112,80},{1... | collective-permute-start | bytes 110600 | tf_op jit(solution)/shard_map/ppermute | solution.py:401
  63.1 6.7 %collective-permute-start.20 = (f32[72,128]{1,0:T(8,128)S(1)}, f32[72,128]{1,0:T(8,128)S(1)}, u32[]{:S(2)}, u32[]{:S(2)}) collective-permute-start(f32[72,128]{1,0:T(8,128)S(1)} %get-tuple-element.56), channel_id=1, source_target_pairs={{0,64},{16,80},{32,96},{48,112},{64,0},{80,16},{96,32},{112,48},{1... | collective-permute-start | bytes 110600 | tf_op jit(solution)/shard_map/ppermute | solution.py:401
  66.9 4.9 %collective-permute-start.21 = (f32[72,128]{1,0:T(8,128)S(1)}, f32[72,128]{1,0:T(8,128)S(1)}, u32[]{:S(2)}, u32[]{:S(2)}) collective-permute-start(f32[72,128]{1,0:T(8,128)S(1)} %get-tuple-element.57), channel_id=1, source_target_pairs={{0,96},{16,112},{32,64},{48,80},{64,32},{80,48},{96,0},{112,16},{1... | collective-permute-start | bytes 110600 | tf_op jit(solution)/shard_map/ppermute | solution.py:401

commit v5 on v4

--- a/solution.py
+++ b/solution.py
@@ -236,7 +236,7 @@
     keep_ref, give_ref, wide_ref, chunk_ref = refs
     half = lax.div(lax.axis_index("normal"), 2)
     span = lax.axis_index("span")
-    nearest = lax.div(span, 8) * 8 + lax.rem(span, 2)
+    nearest = lax.div(span, 4) * 4
     where = got_ref[pl.ds(12, WINDOWS, stride=SLOT), :]
     start = got_ref[pl.ds(13, WINDOWS, stride=SLOT), :]
     lane = lax.broadcasted_iota(jnp.int32, (WINDOWS, 128), 1)
@@ -249,7 +249,7 @@
     line = lax.broadcasted_iota(jnp.int32, (64, 128), 0)
     chunk = lax.div(line, 8)
     owner = lax.axis_index("chord") * 4 + half * 2 + lax.rem(chunk, 2)
-    same = (nearest + 2 * lax.div(chunk, 2)).astype(F32) == jnp.broadcast_to(boxes, (64, 128))
+    same = (nearest + lax.div(chunk, 2)).astype(F32) == jnp.broadcast_to(boxes, (64, 128))
     point = jnp.where(lax.rem(line, 8) < ROWS, owner * ROWS + lax.rem(line, 8), -1).astype(F32)
     hits = jnp.concatenate(
         [jnp.where(same & (point == jnp.broadcast_to(first + 4.0 * h, (64, 128))), 1.0, 0.0) for h in range(2)], axis=1
@@ -280,7 +280,7 @@
 
 
 def join_kernel(keep_ref, got_ref, *sends):
-    mine = lax.div(lax.rem(lax.axis_index("span"), 8), 2)
+    mine = lax.rem(lax.axis_index("span"), 4)
     for d in range(4):
         at = lax.bitwise_xor(mine, d)
         sends[d][...] = keep_ref[at] + got_ref[at]
@@ -348,8 +348,8 @@
 
 
 def owners():
-    index = np.arange(256).reshape(2, 4, 2, 4, 2, 2)
-    return index.transpose(1, 5, 0, 2, 3, 4).reshape(8, 32).tolist()
+    index = np.arange(256).reshape(2, 2, 4, 4, 2, 2)
+    return index.transpose(2, 5, 0, 1, 3, 4).reshape(8, 32).tolist()
 
 
 def ends(v):
@@ -398,7 +398,7 @@
     mine, *chunks = call(join_kernel, (shape(72, 128),) * 4, (keep, got))
     got = []
     for d, one in enumerate(chunks, 1):
-        got.append(lax.ppermute(one, "span", [(i, i ^ (2 * d)) for i in range(16)]))
+        got.append(lax.ppermute(one, "span", [(i, i ^ d) for i in range(16)]))
     grad = call(sum_kernel, shape(3, 1, 3072), (mine, *got), scratch=((72, 128),))
     return final, grad.reshape(1, 3, 3072)
 

time: 72.6 us -> 77.2 us (1.063)
  blocking collectives: 13.5 us -> 20.3 us
  waiting for transfers between devices: 11.8 us -> 10.5 us
    all_to_all x1, blocking collectives: 13.5 us -> 20.3 us  [local(): lax.all_to_all(windows, ALL, 0, 0, axis_index_groups=owners(), tiled=True)]
    ppermute x3, waiting for transfers between devices: 3.9 us -> 2.56 us  [local(): got.append(lax.ppermute(one, 'span', [(i, i ^ d) for i in range(16)]))]
    ppermute x3, starting transfers between devices: 5.74 us -> 4.77 us  [local(): got.append(lax.ppermute(one, 'span', [(i, i ^ d) for i in range(16)]))]
where the time goes in v5:
time: 77.2 us; the launch traced here: 77.1 us
  starting transfers between devices  38 us (49%)
  blocking collectives  20.3 us (26%)
  waiting for transfers between devices  10.5 us (14%)
  Pallas kernels  6.87 us (9%)
  between operations  1.46 us (2%)
    ppermute x18, starting transfers between devices, swap(): got.append(lax.ppermute(one, AXES[name], pairing(AXES[name], at % 2)))  31.4 us
    all_to_all x1, blocking collectives, local(): lax.all_to_all(windows, ALL, 0, 0, axis_index_groups=owners(), tiled=True)  20.3 us
    ppermute x18, waiting for transfers between devices, swap(): got.append(lax.ppermute(one, AXES[name], pairing(AXES[name], at % 2)))  6.91 us
    pallas_call x7, Pallas kernels, call(): pl.pallas_call(body, out_shape=outs, in_specs=specs, out_specs=jax.tree.m...  6.87 us
    ppermute x3, starting transfers between devices, local(): got.append(lax.ppermute(one, 'span', [(i, i ^ d) for i in range(16)]))  4.77 us
    ppermute x3, waiting for transfers between devices, local(): got.append(lax.ppermute(one, 'span', [(i, i ^ d) for i in range(16)]))  2.56 us
    ppermute x1, starting transfers between devices, local(): got = lax.ppermute(give, 'normal', pairing('normal', 0))  1.77 us
  transfers between devices with their start and end apart: 22, of which 9 were waited for; matrix products, arithmetic and copies ran while one was open for 0% of the time, Pallas kernels for 0%

profile of v5, /device:TPU:1, one launch (start us, length us, event | category | flops | bytes accessed | tf_op | source)
XLA Modules:
  0.0 77.1 jit_solution(9274900371133657649)
XLA Ops:
  0.6 0.0 copy-start.2
  0.6 0.0 copy-start.3
  0.7 0.0 copy-start.1
  0.7 0.0 copy-start
  0.7 1.2 %shard_map.122 = (f32[5,8,128]{2,1,0:T(8,128)S(1)}, f32[5,8,128]{2,1,0:T(8,128)S(1)}, f32[40,128]{1,0:T(8,128)S(1)}, f32[40,128]{1,0:T(8,128)S(1)}, f32[8,128]{1,0:T(8,128)S(1)}, /*index=5*/f32[8,128]{1,0:T(8,128)S(1)}) custom-call(f32[5,8,8,128]{3,2,1,0:T(8,128)} %adjoint_any.3), custom_call_target="tpu_custom_call" | custom-call | tf_op jit(solution)/shard_map/pallas_call | solution.py:315
  1.9 2.5 %collective-permute-start = (f32[5,8,128]{2,1,0:T(8,128)S(1)}, f32[5,8,128]{2,1,0:T(8,128)S(1)}, u32[]{:S(2)}, u32[]{:S(2)}) collective-permute-start(f32[5,8,128]{2,1,0:T(8,128)S(1)} %get-tuple-element.30), channel_id=1, source_target_pairs={{0,16},{32,48},{64,80},{96,112},{128,144},{160,176},{192,208},{224... | collective-permute-start | bytes 61448 | tf_op jit(solution)/shard_map/ppermute | solution.py:346
  4.4 5.7 %collective-permute-start.1 = (f32[5,8,128]{2,1,0:T(8,128)S(1)}, f32[5,8,128]{2,1,0:T(8,128)S(1)}, u32[]{:S(2)}, u32[]{:S(2)}) collective-permute-start(f32[5,8,128]{2,1,0:T(8,128)S(1)} %get-tuple-element.31), channel_id=1, source_target_pairs={{16,32},{48,64},{80,96},{112,128},{144,160},{176,192},{208,224},{2... | collective-permute-start | bytes 61448 | tf_op jit(solution)/shard_map/ppermute | solution.py:346
  10.1 1.2 %collective-permute-start.2 = (f32[40,128]{1,0:T(8,128)S(1)}, f32[40,128]{1,0:T(8,128)S(1)}, u32[]{:S(2)}, u32[]{:S(2)}) collective-permute-start(f32[40,128]{1,0:T(8,128)S(1)} %get-tuple-element.32), channel_id=1, source_target_pairs={{0,4},{8,12},{4,0},{12,8},{1,5},{9,13},{5,1},{13,9},{2,6},{10,14},... | collective-permute-start | bytes 61448 | tf_op jit(solution)/shard_map/ppermute | solution.py:346
  11.3 1.8 %collective-permute-start.3 = (f32[40,128]{1,0:T(8,128)S(1)}, f32[40,128]{1,0:T(8,128)S(1)}, u32[]{:S(2)}, u32[]{:S(2)}) collective-permute-start(f32[40,128]{1,0:T(8,128)S(1)} %get-tuple-element.33), channel_id=1, source_target_pairs={{4,8},{12,0},{8,4},{0,12},{5,9},{13,1},{9,5},{1,13},{6,10},{14,2},... | collective-permute-start | bytes 61448 | tf_op jit(solution)/shard_map/ppermute | solution.py:346
  13.1 1.8 %collective-permute-start.4 = (f32[8,128]{1,0:T(8,128)S(1)}, f32[8,128]{1,0:T(8,128)S(1)}, u32[]{:S(2)}, u32[]{:S(2)}) collective-permute-start(f32[8,128]{1,0:T(8,128)S(1)} %get-tuple-element.34), channel_id=1, source_target_pairs={{0,1},{2,3},{1,0},{3,2},{4,5},{6,7},{5,4},{7,6},{8,9},{10,11},{9,8... | collective-permute-start | bytes 12296 | tf_op jit(solution)/shard_map/ppermute | solution.py:346
  14.9 0.8 %collective-permute-done.4.refs_4_ = f32[8,128]{1,0:T(8,128)S(1)} collective-permute-done((f32[8,128]{1,0:T(8,128)S(1)}, f32[8,128]{1,0:T(8,128)S(1)}, u32[]{:S(2)}, u32[]{:S(2)}) %collective-permute-start.4) | collective-permute-done | bytes 4128 | tf_op jit(solution)/shard_map/ppermute | solution.py:346
  15.7 2.8 %collective-permute-start.5 = (f32[8,128]{1,0:T(8,128)S(1)}, f32[8,128]{1,0:T(8,128)S(1)}, u32[]{:S(2)}, u32[]{:S(2)}) collective-permute-start(f32[8,128]{1,0:T(8,128)S(1)} %get-tuple-element.35), channel_id=1, source_target_pairs={{1,2},{3,0},{2,1},{0,3},{5,6},{7,4},{6,5},{4,7},{9,10},{11,8},{10,... | collective-permute-start | bytes 12296 | tf_op jit(solution)/shard_map/ppermute | solution.py:346
  18.6 1.7 %collective-permute-done.5.refs_5_ = f32[8,128]{1,0:T(8,128)S(1)} collective-permute-done((f32[8,128]{1,0:T(8,128)S(1)}, f32[8,128]{1,0:T(8,128)S(1)}, u32[]{:S(2)}, u32[]{:S(2)}) %collective-permute-start.5) | collective-permute-done | bytes 4128 | tf_op jit(solution)/shard_map/ppermute | solution.py:346
  20.3 0.0 collective-permute-done.refs_0_
  20.3 0.0 collective-permute-done.1.refs_1_
  20.3 0.0 collective-permute-done.2.refs_2_
  20.3 0.0 collective-permute-done.3.refs_3_
  20.3 2.6 %shard_map.123 = (f32[3,8,8,128]{3,2,1,0:T(8,128)S(1)}, f32[3,8,128]{2,1,0:T(8,128)S(1)}, f32[3,8,128]{2,1,0:T(8,128)S(1)}, f32[24,128]{1,0:T(8,128)S(1)}, f32[2...) custom-call(f32[5,3,5]{2,1,0:T(4,128)} %bitcast.9, f32[3,5]{1,0:T(4,128)} %map_any.1, ...), custom_call_target="tpu_custom_call" | custom-call | tf_op jit(solution)/shard_map/pallas_call | solution.py:315
  22.9 0.1 collective-permute-start.6
  23.0 1.4 %collective-permute-start.7 = (f32[3,8,128]{2,1,0:T(8,128)S(1)}, f32[3,8,128]{2,1,0:T(8,128)S(1)}, u32[]{:S(2)}, u32[]{:S(2)}) collective-permute-start(f32[3,8,128]{2,1,0:T(8,128)S(1)} %get-tuple-element.38), channel_id=1, source_target_pairs={{16,32},{48,64},{80,96},{112,128},{144,160},{176,192},{208,224},{2... | collective-permute-start | bytes 36872 | tf_op jit(solution)/shard_map/ppermute | solution.py:346
  24.5 0.3 collective-permute-start.8
  24.8 0.6 collective-permute-start.9
  25.3 1.2 %collective-permute-start.10 = (f32[8,128]{1,0:T(8,128)S(1)}, f32[8,128]{1,0:T(8,128)S(1)}, u32[]{:S(2)}, u32[]{:S(2)}) collective-permute-start(f32[8,128]{1,0:T(8,128)S(1)} %get-tuple-element.41), channel_id=1, source_target_pairs={{0,1},{2,3},{1,0},{3,2},{4,5},{6,7},{5,4},{7,6},{8,9},{10,11},{9,8... | collective-permute-start | bytes 12296 | tf_op jit(solution)/shard_map/ppermute | solution.py:346
  26.6 0.8 %collective-permute-done.10.refs_4_ = f32[8,128]{1,0:T(8,128)S(1)} collective-permute-done((f32[8,128]{1,0:T(8,128)S(1)}, f32[8,128]{1,0:T(8,128)S(1)}, u32[]{:S(2)}, u32[]{:S(2)}) %collective-permute-start.10) | collective-permute-done | bytes 4128 | tf_op jit(solution)/shard_map/ppermute | solution.py:346
  27.4 2.8 %collective-permute-start.11 = (f32[8,128]{1,0:T(8,128)S(1)}, f32[8,128]{1,0:T(8,128)S(1)}, u32[]{:S(2)}, u32[]{:S(2)}) collective-permute-start(f32[8,128]{1,0:T(8,128)S(1)} %get-tuple-element.42), channel_id=1, source_target_pairs={{1,2},{3,0},{2,1},{0,3},{5,6},{7,4},{6,5},{4,7},{9,10},{11,8},{10,... | collective-permute-start | bytes 12296 | tf_op jit(solution)/shard_map/ppermute | solution.py:346
  30.3 1.7 %collective-permute-done.11.refs_5_ = f32[8,128]{1,0:T(8,128)S(1)} collective-permute-done((f32[8,128]{1,0:T(8,128)S(1)}, f32[8,128]{1,0:T(8,128)S(1)}, u32[]{:S(2)}, u32[]{:S(2)}) %collective-permute-start.11) | collective-permute-done | bytes 4128 | tf_op jit(solution)/shard_map/ppermute | solution.py:346
  31.9 0.0 collective-permute-done.6.refs_0_
  32.0 0.3 shard_map.124
  32.3 0.1 collective-permute-start.12
  32.4 2.0 %collective-permute-start.13 = (f32[3,8,128]{2,1,0:T(8,128)S(1)}, f32[3,8,128]{2,1,0:T(8,128)S(1)}, u32[]{:S(2)}, u32[]{:S(2)}) collective-permute-start(f32[3,8,128]{2,1,0:T(8,128)S(1)} %get-tuple-element.45), channel_id=1, source_target_pairs={{16,32},{48,64},{80,96},{112,128},{144,160},{176,192},{208,224},{2... | collective-permute-start | bytes 36872 | tf_op jit(solution)/shard_map/ppermute | solution.py:346
  34.4 1.1 %collective-permute-start.14 = (f32[24,128]{1,0:T(8,128)S(1)}, f32[24,128]{1,0:T(8,128)S(1)}, u32[]{:S(2)}, u32[]{:S(2)}) collective-permute-start(f32[24,128]{1,0:T(8,128)S(1)} %get-tuple-element.46), channel_id=1, source_target_pairs={{0,4},{8,12},{4,0},{12,8},{1,5},{9,13},{5,1},{13,9},{2,6},{10,14},... | collective-permute-start | bytes 36872 | tf_op jit(solution)/shard_map/ppermute | solution.py:346
  35.5 1.8 %collective-permute-start.15 = (f32[24,128]{1,0:T(8,128)S(1)}, f32[24,128]{1,0:T(8,128)S(1)}, u32[]{:S(2)}, u32[]{:S(2)}) collective-permute-start(f32[24,128]{1,0:T(8,128)S(1)} %get-tuple-element.47), channel_id=1, source_target_pairs={{4,8},{12,0},{8,4},{0,12},{5,9},{13,1},{9,5},{1,13},{6,10},{14,2},... | collective-permute-start | bytes 36872 | tf_op jit(solution)/shard_map/ppermute | solution.py:346
  37.3 1.2 %collective-permute-start.16 = (f32[8,128]{1,0:T(8,128)S(1)}, f32[8,128]{1,0:T(8,128)S(1)}, u32[]{:S(2)}, u32[]{:S(2)}) collective-permute-start(f32[8,128]{1,0:T(8,128)S(1)} %get-tuple-element.48), channel_id=1, source_target_pairs={{0,1},{2,3},{1,0},{3,2},{4,5},{6,7},{5,4},{7,6},{8,9},{10,11},{9,8... | collective-permute-start | bytes 12296 | tf_op jit(solution)/shard_map/ppermute | solution.py:346
  38.5 0.8 %collective-permute-done.16.refs_4_ = f32[8,128]{1,0:T(8,128)S(1)} collective-permute-done((f32[8,128]{1,0:T(8,128)S(1)}, f32[8,128]{1,0:T(8,128)S(1)}, u32[]{:S(2)}, u32[]{:S(2)}) %collective-permute-start.16) | collective-permute-done | bytes 4128 | tf_op jit(solution)/shard_map/ppermute | solution.py:346
  39.3 2.8 %collective-permute-start.17 = (f32[8,128]{1,0:T(8,128)S(1)}, f32[8,128]{1,0:T(8,128)S(1)}, u32[]{:S(2)}, u32[]{:S(2)}) collective-permute-start(f32[8,128]{1,0:T(8,128)S(1)} %get-tuple-element.49), channel_id=1, source_target_pairs={{1,2},{3,0},{2,1},{0,3},{5,6},{7,4},{6,5},{4,7},{9,10},{11,8},{10,... | collective-permute-start | bytes 12296 | tf_op jit(solution)/shard_map/ppermute | solution.py:346
  42.8 1.0 %collective-permute-done.17.refs_5_ = f32[8,128]{1,0:T(8,128)S(1)} collective-permute-done((f32[8,128]{1,0:T(8,128)S(1)}, f32[8,128]{1,0:T(8,128)S(1)}, u32[]{:S(2)}, u32[]{:S(2)}) %collective-permute-start.17) | collective-permute-done | bytes 4128 | tf_op jit(solution)/shard_map/ppermute | solution.py:346
  43.8 0.0 collective-permute-done.14.refs_2_
  43.8 0.0 collective-permute-done.15.refs_3_
  43.9 1.4 %shard_map.125 = (f32[3,8,8,128]{3,2,1,0:T(8,128)}, f32[32,16,128]{2,1,0:T(8,128)S(1)}) custom-call(s32[1]{0:T(128)} %bitcast.5.box_ref, s32[3]{0:T(128)S(1)} %bitcast.7, f32[3,8,8,128]{3,2,1,0:T(8,128)S(1)} %get-tuple-element.43.now_ref, f32[3,8,8,128]{3,2,1,0:T(8,128)S(1)} %get-tuple-element.36.start_ref, f32[7,8,8,128]{3,2,1,0:T(8,128)S(1)} %copy-done, ...), custom_call_target="tpu_custom_call" | custom-call | tf_op jit(solution)/shard_map/pallas_call | solution.py:315
  45.3 20.3 %all_to_all.5 = f32[32,16,128]{2,1,0:T(8,128)S(1)} all-to-all(f32[32,16,128]{2,1,0:T(8,128)S(1)} %get-tuple-element.51), channel_id=1, replica_groups={{0,2,4,6,8,10,12,14,64,66,68,70,72,74,76,78,128,130,132,134,136,138,140..., dimensions={0} | all-to-all | bytes 524288 | tf_op jit(solution)/shard_map/all_to_all | solution.py:390
  65.6 0.7 shard_map.126
  66.3 1.8 %collective-permute-start.18 = (f32[4,72,128]{2,1,0:T(8,128)S(1)}, f32[4,72,128]{2,1,0:T(8,128)S(1)}, u32[]{:S(2)}, u32[]{:S(2)}) collective-permute-start(f32[4,72,128]{2,1,0:T(8,128)S(1)} %get-tuple-element.53), channel_id=1, source_target_pairs={{0,1},{2,3},{1,0},{3,2},{4,5},{6,7},{5,4},{7,6},{8,9},{10,11},{9,8... | collective-permute-start | bytes 442376 | tf_op jit(solution)/shard_map/ppermute | solution.py:397
  68.1 1.0 %collective-permute-done.18.got_ref = f32[4,72,128]{2,1,0:T(8,128)S(1)} collective-permute-done((f32[4,72,128]{2,1,0:T(8,128)S(1)}, f32[4,72,128]{2,1,0:T(8,128)S(1)}, u32[]{:S(2)}, u32[]{:S(2)}) %collective-permute-start.18) | collective-permute-done | bytes 147488 | tf_op jit(solution)/shard_map/ppermute | solution.py:397
  69.1 2.6 %collective-permute-start.19 = (f32[72,128]{1,0:T(8,128)S(1)}, f32[72,128]{1,0:T(8,128)S(1)}, u32[]{:S(2)}, u32[]{:S(2)}) collective-permute-start(f32[72,128]{1,0:T(8,128)S(1)} %get-tuple-element.55), channel_id=1, source_target_pairs={{0,16},{16,0},{32,48},{48,32},{64,80},{80,64},{96,112},{112,96},{1... | collective-permute-start | bytes 110600 | tf_op jit(solution)/shard_map/ppermute | solution.py:401
  71.7 2.2 %collective-permute-start.21 = (f32[72,128]{1,0:T(8,128)S(1)}, f32[72,128]{1,0:T(8,128)S(1)}, u32[]{:S(2)}, u32[]{:S(2)}) collective-permute-start(f32[72,128]{1,0:T(8,128)S(1)} %get-tuple-element.57), channel_id=1, source_target_pairs={{0,48},{16,32},{32,16},{48,0},{64,112},{80,96},{96,80},{112,64},{1... | collective-permute-start | bytes 110600 | tf_op jit(solution)/shard_map/ppermute | solution.py:401
  73.9 1.7 %collective-permute-done.20.refs_2_ = f32[72,128]{1,0:T(8,128)S(1)} collective-permute-done((f32[72,128]{1,0:T(8,128)S(1)}, f32[72,128]{1,0:T(8,128)S(1)}, u32[]{:S(2)}, u32[]{:S(2)}) %collective-permute-start.20) | collective-permute-done | bytes 36896 | tf_op jit(solution)/shard_map/ppermute | solution.py:401
  75.6 0.8 %collective-permute-done.21.refs_3_ = f32[72,128]{1,0:T(8,128)S(1)} collective-permute-done((f32[72,128]{1,0:T(8,128)S(1)}, f32[72,128]{1,0:T(8,128)S(1)}, u32[]{:S(2)}, u32[]{:S(2)}) %collective-permute-start.21) | collective-permute-done | bytes 36896 | tf_op jit(solution)/shard_map/ppermute | solution.py:401
  76.4 0.7 shard_map.128
  (14 shorter events, 0.0 us)
Async XLA Ops:
  0.6 43.2 %copy-start.2 = (f32[32,192]{1,0:T(8,128)S(1)}, f32[32,192]{1,0:T(8,128)}, u32[]{:S(2)}) copy-start(f32[32,192]{1,0:T(8,128)} %constant.8.clone.bx_ref) | copy-start | bytes 73732
  0.6 43.2 %copy-start.3 = (f32[8,128]{1,0:T(8,128)S(1)}, f32[8,128]{1,0:T(8,128)}, u32[]{:S(2)}) copy-start(f32[8,128]{1,0:T(8,128)} %constant.7.clone.by_ref) | copy-start | bytes 12292
  0.7 43.2 %copy-start.1 = (f32[128,128]{1,0:T(8,128)S(1)}, f32[128,128]{1,0:T(8,128)}, u32[]{:S(2)}) copy-start(f32[128,128]{1,0:T(8,128)} %constant.6.clone.bz_ref) | copy-start | bytes 196612
  0.7 31.3 %copy-start = (f32[7,8,8,128]{3,2,1,0:T(8,128)S(1)}, f32[7,8,8,128]{3,2,1,0:T(8,128)}, u32[]{:S(2)}) copy-start(f32[7,8,8,128]{3,2,1,0:T(8,128)} %stiff_ref.3) | copy-start | bytes 688132
  0.7 43.2 %copy-start.4 = (s32[1,1,1,3]{3,2,1,0:T(1,128)S(1)}, s32[1,1,1,3]{3,2,1,0:T(1,128)}, u32[]{:S(2)}) copy-start(s32[1,1,1,3]{3,2,1,0:T(1,128)} %param.18) | copy-start | bytes 40
  1.9 18.4 %collective-permute-start = (f32[5,8,128]{2,1,0:T(8,128)S(1)}, f32[5,8,128]{2,1,0:T(8,128)S(1)}, u32[]{:S(2)}, u32[]{:S(2)}) collective-permute-start(f32[5,8,128]{2,1,0:T(8,128)S(1)} %get-tuple-element.30), channel_id=1, source_target_pairs={{0,16},{32,48},{64,80},{96,112},{128,144},{160,176},{192,208},{224... | collective-permute-start | bytes 61448 | tf_op jit(solution)/shard_map/ppermute | solution.py:346
  4.4 15.9 %collective-permute-start.1 = (f32[5,8,128]{2,1,0:T(8,128)S(1)}, f32[5,8,128]{2,1,0:T(8,128)S(1)}, u32[]{:S(2)}, u32[]{:S(2)}) collective-permute-start(f32[5,8,128]{2,1,0:T(8,128)S(1)} %get-tuple-element.31), channel_id=1, source_target_pairs={{16,32},{48,64},{80,96},{112,128},{144,160},{176,192},{208,224},{2... | collective-permute-start | bytes 61448 | tf_op jit(solution)/shard_map/ppermute | solution.py:346
  10.1 10.2 %collective-permute-start.2 = (f32[40,128]{1,0:T(8,128)S(1)}, f32[40,128]{1,0:T(8,128)S(1)}, u32[]{:S(2)}, u32[]{:S(2)}) collective-permute-start(f32[40,128]{1,0:T(8,128)S(1)} %get-tuple-element.32), channel_id=1, source_target_pairs={{0,4},{8,12},{4,0},{12,8},{1,5},{9,13},{5,1},{13,9},{2,6},{10,14},... | collective-permute-start | bytes 61448 | tf_op jit(solution)/shard_map/ppermute | solution.py:346
  11.3 9.0 %collective-permute-start.3 = (f32[40,128]{1,0:T(8,128)S(1)}, f32[40,128]{1,0:T(8,128)S(1)}, u32[]{:S(2)}, u32[]{:S(2)}) collective-permute-start(f32[40,128]{1,0:T(8,128)S(1)} %get-tuple-element.33), channel_id=1, source_target_pairs={{4,8},{12,0},{8,4},{0,12},{5,9},{13,1},{9,5},{1,13},{6,10},{14,2},... | collective-permute-start | bytes 61448 | tf_op jit(solution)/shard_map/ppermute | solution.py:346
  13.1 2.6 %collective-permute-start.4 = (f32[8,128]{1,0:T(8,128)S(1)}, f32[8,128]{1,0:T(8,128)S(1)}, u32[]{:S(2)}, u32[]{:S(2)}) collective-permute-start(f32[8,128]{1,0:T(8,128)S(1)} %get-tuple-element.34), channel_id=1, source_target_pairs={{0,1},{2,3},{1,0},{3,2},{4,5},{6,7},{5,4},{7,6},{8,9},{10,11},{9,8... | collective-permute-start | bytes 12296 | tf_op jit(solution)/shard_map/ppermute | solution.py:346
  15.7 4.5 %collective-permute-start.5 = (f32[8,128]{1,0:T(8,128)S(1)}, f32[8,128]{1,0:T(8,128)S(1)}, u32[]{:S(2)}, u32[]{:S(2)}) collective-permute-start(f32[8,128]{1,0:T(8,128)S(1)} %get-tuple-element.35), channel_id=1, source_target_pairs={{1,2},{3,0},{2,1},{0,3},{5,6},{7,4},{6,5},{4,7},{9,10},{11,8},{10,... | collective-permute-start | bytes 12296 | tf_op jit(solution)/shard_map/ppermute | solution.py:346
  22.9 9.0 %collective-permute-start.6 = (f32[3,8,128]{2,1,0:T(8,128)S(1)}, f32[3,8,128]{2,1,0:T(8,128)S(1)}, u32[]{:S(2)}, u32[]{:S(2)}) collective-permute-start(f32[3,8,128]{2,1,0:T(8,128)S(1)} %get-tuple-element.37), channel_id=1, source_target_pairs={{0,16},{32,48},{64,80},{96,112},{128,144},{160,176},{192,208},{224... | collective-permute-start | bytes 36872 | tf_op jit(solution)/shard_map/ppermute | solution.py:346
  23.0 8.9 %collective-permute-start.7 = (f32[3,8,128]{2,1,0:T(8,128)S(1)}, f32[3,8,128]{2,1,0:T(8,128)S(1)}, u32[]{:S(2)}, u32[]{:S(2)}) collective-permute-start(f32[3,8,128]{2,1,0:T(8,128)S(1)} %get-tuple-element.38), channel_id=1, source_target_pairs={{16,32},{48,64},{80,96},{112,128},{144,160},{176,192},{208,224},{2... | collective-permute-start | bytes 36872 | tf_op jit(solution)/shard_map/ppermute | solution.py:346
  24.5 7.5 %collective-permute-start.8 = (f32[24,128]{1,0:T(8,128)S(1)}, f32[24,128]{1,0:T(8,128)S(1)}, u32[]{:S(2)}, u32[]{:S(2)}) collective-permute-start(f32[24,128]{1,0:T(8,128)S(1)} %get-tuple-element.39), channel_id=1, source_target_pairs={{0,4},{8,12},{4,0},{12,8},{1,5},{9,13},{5,1},{13,9},{2,6},{10,14},... | collective-permute-start | bytes 36872 | tf_op jit(solution)/shard_map/ppermute | solution.py:346
  24.8 7.2 %collective-permute-start.9 = (f32[24,128]{1,0:T(8,128)S(1)}, f32[24,128]{1,0:T(8,128)S(1)}, u32[]{:S(2)}, u32[]{:S(2)}) collective-permute-start(f32[24,128]{1,0:T(8,128)S(1)} %get-tuple-element.40), channel_id=1, source_target_pairs={{4,8},{12,0},{8,4},{0,12},{5,9},{13,1},{9,5},{1,13},{6,10},{14,2},... | collective-permute-start | bytes 36872 | tf_op jit(solution)/shard_map/ppermute | solution.py:346
  25.3 2.1 %collective-permute-start.10 = (f32[8,128]{1,0:T(8,128)S(1)}, f32[8,128]{1,0:T(8,128)S(1)}, u32[]{:S(2)}, u32[]{:S(2)}) collective-permute-start(f32[8,128]{1,0:T(8,128)S(1)} %get-tuple-element.41), channel_id=1, source_target_pairs={{0,1},{2,3},{1,0},{3,2},{4,5},{6,7},{5,4},{7,6},{8,9},{10,11},{9,8... | collective-permute-start | bytes 12296 | tf_op jit(solution)/shard_map/ppermute | solution.py:346
  27.4 4.5 %collective-permute-start.11 = (f32[8,128]{1,0:T(8,128)S(1)}, f32[8,128]{1,0:T(8,128)S(1)}, u32[]{:S(2)}, u32[]{:S(2)}) collective-permute-start(f32[8,128]{1,0:T(8,128)S(1)} %get-tuple-element.42), channel_id=1, source_target_pairs={{1,2},{3,0},{2,1},{0,3},{5,6},{7,4},{6,5},{4,7},{9,10},{11,8},{10,... | collective-permute-start | bytes 12296 | tf_op jit(solution)/shard_map/ppermute | solution.py:346
  32.3 11.6 %collective-permute-start.12 = (f32[3,8,128]{2,1,0:T(8,128)S(1)}, f32[3,8,128]{2,1,0:T(8,128)S(1)}, u32[]{:S(2)}, u32[]{:S(2)}) collective-permute-start(f32[3,8,128]{2,1,0:T(8,128)S(1)} %get-tuple-element.44), channel_id=1, source_target_pairs={{0,16},{32,48},{64,80},{96,112},{128,144},{160,176},{192,208},{224... | collective-permute-start | bytes 36872 | tf_op jit(solution)/shard_map/ppermute | solution.py:346
  32.4 11.5 %collective-permute-start.13 = (f32[3,8,128]{2,1,0:T(8,128)S(1)}, f32[3,8,128]{2,1,0:T(8,128)S(1)}, u32[]{:S(2)}, u32[]{:S(2)}) collective-permute-start(f32[3,8,128]{2,1,0:T(8,128)S(1)} %get-tuple-element.45), channel_id=1, source_target_pairs={{16,32},{48,64},{80,96},{112,128},{144,160},{176,192},{208,224},{2... | collective-permute-start | bytes 36872 | tf_op jit(solution)/shard_map/ppermute | solution.py:346
  34.4 9.5 %collective-permute-start.14 = (f32[24,128]{1,0:T(8,128)S(1)}, f32[24,128]{1,0:T(8,128)S(1)}, u32[]{:S(2)}, u32[]{:S(2)}) collective-permute-start(f32[24,128]{1,0:T(8,128)S(1)} %get-tuple-element.46), channel_id=1, source_target_pairs={{0,4},{8,12},{4,0},{12,8},{1,5},{9,13},{5,1},{13,9},{2,6},{10,14},... | collective-permute-start | bytes 36872 | tf_op jit(solution)/shard_map/ppermute | solution.py:346
  35.5 8.4 %collective-permute-start.15 = (f32[24,128]{1,0:T(8,128)S(1)}, f32[24,128]{1,0:T(8,128)S(1)}, u32[]{:S(2)}, u32[]{:S(2)}) collective-permute-start(f32[24,128]{1,0:T(8,128)S(1)} %get-tuple-element.47), channel_id=1, source_target_pairs={{4,8},{12,0},{8,4},{0,12},{5,9},{13,1},{9,5},{1,13},{6,10},{14,2},... | collective-permute-start | bytes 36872 | tf_op jit(solution)/shard_map/ppermute | solution.py:346
  37.3 2.0 %collective-permute-start.16 = (f32[8,128]{1,0:T(8,128)S(1)}, f32[8,128]{1,0:T(8,128)S(1)}, u32[]{:S(2)}, u32[]{:S(2)}) collective-permute-start(f32[8,128]{1,0:T(8,128)S(1)} %get-tuple-element.48), channel_id=1, source_target_pairs={{0,1},{2,3},{1,0},{3,2},{4,5},{6,7},{5,4},{7,6},{8,9},{10,11},{9,8... | collective-permute-start | bytes 12296 | tf_op jit(solution)/shard_map/ppermute | solution.py:346
  39.3 4.5 %collective-permute-start.17 = (f32[8,128]{1,0:T(8,128)S(1)}, f32[8,128]{1,0:T(8,128)S(1)}, u32[]{:S(2)}, u32[]{:S(2)}) collective-permute-start(f32[8,128]{1,0:T(8,128)S(1)} %get-tuple-element.49), channel_id=1, source_target_pairs={{1,2},{3,0},{2,1},{0,3},{5,6},{7,4},{6,5},{4,7},{9,10},{11,8},{10,... | collective-permute-start | bytes 12296 | tf_op jit(solution)/shard_map/ppermute | solution.py:346
  66.3 2.8 %collective-permute-start.18 = (f32[4,72,128]{2,1,0:T(8,128)S(1)}, f32[4,72,128]{2,1,0:T(8,128)S(1)}, u32[]{:S(2)}, u32[]{:S(2)}) collective-permute-start(f32[4,72,128]{2,1,0:T(8,128)S(1)} %get-tuple-element.53), channel_id=1, source_target_pairs={{0,1},{2,3},{1,0},{3,2},{4,5},{6,7},{5,4},{7,6},{8,9},{10,11},{9,8... | collective-permute-start | bytes 442376 | tf_op jit(solution)/shard_map/ppermute | solution.py:397
  69.1 4.8 %collective-permute-start.19 = (f32[72,128]{1,0:T(8,128)S(1)}, f32[72,128]{1,0:T(8,128)S(1)}, u32[]{:S(2)}, u32[]{:S(2)}) collective-permute-start(f32[72,128]{1,0:T(8,128)S(1)} %get-tuple-element.55), channel_id=1, source_target_pairs={{0,16},{16,0},{32,48},{48,32},{64,80},{80,64},{96,112},{112,96},{1... | collective-permute-start | bytes 110600 | tf_op jit(solution)/shard_map/ppermute | solution.py:401
  71.7 3.9 %collective-permute-start.20 = (f32[72,128]{1,0:T(8,128)S(1)}, f32[72,128]{1,0:T(8,128)S(1)}, u32[]{:S(2)}, u32[]{:S(2)}) collective-permute-start(f32[72,128]{1,0:T(8,128)S(1)} %get-tuple-element.56), channel_id=1, source_target_pairs={{0,32},{16,48},{32,0},{48,16},{64,96},{80,112},{96,64},{112,80},{1... | collective-permute-start | bytes 110600 | tf_op jit(solution)/shard_map/ppermute | solution.py:401
  71.7 4.7 %collective-permute-start.21 = (f32[72,128]{1,0:T(8,128)S(1)}, f32[72,128]{1,0:T(8,128)S(1)}, u32[]{:S(2)}, u32[]{:S(2)}) collective-permute-start(f32[72,128]{1,0:T(8,128)S(1)} %get-tuple-element.57), channel_id=1, source_target_pairs={{0,48},{16,32},{32,16},{48,0},{64,112},{80,96},{96,80},{112,64},{1... | collective-permute-start | bytes 110600 | tf_op jit(solution)/shard_map/ppermute | solution.py:401
